TPU v7x, 128 devices: a whole 4x4x4 slice. The times are simulated.
128 devices in a mesh: pts: 32 (over x, y, core), top: 4 (over z).
Axes of the slice: x: 4, y: 4, z: 4, core: 2. Of those that a mesh axis runs over, the one named last changes fastest.
Arguments:
- local_pos: float32 [3, 131072], P(None, ('pts', 'top')), may hold values from -1 to 1
- densities: float32 [8, 131072], P(None, ('pts', 'top')), may hold values from -6 to 6
- morton_slot: int32 [131072], P(('pts', 'top')), may hold values from 0 to 131071, as said below
- slot_leaf: int32 [131072], P(('pts', 'top')), may hold values from 0 to 4095, as said below
- uc2e: float32 [152, 152], replicated, may hold values from -0.5 to 0.5
- m2m: float32 [184832], replicated, may hold values from -0.15625 to 0.15625
- m2l_ops: bfloat16 [7300864], replicated, may hold values from -0.02734375 to 0.02734375
- dc2e: float32 [152, 152], replicated, may hold values from -0.5 to 0.5
- lattice: float32 [152, 152], replicated, may hold values from -0.5 to 0.5
- l2l: float32 [184832], replicated, may hold values from -0.5 to 0.5
Outputs:
- potentials: float32 [8, 131072], P(None, ('pts', 'top'))
Inputs may be any that keep to these rules, and one draw needn't show every extreme that they name: `morton_slot`: every slot 0 to 131071 appears once. The points of one device go to at most 16 slots of any one device of the Morton layout (slot // 1024). `slot_leaf`: Non-decreasing. The leaves of the 4096 slots of one owner (slot // 4096) lie in at most 32 consecutive boxes of level 3 (leaf // 8).
All inputs are finite; a program needn't handle non-finite values.
Results may differ from a plain program's by a relative error of at most 0.003.
Values may be sent and summed in bfloat16 or wider, within the bound.
A program may use at most 192 MiB of HBM per device.

v0:
```python
import math

import jax
import jax.numpy as jnp
import numpy as np
from jax import lax
from jax.sharding import PartitionSpec as P

LEVEL = 3
EDGE = 6
DENS = 8
BOXES4 = 512


def surface_table():
    grid_vals = np.linspace(-1.0, 1.0, EDGE)
    points_list = []
    for index_a in range(EDGE):
        for index_b in range(EDGE):
            for index_c in range(EDGE):
                if (
                    min(index_a, index_b, index_c) == 0
                    or max(index_a, index_b, index_c) == EDGE - 1
                ):
                    points_list.append([grid_vals[index_a], grid_vals[index_b], grid_vals[index_c]])
    return np.array(points_list, dtype=np.float32).T


def offset_table():
    points_list = []
    for shift_x in range(-3, 4):
        for shift_y in range(-3, 4):
            for shift_z in range(-3, 4):
                if max(abs(shift_x), abs(shift_y), abs(shift_z)) >= 2:
                    points_list.append([shift_x, shift_y, shift_z])
    return np.array(points_list, dtype=np.int32)


def morton_decode(number, bit_count):
    coord_x = jnp.zeros_like(number)
    coord_y = jnp.zeros_like(number)
    coord_z = jnp.zeros_like(number)
    for level_idx in range(bit_count):
        digit_val = number // 8**level_idx % 8
        coord_x = coord_x + digit_val // 4 * 2**level_idx
        coord_y = coord_y + digit_val // 2 % 2 * 2**level_idx
        coord_z = coord_z + digit_val % 2 * 2**level_idx
    return (coord_x, coord_y, coord_z)


def morton_encode(coord_x, coord_y, coord_z, bit_count):
    number = jnp.zeros_like(coord_x)
    for level_idx in range(bit_count):
        digit_val = (
            coord_x // 2**level_idx % 2 * 4
            + coord_y // 2**level_idx % 2 * 2
            + coord_z // 2**level_idx % 2
        )
        number = number + digit_val * 8**level_idx
    return number


def source_boxes(targets):
    side_len = 2**LEVEL
    coord_x, coord_y, coord_z = morton_decode(targets, LEVEL)
    shift_table = jnp.asarray(offset_table())
    return morton_encode(
        (coord_x[None, :] + shift_table[:, 0:1]) % side_len,
        (coord_y[None, :] + shift_table[:, 1:2]) % side_len,
        (coord_z[None, :] + shift_table[:, 2:3]) % side_len,
        LEVEL,
    ).astype(jnp.int32)


def kernel_tile(local_pos):
    surface = surface_table()
    squared = jnp.zeros((local_pos.shape[1], surface.shape[1]), jnp.float32)
    for dim_index in range(3):
        spacing = 1.25 * jnp.asarray(surface[dim_index])[None, :] - local_pos[dim_index][:, None]
        squared = squared + spacing * spacing
    return 1.0 / (4.0 * math.pi * jnp.sqrt(squared))


def upward(level_mult, m2m):
    current = level_mult
    for level_idx in range(LEVEL):
        parents = current.shape[2] // 8
        current = jnp.einsum(
            "oce,ekpo->ckp",
            m2m,
            current.reshape(current.shape[0], current.shape[1], parents, 8),
            precision=lax.Precision.HIGHEST,
        )
    return current


def downward(root_local, l2l, levels):
    current = root_local
    for level_idx in range(levels):
        current = jnp.einsum("oce,ekp->ckpo", l2l, current, precision=lax.Precision.HIGHEST)
        current = current.reshape(current.shape[0], current.shape[1], -1)
    return current


def leaf_window(kernel, dens_vals, leaf_local, uc2e, m2m, box_cap):
    coef_len = kernel.shape[1]
    dens_len = dens_vals.shape[0]
    contrib = (dens_vals.T[:, :, None] * kernel[:, None, :]).reshape(
        kernel.shape[0], dens_len * coef_len
    )
    checks = jax.ops.segment_sum(
        contrib, leaf_local, num_segments=8 * box_cap, indices_are_sorted=True
    )
    checks = checks.reshape(box_cap, 8, dens_len, coef_len)
    leaf_mult = jnp.einsum("ef,bokf->boke", uc2e, checks, precision=lax.Precision.HIGHEST)
    return jnp.einsum("oce,boke->ckb", m2m, leaf_mult, precision=lax.Precision.HIGHEST)


def box_locals(targets, level4_low, m2l_ops, dc2e, coarse, l2l):
    coef_len = m2l_ops.shape[0]
    dens_len = level4_low.shape[1]
    count = targets.shape[0]
    block_len = math.gcd(count, 128)
    sources = source_boxes(targets)

    def one_block(block_idx):
        gathered = level4_low[:, :, sources]
        return jnp.einsum("cds,skdt->ckt", m2l_ops, gathered, preferred_element_type=jnp.float32)

    checks = lax.map(one_block, jnp.arange(count // block_len, dtype=jnp.int32))
    checks = checks.transpose(1, 2, 0, 3).reshape(coef_len, dens_len, count)
    from_checks = jnp.einsum("cd,dkt->ckt", dc2e, checks, precision=lax.Precision.HIGHEST)
    parents = coarse[:, :, targets // 8]
    children = jnp.einsum("oce,ekt->ockt", l2l, parents, precision=lax.Precision.HIGHEST)
    octant_mask = (targets % 8)[None, :] == jnp.arange(8, dtype=jnp.int32)[:, None]
    lattice_part = jnp.sum(jnp.where(octant_mask[:, None, None, :], children, 0.0), axis=0)
    return from_checks + lattice_part


def per_device(
    local_pos, densities, morton_slot, slot_leaf, uc2e, m2m, m2l_ops, dc2e, lattice, l2l
):
    devices = lax.axis_size(("pts", "top"))
    n_pts = lax.axis_size("pts")
    n_top = lax.axis_size("top")
    points_dev = local_pos.shape[1]
    send_cap = 2 * points_dev // devices
    box_cap = 2 * BOXES4 // n_pts
    dens_dev = DENS // n_top
    coef_len = uc2e.shape[0]
    m2m = m2m.reshape(8, coef_len, coef_len)
    l2l = l2l.reshape(8, coef_len, coef_len)
    m2l_ops = m2l_ops.reshape(coef_len, -1, coef_len)
    dest_dev = morton_slot // points_dev
    slot_local = morton_slot % points_dev
    dest_order = jnp.argsort(dest_dev, stable=True)
    sorted_dest = dest_dev[dest_order]
    first_pos = jnp.searchsorted(sorted_dest, jnp.arange(devices, dtype=jnp.int32), side="left")
    rank_sorted = jnp.arange(points_dev, dtype=jnp.int32) - first_pos[sorted_dest]
    rank_vals = jnp.zeros((points_dev,), jnp.int32).at[dest_order].set(rank_sorted)
    position = dest_dev * send_cap + rank_vals
    payload = jnp.concatenate([local_pos, densities], axis=0)
    outgoing = jnp.zeros((3 + DENS, devices * send_cap), jnp.float32).at[:, position].set(payload)
    labels = (
        jnp.full((1, devices * send_cap), points_dev, jnp.int32).at[0, position].set(slot_local)
    )
    incoming, arrivals = (
        lax.all_to_all(outgoing, ("pts", "top"), split_axis=1, concat_axis=1, tiled=True),
        lax.all_to_all(labels, ("pts", "top"), split_axis=1, concat_axis=1, tiled=True),
    )
    slot_vals = (
        jnp.zeros((3 + DENS, points_dev), jnp.float32).at[:, arrivals[0]].set(incoming, mode="drop")
    )
    my_pos = slot_vals[:3]
    my_dens = slot_vals[3:]
    first_box = lax.pmin(slot_leaf[0] // 8, "top")
    leaf_local = slot_leaf - 8 * first_box
    kernel = kernel_tile(my_pos)
    partial_value = leaf_window(kernel, my_dens, leaf_local, uc2e, m2m, box_cap)
    owner_part = lax.psum_scatter(partial_value, "top", scatter_dimension=1, tiled=True)
    rounded = owner_part.astype(jnp.bfloat16)
    box_ids = (first_box + jnp.arange(box_cap, dtype=jnp.int32)).reshape(1, 1, box_cap)
    values = lax.all_gather(rounded, "pts", axis=2, tiled=True)
    id_vals = lax.all_gather(box_ids, "pts", axis=2, tiled=True)
    level4 = (
        jnp.zeros((coef_len, dens_dev, BOXES4), jnp.float32)
        .at[:, :, id_vals[0, 0]]
        .add(values.astype(jnp.float32), mode="drop")
    )
    level4_low = level4.astype(jnp.bfloat16)
    root_mult = upward(level4, m2m)
    root_local = jnp.einsum("ce,ekp->ckp", lattice, root_mult, precision=lax.Precision.HIGHEST)
    coarse = downward(root_local, l2l, LEVEL - 1)
    targets = (first_box + jnp.arange(box_cap, dtype=jnp.int32)) % BOXES4
    locals4 = box_locals(targets, level4_low, m2l_ops, dc2e, coarse, l2l)
    full_locals = lax.all_gather(locals4, "top", axis=1, tiled=True)
    leaf_locals = jnp.einsum("oce,ekb->ckbo", l2l, full_locals, precision=lax.Precision.HIGHEST)
    leaf_locals = leaf_locals.reshape(coef_len, DENS, 8 * box_cap)
    at_slots = leaf_locals[:, :, leaf_local]
    potential = jnp.einsum("sc,cks->ks", kernel, at_slots, precision=lax.Precision.HIGHEST)
    reply_index = jnp.minimum(arrivals[0], points_dev - 1)
    reply_vals = potential[:, reply_index]
    returned = lax.all_to_all(reply_vals, ("pts", "top"), split_axis=1, concat_axis=1, tiled=True)
    return returned[:, position]


def solution(mesh):
    placed = (
        P(None, ("pts", "top")),
        P(None, ("pts", "top")),
        P(("pts", "top")),
        P(("pts", "top")),
        P(),
        P(),
        P(),
        P(),
        P(),
        P(),
    )
    return jax.shard_map(
        per_device, mesh=mesh, in_specs=placed, out_specs=P(None, ("pts", "top")), check_vma=False
    )
```

profile of v0, /device:TPU:1, one launch (start us, length us, event | category | flops | bytes accessed | tf_op | source)
XLA Modules:
  0.0 522.9 jit_solution(7373519447945422075)
XLA Ops:
  11.6 4.5 gather_fusion.1
  16.2 11.4 %while.28 = (s32[]{:T(128)}, u32[128]{0:T(128)S(1)}, u32[128]{0:T(128)S(1)}, s32[1024]{0:T(1024)S(1)}, s32[]{:T(128)}, /*index=5*/s32[]{:T(128)}, s32[]{}) while((s32[]{:T(128)}, u32[128]{0:T(128)S(1)}, u32[128]{0:T(128)S(1)}, s32[1024]{0:T(1024)S(1)}, s32[]{:T(128)}, /*index=5*/s32[]{:T(128)}, s32[]{}) %tuple.45), condition=%wide.region_3.4_spmd.clone, body=%wide.region_2.3_spmd.clone.sunk | while | flops 2692 | bytes 10348 | solution.py:158
  27.8 6.6 %gather_fusion.2 = s32[1024]{0:T(1024)S(1)} fusion(s32[128]{0:T(128)S(1)} %convert_element_type.19, s32[1024]{0:T(1024)S(1)} %broadcast_clamp_fusion.2), kind=kCustom, calls=%fused_computation.2 | custom fusion | bytes 12288 | tf_op jit(solution)/shard_map/gather | solution.py:159
  44.0 11.5 %all-to-all-start = ((s32[1,128,16]{2,0,1:T(1,128)}), s32[1,128,16]{2,0,1:T(1,128)S(1)}, u32[]{:S(2)}, u32[]{:S(2)}) async-start(s32[1,128,16]{2,0,1:T(1,128)} %bitcast.8), calls=%async_computation | async-start | bytes 131072 | tf_op jit(solution)/shard_map/all_to_all | solution.py:169
  58.6 8.2 %pmin.7 = s32[]{:T(128)} all-reduce(s32[]{:T(128)S(6)} %select_n.515), channel_id=1, replica_groups=mesh['pts'=32,'top'=4] {'top'}, use_global_device_ids=true, to_apply=%region_0.1 | all-reduce | flops 1 | bytes 8 | tf_op jit(solution)/shard_map/pmin | solution.py:176
  70.3 15.4 %all-reduce.1 = s32[1024]{0:T(1024)S(1)} all-reduce(s32[1024]{0:T(1024)S(1)} %bitcast_dynamic-update-slice_fusion), channel_id=1, replica_groups=mesh['pts'=32,'top'=4] {'pts'}, use_global_device_ids=true, to_apply=%add.1 | all-reduce | flops 1024 | bytes 8192
  103.4 60.9 %reshape.1366 = bf16[152,316,152]{2,1,0:T(8,128)(2,1)} reshape(bf16[7300864]{0:T(1024)(128)(2,1)} %param.22) | data formatting | bytes 29203456 | tf_op jit(solution)/shard_map/reshape | solution.py:153
  164.4 34.7 %copy.50 = bf16[152,316,152]{1,0,2:T(8,128)(2,1)} copy(bf16[152,316,152]{2,1,0:T(8,128)(2,1)} %reshape.1366) | data formatting | bytes 29203456 | tf_op jit(solution)/shard_map/reshape | solution.py:153
  199.1 7.4 %all-to-all-start.1 = ((f32[128,1,176]{2,1,0:T(1,128)}), f32[128,1,176]{2,1,0:T(1,128)S(1)}, u32[]{:S(2)}, u32[]{:S(2)}) async-start(f32[128,1,176]{2,1,0:T(1,128)} %reshape.1545), calls=%async_computation.1 | async-start | bytes 262144 | tf_op jit(solution)/shard_map/all_to_all | solution.py:168
  207.9 8.5 %all-to-all-done.1 = f32[128,1,176]{2,1,0:T(1,128)S(1)} async-done(((f32[128,1,176]{2,1,0:T(1,128)}), f32[128,1,176]{2,1,0:T(1,128)S(1)}, u32[]{:S(2)}, u32[]{:S(2)}) %all-to-all-start.1) | async-done | bytes 90144 | tf_op jit(solution)/shard_map/all_to_all | solution.py:168
  218.5 5.7 %scatter_custom_fusion.2 = f32[11,1024]{0,1:T(8,128)S(1)} fusion(s32[2048]{0:T(1024)S(1)} %bitcast.164, f32[2048,11]{1,0:T(8,128)S(1)} %bitcast.154, f32[]{:T(128)} %constant.383.clone.1), kind=kCustom, calls=%fused_computation.65 | custom fusion | bytes 45060 | tf_op jit(solution)/shard_map/scatter | solution.py:172
  229.6 5.9 %copy.46 = f32[1024,1216]{1,0:T(8,128)} copy(f32[1024,1216]{0,1:T(8,128)} %bitcast.146) | data formatting | bytes 9961472 | tf_op jit(solution)/shard_map/mul | solution.py:108
  235.4 11.3 %scatter_custom_fusion.3 = f32[256,1216]{1,0:T(8,128)S(1)} fusion(s32[1024]{0:T(1024)S(1)} %get-tuple-element.119, f32[1024,1216]{1,0:T(8,128)} %copy.46, f32[]{:T(128)} %constant.383.clone.1), kind=kCustom, calls=%fused_computation.45 | custom fusion | flops 1245184 | bytes 1245696 | tf_op jit(solution)/shard_map/scatter-add | solution.py:111
  257.6 12.9 %reduce-scatter.2.cloned.1.call-done = f32[152,2,32]{0,2,1:T(8,128)} async-done(((f32[152,8,32]{0,2,1:T(8,128)}), f32[152,2,32]{0,2,1:T(8,128)}) %reduce-scatter.2.cloned.1.call-update) | async-done | bytes 38928 | tf_op jit(solution)/shard_map/reduce_scatter | solution.py:180
  271.4 27.8 %all_gather.10 = bf16[152,2,1024]{0,1,2:T(2,128)(2,1)S(1)} all-gather(bf16[152,2,32]{0,1,2:T(2,128)(2,1)S(1)} %copy.48), channel_id=1, replica_groups=mesh['pts'=32,'top'=4] {'pts'}, dimensions={2}, use_global_device_ids=true | all-gather | bytes 642048 | tf_op jit(solution)/shard_map/all_gather | solution.py:183
  301.5 70.7 %scatter_fusion = f32[152,2,512]{0,1,2:T(2,128)S(1)} fusion(f32[152,2,512]{0,1,2:T(2,128)S(1)} %broadcast_in_dim.83, s32[1024]{0:T(1024)S(1)} %bitcast.163, f32[1024,152,2]{1,2,0:T(2,128)} %convert_bitcast_fusion), kind=kCustom, calls=%fused_computation.12 | custom fusion | flops 311296 | bytes 3739648 | tf_op jit(solution)/shard_map/scatter-add | solution.py:188
  379.1 36.8 %gather_fusion.3 = bf16[10112,152,2]{1,2,0:T(2,128)(2,1)} fusion(bf16[152,2,512]{0,1,2:T(2,128)(2,1)S(1)} %convert_element_type.22, s32[10240]{0:T(1024)S(1)} %pad_clamp_fusion.1), kind=kCustom, calls=%fused_computation.3 | custom fusion | bytes 12336640 | tf_op jit(solution)/shard_map/while/body/eval_jaxpr/gather | solution.py:127
  415.9 21.7 %copy.49 = bf16[316,32,152,2]{0,1,2,3:T(8,128)(2,1)} copy(bf16[316,32,152,2]{2,3,1,0:T(2,128)(2,1)} %bitcast.144) | data formatting | bytes 12296192 | tf_op jit(solution)/shard_map/while/body/eval_jaxpr/gather | solution.py:127
  439.6 11.3 %fusion.11 = f32[152,2,32]{0,2,1:T(8,128)S(1)} fusion(bf16[152,316,152]{1,0,2:T(8,128)(2,1)} %copy.50, bf16[316,32,152,2]{0,1,2,3:T(8,128)(2,1)} %copy.49), kind=kOutput, calls=%fused_computation.37 | convolution fusion | flops 934510592 | bytes 20788736 | tf_op jit(solution)/shard_map/while/body/eval_jaxpr/cds,skdt->ckt/dot_general | solution.py:128
  451.2 9.6 %all_gather.11 = f32[152,8,32]{0,2,1:T(8,128)S(1)} all-gather(f32[152,2,32]{0,2,1:T(8,128)S(1)} %fusion.16), channel_id=1, replica_groups=mesh['pts'=32,'top'=4] {'top'}, dimensions={1}, use_global_device_ids=true | all-gather | bytes 194560 | tf_op jit(solution)/shard_map/all_gather | solution.py:196
  465.1 10.6 %gather_fusion.5 = f32[1024,152,8]{1,2,0:T(8,128)} fusion(f32[152,8,256]{0,1,2:T(8,128)S(1)} %copy.59, s32[1024]{0:T(1024)S(1)} %get-tuple-element.118), kind=kCustom, calls=%fused_computation.5 | custom fusion | bytes 9965568 | tf_op jit(solution)/shard_map/gather | solution.py:199
  475.7 10.9 %fusion.6 = f32[1024,1,8]{2,1,0:T(1,128)S(1)} fusion(f32[1024,152,1]{1,2,0:T(1,128)S(1)} %copy-done.6, f32[1024,152,8]{1,2,0:T(8,128)} %gather_fusion.5), kind=kOutput, calls=%fused_computation.24 | convolution fusion | flops 14942208 | bytes 5636096 | tf_op jit(solution)/shard_map/sc,cks->ks/dot_general | solution.py:200
  486.6 5.5 %gather_fusion.6 = f32[2048,8]{1,0:T(8,128)S(1)} fusion(f32[8,1024]{0,1:T(8,128)S(1)} %bitcast.149, s32[2048]{0:T(1024)S(1)} %broadcast_clamp_fusion), kind=kCustom, calls=%fused_computation.6 | custom fusion | bytes 139264 | tf_op jit(solution)/shard_map/gather | solution.py:202
  492.7 18.2 %all_to_all.33 = f32[128,1,128]{2,1,0:T(1,128)S(1)} all-to-all(f32[128,1,128]{2,1,0:T(1,128)S(1)} %reshape.1547), channel_id=1, replica_groups=mesh['pts'=32,'top'=4] {'pts','top'}, dimensions={0} | all-to-all | bytes 131072 | tf_op jit(solution)/shard_map/all_to_all | solution.py:203
  (180 shorter events, 87.7 us)
Async XLA Ops:
  6.5 243.0 %copy-start = (f32[152,152]{1,0:T(8,128)S(1)}, f32[152,152]{1,0:T(8,128)}, u32[]{:S(2)}) copy-start(f32[152,152]{1,0:T(8,128)} %param.20) | copy-start | bytes 277252
  27.7 11.0 %copy-start.14 = (s32[1024]{0:T(1024)S(1)}, s32[1024]{0:T(1024)}, u32[]{:S(2)}) copy-start(s32[1024]{0:T(1024)} %param.18) | copy-start | bytes 12292
  27.7 11.1 %copy-start.23 = (s32[2]{0:T(128)S(1)}, s32[2]{0:T(128)}, u32[]{:S(2)}) copy-start(s32[2]{0:T(128)} %constant.418) | copy-start | bytes 28
  27.7 11.2 %copy-start.22 = (s32[2]{0:T(128)S(1)}, s32[2]{0:T(128)}, u32[]{:S(2)}) copy-start(s32[2]{0:T(128)} %constant.415) | copy-start | bytes 28
  27.7 27.8 %copy-start.15 = (s32[1024]{0:T(1024)S(1)}, s32[1024]{0:T(1024)}, u32[]{:S(2)}) copy-start(s32[1024]{0:T(1024)} %param.19) | copy-start | bytes 12292
  27.7 40.5 %copy-start.24 = (u32[128]{0:T(128)S(1)}, u32[128]{0:T(128)}, u32[]{:S(2)}) copy-start(u32[128]{0:T(128)} %constant.434) | copy-start | bytes 1540
  27.7 58.7 %copy-start.16 = (s32[316]{0:T(512)S(1)}, s32[316]{0:T(512)}, u32[]{:S(2)}) copy-start(s32[316]{0:T(512)} %constant.431) | copy-start | bytes 3796
  27.7 58.7 %copy-start.17 = (s32[316]{0:T(512)S(1)}, s32[316]{0:T(512)}, u32[]{:S(2)}) copy-start(s32[316]{0:T(512)} %constant.429) | copy-start | bytes 3796
  27.7 58.7 %copy-start.18 = (s32[316]{0:T(512)S(1)}, s32[316]{0:T(512)}, u32[]{:S(2)}) copy-start(s32[316]{0:T(512)} %constant.427) | copy-start | bytes 3796
  27.8 60.1 %copy-start.12 = (f32[8,1024]{1,0:T(8,128)S(1)}, f32[8,1024]{1,0:T(8,128)}, u32[]{:S(2)}) copy-start(f32[8,1024]{1,0:T(8,128)} %param.17) | copy-start | bytes 98308
  27.8 60.1 %copy-start.13 = (f32[3,1024]{1,0:T(4,128)S(1)}, f32[3,1024]{1,0:T(4,128)}, u32[]{:S(2)}) copy-start(f32[3,1024]{1,0:T(4,128)} %param.16) | copy-start | bytes 36868
  27.8 60.9 %copy-start.7 = (f32[184832]{0:T(1024)S(1)}, f32[184832]{0:T(1024)}, u32[]{:S(2)}) copy-start(f32[184832]{0:T(1024)} %param.21) | copy-start | bytes 2217988
  44.0 155.1 %all-to-all-start = ((s32[1,128,16]{2,0,1:T(1,128)}), s32[1,128,16]{2,0,1:T(1,128)S(1)}, u32[]{:S(2)}, u32[]{:S(2)}) async-start(s32[1,128,16]{2,0,1:T(1,128)} %bitcast.8), calls=%async_computation | async-start | bytes 131072 | tf_op jit(solution)/shard_map/all_to_all | solution.py:169
  87.9 5.2 copy-start.8
  199.1 17.4 %all-to-all-start.1 = ((f32[128,1,176]{2,1,0:T(1,128)}), f32[128,1,176]{2,1,0:T(1,128)S(1)}, u32[]{:S(2)}, u32[]{:S(2)}) async-start(f32[128,1,176]{2,1,0:T(1,128)} %reshape.1545), calls=%async_computation.1 | async-start | bytes 262144 | tf_op jit(solution)/shard_map/all_to_all | solution.py:168
  206.4 64.1 %reduce-scatter.2.cloned.1.call-start = ((), (), s32[]{:S(2)}) async-start(), calls=%async_computation.4 | async-start | bytes 327680 | tf_op jit(solution)/shard_map/reduce_scatter | solution.py:180
  218.5 6.9 %copy-start.19 = (f32[152]{0:T(256)S(1)}, f32[152]{0:T(256)}, u32[]{:S(2)}) copy-start(f32[152]{0:T(256)} %constant.425) | copy-start | bytes 1828
  218.5 6.9 %copy-start.20 = (f32[152]{0:T(256)S(1)}, f32[152]{0:T(256)}, u32[]{:S(2)}) copy-start(f32[152]{0:T(256)} %constant.424) | copy-start | bytes 1828
  218.5 6.9 %copy-start.21 = (f32[152]{0:T(256)S(1)}, f32[152]{0:T(256)}, u32[]{:S(2)}) copy-start(f32[152]{0:T(256)} %constant.423) | copy-start | bytes 1828
  372.6 4.1 copy-start.4
  415.9 22.3 %copy-start.3 = (f32[8,152,152,1]{2,1,0,3:T(8,128)S(1)}, f32[8,152,152,1]{2,1,0,3:T(8,128)}, u32[]{:S(2)}) copy-start(f32[8,152,152,1]{2,1,0,3:T(8,128)} %reshape.1516) | copy-start | bytes 2217988
  439.6 11.3 %copy-start.11 = (f32[152,152]{1,0:T(8,128)S(1)}, f32[152,152]{1,0:T(8,128)}, u32[]{:S(2)}) copy-start(f32[152,152]{1,0:T(8,128)} %param.23) | copy-start | bytes 277252
  465.1 10.6 %copy-start.6 = (f32[1024,152,1]{1,2,0:T(1,128)S(1)}, f32[1024,152,1]{1,2,0:T(1,128)}, u32[]{:S(2)}) copy-start(f32[1024,152,1]{1,2,0:T(1,128)} %copy.71) | copy-start | bytes 1867780
  492.1 23.7 %copy-start.1 = (f32[152,152]{1,0:T(8,128)S(1)}, f32[152,152]{1,0:T(8,128)}, u32[]{:S(2)}) copy-start(f32[152,152]{1,0:T(8,128)} %param.20) | copy-start | bytes 277252
  (4 other events, 12.9 us)
Sparse Core Ops, SparseCore 0:
  255.8 14.6 reduce-scatter.1
where the time goes:
time: 533 us; the launch traced here: 523 us
  local copies, waits for them, and re-layouts  245 us (46%)
  other arithmetic  102 us (19%)
  blocking collectives  79.1 us (15%)
  matrix products  37.4 us (7%)
  waiting for transfers between devices  21.4 us (4%)
  starting transfers between devices  18.9 us (4%)
  between operations  18.4 us (3%)
    reshape x2, local copies, waits for them, and re-layouts, per_device(): m2l_ops = m2l_ops.reshape(coef_len, -1, coef_len)  95.6 us
    scatter-add x1, other arithmetic, per_device(): level4 = jnp.zeros((coef_len, dens_dev, BOXES4), jnp.float32).at[:, :, id...  70.7 us
    gather x2, local copies, waits for them, and re-layouts, one_block(): gathered = level4_low[:, :, sources]  58.4 us
    all_gather x1, blocking collectives, per_device(): values = lax.all_gather(rounded, 'pts', axis=2, tiled=True)  27.8 us
    all_to_all x1, blocking collectives, per_device(): lax.all_to_all(reply_vals, ('pts', 'top'), split_axis=1, concat_axis=1, t...  18.2 us
    unnamed x1, blocking collectives  15.4 us
    reduce_scatter x1, waiting for transfers between devices, per_device(): lax.psum_scatter(partial_value, 'top', scatter_dimension=1, tiled=True)  12.9 us
    all_to_all x1, starting transfers between devices, per_device(): lax.all_to_all(labels, ('pts', 'top'), split_axis=1, concat_axis=1, tiled...  11.5 us
  transfers between devices with their start and end apart: 3, of which 2 were waited for; matrix products, arithmetic and copies ran while one was open for 23% of the time, Pallas kernels for 0%

commit v1 on v0

v1 whole, which is shorter than its diff:
```python
import functools
import math

import jax
import jax.numpy as jnp
import numpy as np
from jax import lax
from jax.experimental import pallas as pl
from jax.experimental.pallas import tpu as pltpu
from jax.sharding import PartitionSpec as P

LEVEL = 3
EDGE = 6
COEF = 152
OFFSETS = 316
PTS = 1024
OWN = 4096
CAP = 64
OWNERS = 32
TOP = 4
DEVS = 128
COLS = DEVS * CAP
BOXES = 512
WIN = 32
GROUPS = 38
CHUNKS = 1501
GPAD = 48
CPAD = 1536
CLASS = 80
BROWS = CLASS * COEF
CHUNK = 512

F32 = jnp.float32
BF16 = jnp.bfloat16
VM = pltpu.MemorySpace.VMEM


def surface_table():
    grid_vals = np.linspace(-1.0, 1.0, EDGE)
    points_list = []
    for a in range(EDGE):
        for b in range(EDGE):
            for c in range(EDGE):
                if min(a, b, c) == 0 or max(a, b, c) == EDGE - 1:
                    points_list.append([grid_vals[a], grid_vals[b], grid_vals[c]])
    return np.array(points_list, dtype=np.float32).T


def surface_columns():
    table = np.zeros((COEF, 8), np.float32)
    table[:, :3] = (np.float32(1.25) * surface_table()).T
    return jnp.asarray(table)


def offset_table():
    points_list = []
    for dx in range(-3, 4):
        for dy in range(-3, 4):
            for dz in range(-3, 4):
                if max(abs(dx), abs(dy), abs(dz)) >= 2:
                    points_list.append([dx, dy, dz])
    return np.array(points_list, dtype=np.int32)


def morton_decode(number):
    x = y = z = jnp.zeros_like(number)
    for bit in range(LEVEL):
        digit = number >> (3 * bit)
        x = x | (((digit >> 2) & 1) << bit)
        y = y | (((digit >> 1) & 1) << bit)
        z = z | ((digit & 1) << bit)
    return x, y, z


def morton_encode(x, y, z):
    number = jnp.zeros_like(x)
    for bit in range(LEVEL):
        digit = (((x >> bit) & 1) << 2) | (((y >> bit) & 1) << 1) | ((z >> bit) & 1)
        number = number | (digit << (3 * bit))
    return number


def split2(x):
    hi = x.astype(BF16)
    lo = (x - hi.astype(F32)).astype(BF16)
    return hi, lo


def split3(x):
    hi = x.astype(BF16)
    rest = x - hi.astype(F32)
    mid = rest.astype(BF16)
    lo = (rest - mid.astype(F32)).astype(BF16)
    return hi, mid, lo


def dot_nn(a, b):
    return lax.dot_general(a, b, (((1,), (0,)), ((), ())), preferred_element_type=F32)


def dot_nt(a, b):
    return lax.dot_general(a, b, (((1,), (1,)), ((), ())), preferred_element_type=F32)


def nt3(x, w):
    xh, xl = split2(x)
    wh, wl = split2(w)
    return dot_nt(xh, wh) + dot_nt(xl, wh) + dot_nt(xh, wl)


def iota(shape, dim):
    return lax.broadcasted_iota(jnp.int32, shape, dim)


def onehot(mask):
    return jnp.where(mask, 1.0, 0.0).astype(BF16)


def pack_kernel(pos_ref, dens_ref, slot_ref, out_ref, where_ref, load_ref):
    slot = slot_ref[...]
    owner = slot >> 12
    code = (slot & (OWN - 1)) + 1
    member = jnp.where(iota((OWNERS, PTS), 0) == owner, 1.0, 0.0)
    before = onehot(iota((PTS, PTS), 0) < iota((PTS, PTS), 1))
    prefix = dot_nn(member.astype(BF16), before)
    rank = jnp.sum(member * prefix, axis=0, keepdims=True)
    position = owner * CAP + rank.astype(jnp.int32)
    where_ref[...] = position
    load_ref[...] = jnp.zeros_like(load_ref)
    pos = pos_ref[...]
    hi = pos.astype(BF16).astype(F32)
    rest = pos - hi
    mid = rest.astype(BF16).astype(F32)
    load_ref[0:3] = hi
    load_ref[8:11] = mid
    load_ref[16:19] = rest - mid
    load_ref[3:4] = (code >> 6).astype(F32)
    load_ref[4:5] = (code & 63).astype(F32)
    dens = dens_ref[...]
    hi = dens.astype(BF16).astype(F32)
    rest = dens - hi
    mid = rest.astype(BF16).astype(F32)
    load_ref[24:32] = hi
    load_ref[32:40] = mid
    load_ref[40:48] = rest - mid
    payload = load_ref[...].astype(BF16)
    for block in range(8):
        pick = onehot(iota((256, PTS), 0) + 256 * block == position)
        res = dot_nt(payload, pick)
        head = res[0:8] + res[8:16] + res[16:24]
        slots = head[3:4] * 64.0 + head[4:5]
        dens_out = res[24:32] + res[32:40] + res[40:48]
        for part in range(4):
            own = 4 * block + part
            lanes = slice(CAP * part, CAP * part + CAP)
            for top in range(TOP):
                out_ref[TOP * own + top, 0:3, :] = head[0:3, lanes]
                out_ref[TOP * own + top, 3:4, :] = slots[:, lanes]
                out_ref[TOP * own + top, 4:6, :] = dens_out[2 * top : 2 * top + 2, lanes]


def green(recv_ref, surf_ref, cols):
    squared = None
    for dim in range(3):
        gap = surf_ref[:, dim : dim + 1] - recv_ref[dim : dim + 1, cols]
        squared = gap * gap if squared is None else squared + gap * gap
    return lax.rsqrt(squared) * (1.0 / (4.0 * math.pi))


def p2m_kernel(recv_ref, leaf_ref, surf_ref, uc2e_ref, m2m_ref, part_ref, code_ref, acc_ref):
    acc_ref[...] = jnp.zeros_like(acc_ref)
    table = leaf_ref[...].astype(BF16)

    def step(index, carry):
        cols = pl.ds(pl.multiple_of(index * CHUNK, CHUNK), CHUNK)
        slot = recv_ref[3:4, cols].astype(jnp.int32) - 1
        high = onehot(iota((64, CHUNK), 0) == (slot >> 6))
        rows = dot_nn(table, high)
        leaf = jnp.sum(
            jnp.where(iota((64, CHUNK), 0) == (slot & 63), rows, 0.0), axis=0, keepdims=True
        ).astype(jnp.int32)
        code = (leaf & 7) * WIN + (leaf >> 3)
        code_ref[:, cols] = code
        pick = onehot(iota((256, CHUNK), 0) == code)
        kernel = green(recv_ref, surf_ref, cols)
        for dens in range(2):
            hi, lo = split2(kernel * recv_ref[4 + dens : 5 + dens, cols])
            total = dot_nt(pick, hi) + dot_nt(pick, lo)
            acc_ref[:, dens] += total.reshape(8, WIN, COEF)
        return carry

    lax.fori_loop(0, COLS // CHUNK, step, 0)
    leaf_mult = nt3(acc_ref[...].reshape(2 * 256, COEF), uc2e_ref[...])
    part = nt3(leaf_mult[0:64], m2m_ref[0])
    for octant in range(1, 8):
        part = part + nt3(leaf_mult[64 * octant : 64 * octant + 64], m2m_ref[octant])
    part_ref[...] = part.astype(BF16)


def relayout_kernel(flat_ref, out_ref, stage_ref, wide_ref, sem):
    rows = 2048
    total = GROUPS * CHUNKS
    blocks = total // rows
    tail = total - blocks * rows

    def fetch(index, slot):
        return pltpu.make_async_copy(
            flat_ref.at[pl.ds(index * rows, rows)], stage_ref.at[slot], sem.at[slot]
        )

    @pl.when(pl.program_id(0) == 0)
    def _():
        fetch(0, 0).start()

        def body(index, carry):
            slot = index % 2

            @pl.when(index + 1 < blocks)
            def _():
                fetch(index + 1, 1 - slot).start()

            fetch(index, slot).wait()
            wide_ref[pl.ds(pl.multiple_of(index * rows, rows), rows)] = stage_ref[slot].astype(F32)
            return carry

        lax.fori_loop(0, blocks, body, 0)
        last = pltpu.make_async_copy(
            flat_ref.at[pl.ds(blocks * rows, tail)], stage_ref.at[0, pl.ds(0, tail)], sem.at[0]
        )
        last.start()
        last.wait()
        wide_ref[pl.ds(blocks * rows, tail)] = stage_ref[0, 0:tail].astype(F32)

    base = pl.program_id(0) * 64

    def move(index, carry):
        for part in range(8):
            chunk = base + index * 8 + part
            source = jnp.minimum(chunk, CHUNKS - 1)
            value = wide_ref[pl.ds(source, GROUPS, stride=CHUNKS), :]
            value = jnp.where(chunk < CHUNKS, value, 0.0)
            lanes = pl.ds(pl.multiple_of((index * 8 + part) * 128, 128), 128)
            out_ref[0:GROUPS, lanes] = value.astype(BF16)
        return carry

    lax.fori_loop(0, 8, move, 0)


def far_kernel(
    fb_ref,
    parts_ref,
    tbox_ref,
    nbr_ref,
    wide_hbm,
    m2m_ref,
    l2l_ref,
    lattice_ref,
    dc2e_ref,
    hi_ref,
    lo_ref,
    wide_ref,
    src_ref,
    acc_ref,
    check_ref,
    sem,
):
    bring = pltpu.make_async_copy(wide_hbm, wide_ref, sem)
    bring.start()
    row = iota((BOXES, 1), 0)
    box = ((row & 7) << 6) + (row & 56) + (row >> 6)
    place = onehot(box == tbox_ref[...])
    eye = onehot(iota((COEF, COEF), 0) == iota((COEF, COEF), 1))
    level = []
    low = []
    for dens in range(2):
        parts = parts_ref[:, dens].reshape(OWNERS * WIN, COEF)
        value = dot_nn(place, parts)
        level.append(value)
        low.append(dot_nt(eye, value.astype(BF16)).astype(BF16))
    src_ref[0:128] = jnp.zeros((128, 256), BF16)
    src_ref[128 + BROWS : 384 + BROWS] = jnp.zeros((256, 256), BF16)

    def build(pair, carry):
        pick = onehot(box == nbr_ref[pair])
        first = dot_nn(low[0], pick)
        second = dot_nn(low[1], pick)
        top = jnp.concatenate([first[:, 0:128], second[:, 0:128]], axis=1)
        bottom = jnp.concatenate([first[:, 128:256], second[:, 128:256]], axis=1)
        both = jnp.concatenate([top, bottom], axis=0).astype(BF16)
        src_ref[pl.ds(pl.multiple_of(128 + pair * 304, 16), 304)] = both
        return carry

    lax.fori_loop(0, CLASS // 2, build, 0)

    up = None
    for o in range(8):
        rows = jnp.concatenate(
            [level[0][64 * o : 64 * o + 64], level[1][64 * o : 64 * o + 64]], axis=0
        )
        term = nt3(rows, m2m_ref[o])
        up = term if up is None else up + term
    up2 = None
    for o in range(8):
        rows = jnp.concatenate([up[8 * o : 8 * o + 8], up[64 + 8 * o : 72 + 8 * o]], axis=0)
        term = nt3(rows, m2m_ref[o])
        up2 = term if up2 is None else up2 + term
    row16 = iota((16, 1), 0)
    up3 = None
    for o in range(8):
        term = nt3(jnp.where((row16 & 7) == o, up2, 0.0), m2m_ref[o])
        up3 = term if up3 is None else up3 + term
    root0 = jnp.sum(up3[0:8], axis=0, keepdims=True)
    root1 = jnp.sum(up3[8:16], axis=0, keepdims=True)
    root = jnp.where(row16 < 8, root0, root1)
    down = nt3(root, lattice_ref[...])
    down1 = None
    for o in range(8):
        term = nt3(jnp.where((row16 & 7) == o, down, 0.0), l2l_ref[o])
        down1 = term if down1 is None else down1 + term
    down2 = jnp.concatenate([nt3(down1, l2l_ref[o]) for o in range(8)], axis=0)
    row64 = iota((64, 1), 0)
    target = (fb_ref[0] + (row64 & 31)) & (BOXES - 1)
    parent = ((target >> 3) & 7) * 16 + (row64 >> 5) * 8 + (target >> 6)
    choose = onehot(iota((64, 128), 1) == parent)
    hi, mid, rest = split3(down2)
    parents = dot_nn(choose, hi) + dot_nn(choose, mid) + dot_nn(choose, rest)
    far = None
    for o in range(8):
        term = nt3(jnp.where((target & 7) == o, parents, 0.0), l2l_ref[o])
        far = term if far is None else far + term

    bring.wait()
    acc_ref[...] = jnp.zeros_like(acc_ref)
    width = 1024

    def mult(index, carry):
        for r in range(4):
            lhs = []
            for m in range(4):
                lane = pl.multiple_of(128 * (375 * r + 95 * m) + index * width, 128)
                lhs.append(wide_ref[:, pl.ds(lane, width)])
            start = pl.multiple_of(128 - 32 * r + index * width, 32)
            acc_ref[r] += dot_nn(jnp.concatenate(lhs, axis=0), src_ref[pl.ds(start, width)])
        return carry

    lax.fori_loop(0, 12, mult, 0)
    block = (iota((1, 256), 1) >> 5) & 3
    for r in range(4):
        value = None
        for m in range(4):
            term = jnp.where(block == m, acc_ref[r, GPAD * m : GPAD * m + GROUPS], 0.0)
            value = term if value is None else value + term
        for half in range(2):
            lanes = slice(128 * half, 128 * half + 128)
            check_ref[half, pl.ds(r, GROUPS, stride=4), :] = value[:, lanes]
    lane = iota((64, 256), 1)
    fold = onehot(((lane & 31) == (row64 & 31)) & ((lane >> 7) == (row64 >> 5)))
    hi, mid, rest = split3(jnp.concatenate([check_ref[0], check_ref[1]], axis=1))
    checks = dot_nt(fold, hi) + dot_nt(fold, mid) + dot_nt(fold, rest)
    local = nt3(checks, dc2e_ref[...]) + far
    leaves = [nt3(local, l2l_ref[o]) for o in range(8)]
    for dens in range(2):
        value = jnp.concatenate([leaf[WIN * dens : WIN * dens + WIN] for leaf in leaves], axis=0)
        hi, lo = split2(value)
        hi_ref[dens] = dot_nt(eye, hi).astype(BF16)
        lo_ref[dens] = dot_nt(eye, lo).astype(BF16)


def l2p_kernel(recv_ref, code_ref, surf_ref, hi_ref, lo_ref, out_ref):
    def step(index, carry):
        cols = pl.ds(pl.multiple_of(index * CHUNK, CHUNK), CHUNK)
        pick = onehot(iota((256, CHUNK), 0) == code_ref[:, cols])
        kernel = green(recv_ref, surf_ref, cols)
        for dens in range(2):
            value = dot_nn(hi_ref[dens], pick) + dot_nn(lo_ref[dens], pick)
            out_ref[dens : dens + 1, cols] = jnp.sum(kernel * value, axis=0, keepdims=True)
        return carry

    lax.fori_loop(0, COLS // CHUNK, step, 0)


def unpack_kernel(back_ref, where_ref, out_ref):
    pieces = split3(back_ref[...])
    position = where_ref[...]
    total = jnp.zeros((8, PTS), F32)
    for block in range(8):
        pick = onehot(iota((256, PTS), 0) + 256 * block == position)
        cols = slice(256 * block, 256 * block + 256)
        for piece in pieces:
            total = total + dot_nn(piece[:, cols], pick)
    out_ref[...] = total


def whole(count):
    return [pl.BlockSpec(memory_space=VM)] * count


def limits(mib):
    return pltpu.CompilerParams(vmem_limit_bytes=mib * 1024 * 1024)


def per_device(
    local_pos, densities, morton_slot, slot_leaf, uc2e, m2m, m2l_ops, dc2e, lattice, l2l
):
    m2m = m2m.reshape(8, COEF, COEF)
    l2l = l2l.reshape(8, COEF, COEF)
    surf = surface_columns()
    leaves = lax.all_gather(slot_leaf, "top", axis=0, tiled=True)
    starts = lax.all_gather(slot_leaf[:1], ("pts", "top"), axis=0, tiled=True)
    first_box = leaves[0] // 8
    leaf_table = (leaves - 8 * first_box).reshape(64, 64).T.astype(F32)
    first_all = starts.reshape(OWNERS, TOP)[:, 0] // 8
    slide = jnp.arange(WIN, dtype=jnp.int32)
    tbox = (first_all[:, None] + slide[None, :]).reshape(1, OWNERS * WIN)
    targets = (first_box + slide) & (BOXES - 1)
    tx, ty, tz = morton_decode(targets)
    offsets = np.zeros((4 * CLASS, 3), np.int32)
    offsets[:OFFSETS] = offset_table()
    offsets = jnp.asarray(offsets.reshape(4, CLASS, 3).transpose(1, 0, 2))
    known = jnp.asarray((np.arange(4 * CLASS) < OFFSETS).reshape(4, CLASS).T)
    nbr = morton_encode(
        (tx + offsets[:, :, 0:1]) & 7, (ty + offsets[:, :, 1:2]) & 7, (tz + offsets[:, :, 2:3]) & 7
    )
    nbr = jnp.where(known[:, :, None], nbr, -1).reshape(CLASS // 2, 1, 256)

    flat = m2l_ops.reshape(GROUPS * CHUNKS, 128)
    wide = pl.pallas_call(
        relayout_kernel,
        grid=(CPAD // 64,),
        out_shape=jax.ShapeDtypeStruct((GPAD, CPAD * 128), BF16),
        in_specs=[pl.BlockSpec(memory_space=pl.ANY)],
        out_specs=pl.BlockSpec((GPAD, 64 * 128), lambda i: (0, i)),
        scratch_shapes=[
            pltpu.VMEM((2, 2048, 128), BF16),
            pltpu.VMEM((GROUPS * CHUNKS, 128), F32),
            pltpu.SemaphoreType.DMA((2,)),
        ],
        compiler_params=limits(60),
        name="relayout",
    )(flat)

    send, position = pl.pallas_call(
        pack_kernel,
        out_shape=(
            jax.ShapeDtypeStruct((DEVS, 6, CAP), F32),
            jax.ShapeDtypeStruct((1, PTS), jnp.int32),
        ),
        in_specs=whole(3),
        out_specs=tuple(whole(2)),
        scratch_shapes=[pltpu.VMEM((48, PTS), F32)],
        compiler_params=limits(32),
        name="pack",
    )(local_pos, densities, morton_slot.reshape(1, PTS))

    recv = lax.all_to_all(send, ("pts", "top"), split_axis=0, concat_axis=0, tiled=True)
    recv = recv.transpose(1, 0, 2).reshape(6, COLS)

    part, code = pl.pallas_call(
        p2m_kernel,
        out_shape=(
            jax.ShapeDtypeStruct((2 * WIN, COEF), BF16),
            jax.ShapeDtypeStruct((1, COLS), jnp.int32),
        ),
        in_specs=whole(5),
        out_specs=tuple(whole(2)),
        scratch_shapes=[pltpu.VMEM((8, 2, WIN, COEF), F32)],
        compiler_params=limits(32),
        name="p2m",
    )(recv, leaf_table, surf, uc2e, m2m)

    parts = lax.all_gather(part, "pts", axis=0, tiled=False).reshape(OWNERS, 2, WIN, COEF)

    hi, lo = pl.pallas_call(
        far_kernel,
        out_shape=(
            jax.ShapeDtypeStruct((2, COEF, 256), BF16),
            jax.ShapeDtypeStruct((2, COEF, 256), BF16),
        ),
        in_specs=[pl.BlockSpec(memory_space=pltpu.MemorySpace.SMEM)]
        + whole(3)
        + [pl.BlockSpec(memory_space=pl.ANY)]
        + whole(4),
        out_specs=tuple(whole(2)),
        scratch_shapes=[
            pltpu.VMEM((GPAD, CPAD * 128), BF16),
            pltpu.VMEM((BROWS + 384, 256), BF16),
            pltpu.VMEM((4, 4 * GPAD, 256), F32),
            pltpu.VMEM((2, COEF, 128), F32),
            pltpu.SemaphoreType.DMA,
        ],
        compiler_params=limits(60),
        name="far",
    )(first_box.reshape(1), parts, tbox, nbr, wide, m2m, l2l, lattice, dc2e)

    pot = pl.pallas_call(
        l2p_kernel,
        out_shape=jax.ShapeDtypeStruct((2, COLS), F32),
        in_specs=whole(5),
        out_specs=whole(1)[0],
        compiler_params=limits(32),
        name="l2p",
    )(recv, code, surf, hi, lo)

    reply = pot.reshape(2, DEVS, CAP).transpose(1, 0, 2)
    back = lax.all_to_all(reply, ("pts", "top"), split_axis=0, concat_axis=0, tiled=True)
    back = back.reshape(OWNERS, TOP, 2, CAP).transpose(1, 2, 0, 3).reshape(8, OWNERS * CAP)
    return pl.pallas_call(
        unpack_kernel,
        out_shape=jax.ShapeDtypeStruct((8, PTS), F32),
        in_specs=whole(2),
        out_specs=whole(1)[0],
        compiler_params=limits(32),
        name="unpack",
    )(back, position)


def solution(mesh):
    placed = (
        P(None, ("pts", "top")),
        P(None, ("pts", "top")),
        P(("pts", "top")),
        P(("pts", "top")),
        P(),
        P(),
        P(),
        P(),
        P(),
        P(),
    )
    return jax.shard_map(
        per_device, mesh=mesh, in_specs=placed, out_specs=P(None, ("pts", "top")), check_vma=False
    )
```

time: 533 us -> 238 us (0.45); the launches traced: 523 us -> 237 us
  local copies, waits for them, and re-layouts: 245 us -> 16.6 us
  other arithmetic: 102 us -> 3.11 us
  Pallas kernels: 0 us -> 84 us
  blocking collectives: 79.1 us -> 119 us
  matrix products: 37.4 us -> 0 us
  waiting for transfers between devices: 21.4 us -> 0.01 us
  between operations: 18.4 us -> 2.84 us
  starting transfers between devices: 18.9 us -> 11.5 us
    reshape x9 -> x6, local copies, waits for them, and re-layouts: 109 us -> 7.48 us  [the longest x1 4.26 us: per_device(): l2l = l2l.reshape(8, COEF, COEF)]
    gather x20 -> x0, local copies, waits for them, and re-layouts: 101 us -> none  [the longest x2 58.4 us: one_block(): gathered = level4_low[:, :, sources]]
    pallas_call x0 -> x6, Pallas kernels: none -> 84 us  [the longest x1 32.2 us: per_device(): pl.pallas_call(relayout_kernel, grid=(CPAD // 64,), out_shape=jax.ShapeDt...]
    scatter-add x2 -> x0, other arithmetic: 82 us -> none  [the longest x1 70.7 us: per_device(): level4 = jnp.zeros((coef_len, dens_dev, BOXES4), jnp.float32).at[:, :, id...]
    unnamed x1, blocking collectives: 15.4 us -> 67.1 us
    dot_general x13 -> x0, matrix products: 37.4 us -> none  [the longest x1 11.3 us: one_block(): jnp.einsum('cds,skdt->ckt', m2l_ops, gathered, preferred_element_type=jnp...]
    scatter x3 -> x0, local copies, waits for them, and re-layouts: 13.4 us -> none  [the longest x1 5.72 us: per_device(): jnp.zeros((3 + DENS, points_dev), jnp.float32).at[:, arrivals[0]]]
    reduce_scatter x1 -> x0, waiting for transfers between devices: 12.9 us -> none  [per_device(): lax.psum_scatter(partial_value, 'top', scatter_dimension=1, tiled=True)]
  transfers between devices with their start and end apart: 3 -> 1, of which waited for: 2 -> 0; matrix products, arithmetic and copies ran while one was open for 23% -> 5% of each run, Pallas kernels for 0% -> 14%
where the time goes in v1:
time: 238 us; the launch traced here: 237 us
  blocking collectives  119 us (50%)
  Pallas kernels  84 us (35%)
  local copies, waits for them, and re-layouts  16.6 us (7%)
  starting transfers between devices  11.5 us (5%)
  other arithmetic  3.11 us (1%)
  between operations  2.84 us (1%)
    unnamed x1, blocking collectives  67.1 us
    pallas_call x1, Pallas kernels, per_device(): pl.pallas_call(relayout_kernel, grid=(CPAD // 64,), out_shape=jax.ShapeDt...  32.2 us
    pallas_call x1, Pallas kernels, per_device(): pl.pallas_call(far_kernel, out_shape=(jax.ShapeDtypeStruct((2, COEF, 256)...  29.7 us
    all_gather x1, blocking collectives, per_device(): lax.all_gather(part, 'pts', axis=0, tiled=False)  27.1 us
    all_to_all x1, blocking collectives, per_device(): lax.all_to_all(reply, ('pts', 'top'), split_axis=0, concat_axis=0, tiled=...  14.3 us
    pallas_call x1, Pallas kernels, per_device(): pl.pallas_call(p2m_kernel, out_shape=(jax.ShapeDtypeStruct((2 * WIN, COEF...  12.1 us
    all_to_all x1, starting transfers between devices, per_device(): lax.all_to_all(send, ('pts', 'top'), split_axis=0, concat_axis=0, tiled=T...  11.5 us
    all_gather x1, blocking collectives, per_device(): leaves = lax.all_gather(slot_leaf, 'top', axis=0, tiled=True)  10.6 us
  transfers between devices with their start and end apart: 1, of which 0 were waited for; matrix products, arithmetic and copies ran while one was open for 5% of the time, Pallas kernels for 14%

profile of v1, /device:TPU:1, one launch (start us, length us, event | category | flops | bytes accessed | tf_op | source)
XLA Modules:
  0.0 237.2 jit_solution(10532723388273239767)
XLA Ops:
  0.0 0.8 copy-done.5
  0.8 0.7 copy-done.6
  1.5 0.7 copy-done.7
  2.2 1.9 pack.1
  4.0 1.0 reshape.367
  5.0 11.5 %all-to-all-start = ((f32[128,1,384]{2,1,0:T(1,128)}), f32[128,1,384]{2,1,0:T(1,128)S(1)}, u32[]{:S(2)}, u32[]{:S(2)}) async-start(f32[128,1,384]{2,1,0:T(1,128)} %reshape.367), calls=%async_computation | async-start | bytes 393216 | tf_op jit(solution)/shard_map/all_to_all | solution.py:455
  16.5 10.6 %all_gather.12 = s32[4096]{0:T(1024)S(1)} all-gather(s32[1024]{0:T(1024)} %param.16), channel_id=1, replica_groups=mesh['pts'=32,'top'=4] {'top'}, dimensions={0}, use_global_device_ids=true | all-gather | bytes 20480 | tf_op jit(solution)/shard_map/all_gather | solution.py:408
  30.2 0.8 slice_dynamic-update-slice_fusion
  31.0 67.1 %all-reduce = s32[128]{0:T(128)S(1)} all-reduce(s32[128]{0:T(128)S(1)} %slice_dynamic-update-slice_fusion), channel_id=1, replica_groups=mesh['pts'=32,'top'=4] {'pts','top'}, use_global_device_ids=true, to_apply=%add | all-reduce | flops 128 | bytes 1024
  99.2 0.9 or_select_fusion
  100.2 0.8 reshape.365.nbr_ref
  101.0 2.8 %reshape.324.m2m_ref = f32[8,152,152]{2,1,0:T(8,128)S(1)} reshape(f32[184832]{0:T(1024)} %param.18) | data formatting | bytes 1478656 | tf_op jit(solution)/shard_map/reshape | solution.py:405
  103.8 4.3 %reshape.329.l2l_ref = f32[8,152,152]{2,1,0:T(8,128)} reshape(f32[184832]{0:T(1024)} %param.22) | data formatting | bytes 1478656 | tf_op jit(solution)/shard_map/reshape | solution.py:406
  108.1 32.2 %relayout.1.wide_hbm = bf16[48,196608]{1,0:T(8,128)(2,1)} custom-call(bf16[57038,128]{1,0:T(8,128)(2,1)} %bitcast.15), custom_call_target="tpu_custom_call" | custom-call | tf_op jit(solution)/shard_map/relayout/pallas_call | solution.py:427
  140.9 1.2 reduce.2
  142.4 12.1 %p2m.1 = (bf16[64,152]{1,0:T(8,128)(2,1)S(1)}, s32[1,8192]{1,0:T(1,128)S(1)}) custom-call(f32[6,8192]{1,0:T(8,128)S(1)} %reshape.323.recv_ref, f32[64,64]{1,0:T(8,128)S(1)} %bitcast.13, f32[152,8]{1,0:T(8,128)S(1)} %copy-done.1, f32[152,152]{1,0:T(8,128)S(1)} %copy-done.2, f32[8,152,152]{2,1,0:T(8,128)S(1)} %reshape.324.m2m_ref), custom_call_target="tpu_custom_call" | custom-call | tf_op jit(solution)/shard_map/p2m/pallas_call | solution.py:458
  154.5 27.1 %all-gather = bf16[2048,152]{1,0:T(8,128)(2,1)} all-gather(bf16[64,152]{1,0:T(8,128)(2,1)S(1)} %get-tuple-element.13), channel_id=2, replica_groups=mesh['pts'=32,'top'=4] {'pts'}, dimensions={0}, use_global_device_ids=true | all-gather | bytes 642048 | tf_op jit(solution)/shard_map/all_gather | solution.py:471
  181.6 29.7 %far.1 = (bf16[2,152,256]{2,1,0:T(8,128)(2,1)}, bf16[2,152,256]{2,1,0:T(8,128)(2,1)}) custom-call(s32[1]{0:T(128)} %bitcast.4.fb_ref, bf16[32,2,32,152]{3,2,1,0:T(8,128)(2,1)} %bitcast.16, s32[1,1024]{1,0:T(1,128)} %add.117.tbox_ref, s32[40,1,256]{2,1,0:T(1,128)} %reshape.365.nbr_ref, bf16[48,196608]{1,0:T(8,128)(2,1)} %relayout.1.wide_hbm, ...), custom_call_target="tpu_custom_call" | custom-call | tf_op jit(solution)/shard_map/far/pallas_call | solution.py:473
  211.4 0.9 copy-done.3
  212.3 0.9 copy-done.4
  213.2 5.8 %l2p.1 = f32[2,8192]{1,0:T(2,128)S(1)} custom-call(f32[6,8192]{1,0:T(8,128)S(1)} %reshape.323.recv_ref, s32[1,8192]{1,0:T(1,128)S(1)} %get-tuple-element.12.code_ref, f32[152,8]{1,0:T(8,128)S(1)} %copy-done.1, bf16[2,152,256]{2,1,0:T(8,128)(2,1)S(1)} %copy-done.3, bf16[2,152,256]{2,1,0:T(8,128)(2,1)S(1)} %copy-done.4), custom_call_target="tpu_custom_call" | custom-call | tf_op jit(solution)/shard_map/l2p/pallas_call | solution.py:495
  219.4 14.3 %all_to_all.10 = f32[128,1,128]{2,1,0:T(1,128)S(1)} all-to-all(f32[128,1,128]{2,1,0:T(1,128)S(1)} %reshape.369), channel_id=1, replica_groups=mesh['pts'=32,'top'=4] {'pts','top'}, dimensions={0} | all-to-all | bytes 131072 | tf_op jit(solution)/shard_map/all_to_all | solution.py:505
  233.7 0.8 reduce.3
  234.8 2.4 %unpack.1 = f32[8,1024]{1,0:T(8,128)} custom-call(f32[8,2048]{1,0:T(8,128)S(1)} %reshape.332.back_ref, s32[1,1024]{1,0:T(1,128)S(1)} %get-tuple-element.16.where_ref), custom_call_target="tpu_custom_call" | custom-call | tf_op jit(solution)/shard_map/unpack/pallas_call | solution.py:507
  (35 shorter events, 3.4 us)
Async XLA Ops:
  0.0 0.8 copy-start.5
  0.8 0.7 copy-start.6
  1.5 0.7 copy-start.7
  5.0 135.3 %all-to-all-start = ((f32[128,1,384]{2,1,0:T(1,128)}), f32[128,1,384]{2,1,0:T(1,128)S(1)}, u32[]{:S(2)}, u32[]{:S(2)}) async-start(f32[128,1,384]{2,1,0:T(1,128)} %reshape.367), calls=%async_computation | async-start | bytes 393216 | tf_op jit(solution)/shard_map/all_to_all | solution.py:455
  103.8 38.6 %copy-start = (f32[8,152,152]{2,1,0:T(8,128)}, f32[8,152,152]{2,1,0:T(8,128)S(1)}, u32[]{:S(2)}) copy-start(f32[8,152,152]{2,1,0:T(8,128)S(1)} %reshape.324.m2m_ref) | copy-start | bytes 2217988
  108.1 34.4 %copy-start.1 = (f32[152,8]{1,0:T(8,128)S(1)}, f32[152,8]{1,0:T(8,128)}, u32[]{:S(2)}) copy-start(f32[152,8]{1,0:T(8,128)} %constant.48.clone.surf_ref) | copy-start | bytes 14596
  108.1 34.4 %copy-start.2 = (f32[152,152]{1,0:T(8,128)S(1)}, f32[152,152]{1,0:T(8,128)}, u32[]{:S(2)}) copy-start(f32[152,152]{1,0:T(8,128)} %uc2e_ref.1) | copy-start | bytes 277252
  211.4 0.9 copy-start.3
  212.3 0.9 copy-start.4

commit v2 on v1

--- a/solution.py
+++ b/solution.py
@@ -24,8 +24,12 @@
 WIN = 32
 GROUPS = 38
 CHUNKS = 1501
-GPAD = 48
-CPAD = 1536
+GPAD = 40
+WIDE = 60048
+PIECE = 1440
+PIECES = 40
+DEPTH = 8
+TAIL = COEF - 128
 CLASS = 80
 BROWS = CLASS * COEF
 CHUNK = 512
@@ -33,6 +37,7 @@
 F32 = jnp.float32
 BF16 = jnp.bfloat16
 VM = pltpu.MemorySpace.VMEM
+MESH = pl.DeviceIdType.MESH
 
 
 def surface_table():
@@ -103,9 +108,11 @@
 
 
 def nt3(x, w):
+    rows = x.shape[0]
     xh, xl = split2(x)
     wh, wl = split2(w)
-    return dot_nt(xh, wh) + dot_nt(xl, wh) + dot_nt(xh, wl)
+    both = dot_nt(jnp.concatenate([xh, xl], axis=0), wh)
+    return both[:rows] + both[rows:] + dot_nt(xh, wl)
 
 
 def iota(shape, dim):
@@ -167,8 +174,38 @@
     return lax.rsqrt(squared) * (1.0 / (4.0 * math.pi))
 
 
-def p2m_kernel(recv_ref, leaf_ref, surf_ref, uc2e_ref, m2m_ref, part_ref, code_ref, acc_ref):
+def p2m_kernel(
+    fb_ref,
+    recv_ref,
+    leaf_ref,
+    surf_ref,
+    uc2e_ref,
+    m2m_ref,
+    gath_ref,
+    code_ref,
+    acc_ref,
+    pad_ref,
+    send_sem,
+    recv_sem,
+    pass_sem,
+    take_sem,
+):
+    me = lax.axis_index("pts")
+    x, y, core = me // 8, (me // 2) % 4, me % 2
+    partner = me + 1 - 2 * core
+
+    def other(step, sign, side):
+        return ((x + sign * (step // 4) + 4) % 4) * 8 + ((y + sign * (step % 4) + 4) % 4) * 2 + side
+
+    barrier = pltpu.get_barrier_semaphore()
+    for step in range(1, 16):
+        pl.semaphore_signal(
+            barrier, inc=1, device_id={"pts": other(step, 1, core)}, device_id_type=MESH
+        )
+    pl.semaphore_signal(barrier, inc=1, device_id={"pts": partner}, device_id_type=MESH)
+
     acc_ref[...] = jnp.zeros_like(acc_ref)
+    pad_ref[...] = jnp.zeros_like(pad_ref)
     table = leaf_ref[...].astype(BF16)
 
     def step(index, carry):
@@ -194,103 +231,149 @@
     part = nt3(leaf_mult[0:64], m2m_ref[0])
     for octant in range(1, 8):
         part = part + nt3(leaf_mult[64 * octant : 64 * octant + 64], m2m_ref[octant])
-    part_ref[...] = part.astype(BF16)
-
-
-def relayout_kernel(flat_ref, out_ref, stage_ref, wide_ref, sem):
-    rows = 2048
-    total = GROUPS * CHUNKS
-    blocks = total // rows
-    tail = total - blocks * rows
-
-    def fetch(index, slot):
-        return pltpu.make_async_copy(
-            flat_ref.at[pl.ds(index * rows, rows)], stage_ref.at[slot], sem.at[slot]
+    pad_ref[:, 0:COEF] = part
+    first = fb_ref[0]
+    lane = iota((16, 128), 1)
+    tail = jnp.where(
+        lane == 96,
+        (first >> 3).astype(F32),
+        jnp.where(lane == 97, (first & 7).astype(F32), 0.0),
+    )
+    for group in range(4):
+        piece = pad_ref[16 * group : 16 * group + 16, 128:256]
+        tail = tail + (pltpu.roll(piece, TAIL * group, 1) if group else piece)
+    gath_ref[me, 0:64] = pad_ref[:, 0:128].astype(BF16)
+    gath_ref[me, 64:80] = tail.astype(BF16)
+
+    pl.semaphore_wait(barrier, 16)
+
+    def copy(slot, sems, index, target):
+        return pltpu.make_async_remote_copy(
+            src_ref=gath_ref.at[slot],
+            dst_ref=gath_ref.at[slot],
+            send_sem=sems[0].at[index],
+            recv_sem=sems[1].at[index],
+            device_id={"pts": target},
+            device_id_type=MESH,
         )
 
-    @pl.when(pl.program_id(0) == 0)
-    def _():
-        fetch(0, 0).start()
-
-        def body(index, carry):
-            slot = index % 2
-
-            @pl.when(index + 1 < blocks)
-            def _():
-                fetch(index + 1, 1 - slot).start()
-
-            fetch(index, slot).wait()
-            wide_ref[pl.ds(pl.multiple_of(index * rows, rows), rows)] = stage_ref[slot].astype(F32)
-            return carry
-
-        lax.fori_loop(0, blocks, body, 0)
-        last = pltpu.make_async_copy(
-            flat_ref.at[pl.ds(blocks * rows, tail)], stage_ref.at[0, pl.ds(0, tail)], sem.at[0]
-        )
-        last.start()
-        last.wait()
-        wide_ref[pl.ds(blocks * rows, tail)] = stage_ref[0, 0:tail].astype(F32)
-
-    base = pl.program_id(0) * 64
-
-    def move(index, carry):
-        for part in range(8):
-            chunk = base + index * 8 + part
-            source = jnp.minimum(chunk, CHUNKS - 1)
-            value = wide_ref[pl.ds(source, GROUPS, stride=CHUNKS), :]
-            value = jnp.where(chunk < CHUNKS, value, 0.0)
-            lanes = pl.ds(pl.multiple_of((index * 8 + part) * 128, 128), 128)
-            out_ref[0:GROUPS, lanes] = value.astype(BF16)
-        return carry
-
-    lax.fori_loop(0, 8, move, 0)
+    far = (send_sem, recv_sem)
+    near = (pass_sem, take_sem)
+    copy(me, near, 0, partner).start()
+    for step in range(1, 16):
+        copy(me, far, step, other(step, 1, core)).start()
+    for step in range(1, 16):
+        slot = other(step, -1, core)
+        copy(slot, far, step, partner).wait_recv()
+        copy(slot, near, step, partner).start()
+    copy(partner, near, 0, partner).wait_recv()
+    for step in range(1, 16):
+        copy(other(step, -1, 1 - core), near, step, partner).wait_recv()
+    copy(me, near, 0, partner).wait_send()
+    for step in range(1, 16):
+        copy(me, far, step, partner).wait_send()
+        copy(other(step, -1, core), near, step, partner).wait_send()
 
 
 def far_kernel(
     fb_ref,
     parts_ref,
-    tbox_ref,
     nbr_ref,
-    wide_hbm,
+    flat_hbm,
     m2m_ref,
     l2l_ref,
     lattice_ref,
     dc2e_ref,
     hi_ref,
     lo_ref,
+    stage_ref,
     wide_ref,
     src_ref,
     acc_ref,
     check_ref,
     sem,
 ):
-    bring = pltpu.make_async_copy(wide_hbm, wide_ref, sem)
-    bring.start()
+    def fetch(index, size):
+        return pltpu.make_async_copy(
+            flat_hbm.at[pl.ds(index * PIECE, size)],
+            stage_ref.at[index % DEPTH, pl.ds(0, size)],
+            sem.at[index % DEPTH],
+        )
+
+    last = GROUPS * CHUNKS - (PIECES - 1) * PIECE
+    for index in range(DEPTH):
+        fetch(index, PIECE).start()
     row = iota((BOXES, 1), 0)
     box = ((row & 7) << 6) + (row & 56) + (row >> 6)
-    place = onehot(box == tbox_ref[...])
     eye = onehot(iota((COEF, COEF), 0) == iota((COEF, COEF), 1))
+    codes = parts_ref[:, 64, :].astype(F32)
+    lane = iota((OWNERS, 128), 1)
+    first = jnp.sum(
+        jnp.where(lane == 96, 8.0 * codes, jnp.where(lane == 97, codes, 0.0)),
+        axis=1,
+        keepdims=True,
+    )
+    spread = jnp.where(iota((OWNERS, 512), 0) == (iota((OWNERS, 512), 1) >> 4), first, 0.0)
+    start = jnp.sum(spread, axis=0, keepdims=True).astype(jnp.int32)
+    start = start + (iota((1, 512), 1) & 15)
+    halves = []
+    for half in range(2):
+        place = onehot(box == start + 16 * half)
+        pieces = [
+            parts_ref[:, 32 * dens + 16 * half : 32 * dens + 16 * half + 16, :].reshape(512, 128)
+            for dens in range(2)
+        ]
+        pieces.append(parts_ref[:, 64:80, :].reshape(512, 128))
+        halves.append(dot_nn(place, jnp.concatenate(pieces, axis=1)))
     level = []
-    low = []
     for dens in range(2):
-        parts = parts_ref[:, dens].reshape(OWNERS * WIN, COEF)
-        value = dot_nn(place, parts)
+        main = slice(128 * dens, 128 * dens + 128)
+        tail = 256 + 2 * TAIL * dens
+        value = jnp.concatenate(
+            [
+                halves[0][:, main] + halves[1][:, main],
+                halves[0][:, tail : tail + TAIL] + halves[1][:, tail + TAIL : tail + 2 * TAIL],
+            ],
+            axis=1,
+        )
         level.append(value)
-        low.append(dot_nt(eye, value.astype(BF16)).astype(BF16))
+    low = jnp.concatenate([dot_nt(eye, value.astype(BF16)) for value in level], axis=0)
+    low = low.astype(BF16)
     src_ref[0:128] = jnp.zeros((128, 256), BF16)
     src_ref[128 + BROWS : 384 + BROWS] = jnp.zeros((256, 256), BF16)
+    wide_ref[PIECES * PIECE : WIDE] = jnp.zeros((WIDE - PIECES * PIECE, 128), F32)
 
     def build(pair, carry):
         pick = onehot(box == nbr_ref[pair])
-        first = dot_nn(low[0], pick)
-        second = dot_nn(low[1], pick)
-        top = jnp.concatenate([first[:, 0:128], second[:, 0:128]], axis=1)
-        bottom = jnp.concatenate([first[:, 128:256], second[:, 128:256]], axis=1)
+        found = dot_nn(low, pick)
+        top = jnp.concatenate([found[0:COEF, 0:128], found[COEF:, 0:128]], axis=1)
+        bottom = jnp.concatenate([found[0:COEF, 128:256], found[COEF:, 128:256]], axis=1)
         both = jnp.concatenate([top, bottom], axis=0).astype(BF16)
         src_ref[pl.ds(pl.multiple_of(128 + pair * 304, 16), 304)] = both
+
+        @pl.when(pair < PIECES - 1)
+        def _():
+            fetch(pair, PIECE).wait()
+
+        @pl.when(pair == PIECES - 1)
+        def _():
+            fetch(pair, last).wait()
+
+        wide_ref[pl.ds(pl.multiple_of(pair * PIECE, 32), PIECE)] = stage_ref[pair % DEPTH].astype(
+            F32
+        )
+
+        @pl.when(pair + DEPTH < PIECES - 1)
+        def _():
+            fetch(pair + DEPTH, PIECE).start()
+
+        @pl.when(pair + DEPTH == PIECES - 1)
+        def _():
+            fetch(pair + DEPTH, last).start()
+
         return carry
 
-    lax.fori_loop(0, CLASS // 2, build, 0)
+    lax.fori_loop(0, PIECES, build, 0)
 
     up = None
     for o in range(8):
@@ -329,18 +412,23 @@
         term = nt3(jnp.where((target & 7) == o, parents, 0.0), l2l_ref[o])
         far = term if far is None else far + term
 
-    bring.wait()
     acc_ref[...] = jnp.zeros_like(acc_ref)
-    width = 1024
 
     def mult(index, carry):
         for r in range(4):
             lhs = []
             for m in range(4):
-                lane = pl.multiple_of(128 * (375 * r + 95 * m) + index * width, 128)
-                lhs.append(wide_ref[:, pl.ds(lane, width)])
-            start = pl.multiple_of(128 - 32 * r + index * width, 32)
-            acc_ref[r] += dot_nn(jnp.concatenate(lhs, axis=0), src_ref[pl.ds(start, width)])
+                chunk = 375 * r + 95 * m + index * 8
+                lhs.append(
+                    jnp.concatenate(
+                        [wide_ref[pl.ds(chunk + q, GPAD, stride=CHUNKS), :] for q in range(8)],
+                        axis=1,
+                    )
+                )
+            begin = pl.multiple_of(128 - 32 * r + index * 1024, 32)
+            acc_ref[r] += dot_nn(
+                jnp.concatenate(lhs, axis=0).astype(BF16), src_ref[pl.ds(begin, 1024)]
+            )
         return carry
 
     lax.fori_loop(0, 12, mult, 0)
@@ -406,12 +494,9 @@
     l2l = l2l.reshape(8, COEF, COEF)
     surf = surface_columns()
     leaves = lax.all_gather(slot_leaf, "top", axis=0, tiled=True)
-    starts = lax.all_gather(slot_leaf[:1], ("pts", "top"), axis=0, tiled=True)
-    first_box = leaves[0] // 8
+    first_box = leaves[0] >> 3
     leaf_table = (leaves - 8 * first_box).reshape(64, 64).T.astype(F32)
-    first_all = starts.reshape(OWNERS, TOP)[:, 0] // 8
     slide = jnp.arange(WIN, dtype=jnp.int32)
-    tbox = (first_all[:, None] + slide[None, :]).reshape(1, OWNERS * WIN)
     targets = (first_box + slide) & (BOXES - 1)
     tx, ty, tz = morton_decode(targets)
     offsets = np.zeros((4 * CLASS, 3), np.int32)
@@ -424,21 +509,6 @@
     nbr = jnp.where(known[:, :, None], nbr, -1).reshape(CLASS // 2, 1, 256)
 
     flat = m2l_ops.reshape(GROUPS * CHUNKS, 128)
-    wide = pl.pallas_call(
-        relayout_kernel,
-        grid=(CPAD // 64,),
-        out_shape=jax.ShapeDtypeStruct((GPAD, CPAD * 128), BF16),
-        in_specs=[pl.BlockSpec(memory_space=pl.ANY)],
-        out_specs=pl.BlockSpec((GPAD, 64 * 128), lambda i: (0, i)),
-        scratch_shapes=[
-            pltpu.VMEM((2, 2048, 128), BF16),
-            pltpu.VMEM((GROUPS * CHUNKS, 128), F32),
-            pltpu.SemaphoreType.DMA((2,)),
-        ],
-        compiler_params=limits(60),
-        name="relayout",
-    )(flat)
-
     send, position = pl.pallas_call(
         pack_kernel,
         out_shape=(
@@ -455,20 +525,29 @@
     recv = lax.all_to_all(send, ("pts", "top"), split_axis=0, concat_axis=0, tiled=True)
     recv = recv.transpose(1, 0, 2).reshape(6, COLS)
 
-    part, code = pl.pallas_call(
+    fb = first_box.reshape(1)
+    smem = [pl.BlockSpec(memory_space=pltpu.MemorySpace.SMEM)]
+    parts, code = pl.pallas_call(
         p2m_kernel,
         out_shape=(
-            jax.ShapeDtypeStruct((2 * WIN, COEF), BF16),
+            jax.ShapeDtypeStruct((OWNERS, 80, 128), BF16),
             jax.ShapeDtypeStruct((1, COLS), jnp.int32),
         ),
-        in_specs=whole(5),
+        in_specs=smem + whole(5),
         out_specs=tuple(whole(2)),
-        scratch_shapes=[pltpu.VMEM((8, 2, WIN, COEF), F32)],
-        compiler_params=limits(32),
+        scratch_shapes=[
+            pltpu.VMEM((8, 2, WIN, COEF), F32),
+            pltpu.VMEM((2 * WIN, 256), F32),
+            pltpu.SemaphoreType.DMA((16,)),
+            pltpu.SemaphoreType.DMA((16,)),
+            pltpu.SemaphoreType.DMA((16,)),
+            pltpu.SemaphoreType.DMA((16,)),
+        ],
+        compiler_params=pltpu.CompilerParams(
+            vmem_limit_bytes=32 * 1024 * 1024, collective_id=0, has_side_effects=True
+        ),
         name="p2m",
-    )(recv, leaf_table, surf, uc2e, m2m)
-
-    parts = lax.all_gather(part, "pts", axis=0, tiled=False).reshape(OWNERS, 2, WIN, COEF)
+    )(fb, recv, leaf_table, surf, uc2e, m2m)
 
     hi, lo = pl.pallas_call(
         far_kernel,
@@ -476,21 +555,19 @@
             jax.ShapeDtypeStruct((2, COEF, 256), BF16),
             jax.ShapeDtypeStruct((2, COEF, 256), BF16),
         ),
-        in_specs=[pl.BlockSpec(memory_space=pltpu.MemorySpace.SMEM)]
-        + whole(3)
-        + [pl.BlockSpec(memory_space=pl.ANY)]
-        + whole(4),
+        in_specs=smem + whole(2) + [pl.BlockSpec(memory_space=pl.ANY)] + whole(4),
         out_specs=tuple(whole(2)),
         scratch_shapes=[
-            pltpu.VMEM((GPAD, CPAD * 128), BF16),
+            pltpu.VMEM((DEPTH, PIECE, 128), BF16),
+            pltpu.VMEM((WIDE, 128), F32),
             pltpu.VMEM((BROWS + 384, 256), BF16),
             pltpu.VMEM((4, 4 * GPAD, 256), F32),
             pltpu.VMEM((2, COEF, 128), F32),
-            pltpu.SemaphoreType.DMA,
+            pltpu.SemaphoreType.DMA((DEPTH,)),
         ],
         compiler_params=limits(60),
         name="far",
-    )(first_box.reshape(1), parts, tbox, nbr, wide, m2m, l2l, lattice, dc2e)
+    )(fb, parts, nbr, flat, m2m, l2l, lattice, dc2e)
 
     pot = pl.pallas_call(
         l2p_kernel,

time: 238 us -> 117 us (0.49)
  blocking collectives: 119 us -> 25.1 us
  Pallas kernels: 84 us -> 63 us
  local copies, waits for them, and re-layouts: 16.6 us -> 13.8 us
    unnamed x1 -> x0, blocking collectives: 67.1 us -> none
    all_gather x1 -> x0, blocking collectives: 27.1 us -> none  [per_device(): lax.all_gather(part, 'pts', axis=0, tiled=False)]
    pallas_call x2 -> x1, Pallas kernels: 44.3 us -> 24.9 us  [per_device(): pl.pallas_call(p2m_kernel, out_shape=(jax.ShapeDtypeStruct((OWNERS, 80, 1...]
    unnamed x22 -> x34, local copies, waits for them, and re-layouts: 6.12 us -> 6.8 us
  transfers between devices with their start and end apart: 1 -> 1, of which waited for: 0 -> 0; matrix products, arithmetic and copies ran while one was open for 5% -> 5% of each run, Pallas kernels for 14% -> 0%
where the time goes in v2:
time: 117 us; the launch traced here: 116 us
  Pallas kernels  63 us (54%)
  blocking collectives  25.1 us (21%)
  local copies, waits for them, and re-layouts  13.8 us (12%)
  starting transfers between devices  11.5 us (10%)
  other arithmetic  2.1 us (2%)
    pallas_call x1, Pallas kernels, per_device(): pl.pallas_call(far_kernel, out_shape=(jax.ShapeDtypeStruct((2, COEF, 256)...  28.1 us
    pallas_call x1, Pallas kernels, per_device(): pl.pallas_call(p2m_kernel, out_shape=(jax.ShapeDtypeStruct((OWNERS, 80, 1...  24.9 us
    all_to_all x1, blocking collectives, per_device(): lax.all_to_all(reply, ('pts', 'top'), split_axis=0, concat_axis=0, tiled=...  14.6 us
    all_to_all x1, starting transfers between devices, per_device(): lax.all_to_all(send, ('pts', 'top'), split_axis=0, concat_axis=0, tiled=T...  11.5 us
    all_gather x1, blocking collectives, per_device(): leaves = lax.all_gather(slot_leaf, 'top', axis=0, tiled=True)  10.6 us
    unnamed x34, local copies, waits for them, and re-layouts  6.8 us
    pallas_call x1, Pallas kernels, per_device(): pl.pallas_call(l2p_kernel, out_shape=jax.ShapeDtypeStruct((2, COLS), F32)...  5.82 us
    reshape x1, local copies, waits for them, and re-layouts, per_device(): l2l = l2l.reshape(8, COEF, COEF)  2.69 us
  transfers between devices with their start and end apart: 1, of which 0 were waited for; matrix products, arithmetic and copies ran while one was open for 5% of the time, Pallas kernels for 0%

profile of v2, /device:TPU:1, one launch (start us, length us, event | category | flops | bytes accessed | tf_op | source)
XLA Modules:
  0.0 116.4 jit_solution(8354402559076442336)
XLA Ops:
  0.0 0.8 copy-done.6
  0.8 0.7 copy-done.7
  1.5 0.7 copy-done.8
  2.2 1.9 %pack.1 = (f32[128,6,64]{2,1,0:T(8,128)S(1)}, s32[1,1024]{1,0:T(1,128)S(1)}) custom-call(f32[3,1024]{1,0:T(4,128)S(1)} %copy-done.7, f32[8,1024]{1,0:T(8,128)S(1)} %copy-done.6, s32[1,1024]{1,0:T(1,128)S(1)} %bitcast.12), custom_call_target="tpu_custom_call" | custom-call | tf_op jit(solution)/shard_map/pack/pallas_call | solution.py:512
  4.1 0.9 reshape.331
  5.0 11.5 %all-to-all-start = ((f32[128,1,384]{2,1,0:T(1,128)}), f32[128,1,384]{2,1,0:T(1,128)S(1)}, u32[]{:S(2)}, u32[]{:S(2)}) async-start(f32[128,1,384]{2,1,0:T(1,128)} %reshape.331), calls=%async_computation | async-start | bytes 393216 | tf_op jit(solution)/shard_map/all_to_all | solution.py:525
  16.5 10.6 %all_gather.3 = s32[4096]{0:T(1024)S(1)} all-gather(s32[1024]{0:T(1024)} %param.16), channel_id=1, replica_groups=mesh['pts'=32,'top'=4] {'top'}, dimensions={0}, use_global_device_ids=true | all-gather | bytes 20480 | tf_op jit(solution)/shard_map/all_gather | solution.py:496
  27.1 0.5 slice.16
  28.5 0.2 or_select_fusion
  28.8 0.8 reshape.330.nbr_ref
  29.6 1.6 %reshape.296.m2m_ref = f32[8,152,152]{2,1,0:T(8,128)S(1)} reshape(f32[184832]{0:T(1024)S(1)} %copy-done.9) | data formatting | bytes 1478656 | tf_op jit(solution)/shard_map/reshape | solution.py:493
  31.2 2.7 %reshape.298.l2l_ref = f32[8,152,152]{2,1,0:T(8,128)} reshape(f32[184832]{0:T(1024)S(1)} %copy-done.10) | data formatting | bytes 1478656 | tf_op jit(solution)/shard_map/reshape | solution.py:494
  33.9 0.5 broadcast.473
  34.4 1.1 reduce
  35.9 0.5 copy-done.2
  36.5 24.9 %p2m.1 = (bf16[32,80,128]{2,1,0:T(8,128)(2,1)S(1)}, s32[1,8192]{1,0:T(1,128)S(1)}) custom-call(s32[1]{0:T(128)} %shift_right_arithmetic.192.fb_ref, f32[6,8192]{1,0:T(8,128)S(1)} %reshape.295.recv_ref, f32[64,64]{1,0:T(8,128)S(1)} %bitcast.11, f32[152,8]{1,0:T(8,128)S(1)} %copy-done.2, f32[152,152]{1,0:T(8,128)S(1)} %copy-done.5, ...), custom_call_target="tpu_custom_call" | custom-call | tf_op jit(solution)/shard_map/p2m/pallas_call | solution.py:530
  61.4 0.8 copy-done.1
  62.3 28.1 %far.1 = (bf16[2,152,256]{2,1,0:T(8,128)(2,1)}, bf16[2,152,256]{2,1,0:T(8,128)(2,1)}) custom-call(s32[1]{0:T(128)} %shift_right_arithmetic.192.fb_ref, bf16[32,80,128]{2,1,0:T(8,128)(2,1)} %copy-done.1, s32[40,1,256]{2,1,0:T(1,128)} %reshape.330.nbr_ref, bf16[57038,128]{1,0:T(8,128)(2,1)} %bitcast.13, f32[8,152,152]{2,1,0:T(8,128)} %copy-done, ...), custom_call_target="tpu_custom_call" | custom-call | tf_op jit(solution)/shard_map/far/pallas_call | solution.py:552
  90.4 0.9 copy-done.3
  91.3 0.9 copy-done.4
  92.2 5.8 %l2p.1 = f32[2,8192]{1,0:T(2,128)S(1)} custom-call(f32[6,8192]{1,0:T(8,128)S(1)} %reshape.295.recv_ref, s32[1,8192]{1,0:T(1,128)S(1)} %get-tuple-element.12.code_ref, f32[152,8]{1,0:T(8,128)S(1)} %copy-done.2, bf16[2,152,256]{2,1,0:T(8,128)(2,1)S(1)} %copy-done.3, bf16[2,152,256]{2,1,0:T(8,128)(2,1)S(1)} %copy-done.4), custom_call_target="tpu_custom_call" | custom-call | tf_op jit(solution)/shard_map/l2p/pallas_call | solution.py:572
  98.4 14.6 %all_to_all.10 = f32[128,1,128]{2,1,0:T(1,128)S(1)} all-to-all(f32[128,1,128]{2,1,0:T(1,128)S(1)} %reshape.333), channel_id=1, replica_groups=mesh['pts'=32,'top'=4] {'pts','top'}, dimensions={0} | all-to-all | bytes 131072 | tf_op jit(solution)/shard_map/all_to_all | solution.py:582
  112.9 0.8 reduce.1
  114.0 2.4 %unpack.1 = f32[8,1024]{1,0:T(8,128)} custom-call(f32[8,2048]{1,0:T(8,128)S(1)} %reshape.301.back_ref, s32[1,1024]{1,0:T(1,128)S(1)} %get-tuple-element.16.where_ref), custom_call_target="tpu_custom_call" | custom-call | tf_op jit(solution)/shard_map/unpack/pallas_call | solution.py:584
  (40 shorter events, 1.4 us)
Async XLA Ops:
  0.0 28.5 %copy-start.11 = (s32[80,4]{0,1:T(4,128)S(1)}, s32[80,4]{0,1:T(4,128)}, u32[]{:S(2)}) copy-start(s32[80,4]{0,1:T(4,128)} %constant.40) | copy-start | bytes 3844
  0.0 28.5 %copy-start.12 = (s32[80,4]{0,1:T(4,128)S(1)}, s32[80,4]{0,1:T(4,128)}, u32[]{:S(2)}) copy-start(s32[80,4]{0,1:T(4,128)} %constant.38) | copy-start | bytes 3844
  0.0 28.5 %copy-start.13 = (s32[80,4]{0,1:T(4,128)S(1)}, s32[80,4]{0,1:T(4,128)}, u32[]{:S(2)}) copy-start(s32[80,4]{0,1:T(4,128)} %constant.36) | copy-start | bytes 3844
  0.0 28.5 %copy-start.14 = (pred[80,4]{0,1:T(4,128)(4,1)S(1)}, pred[80,4]{0,1:T(4,128)(4,1)}, u32[]{:S(2)}) copy-start(pred[80,4]{0,1:T(4,128)(4,1)} %constant.11.clone) | copy-start | bytes 964
  0.0 0.8 copy-start.6
  0.8 0.7 copy-start.7
  1.5 0.7 copy-start.8
  2.2 27.3 %copy-start.9 = (f32[184832]{0:T(1024)S(1)}, f32[184832]{0:T(1024)}, u32[]{:S(2)}) copy-start(f32[184832]{0:T(1024)} %param.18) | copy-start | bytes 2217988
  5.0 28.9 %all-to-all-start = ((f32[128,1,384]{2,1,0:T(1,128)}), f32[128,1,384]{2,1,0:T(1,128)S(1)}, u32[]{:S(2)}, u32[]{:S(2)}) async-start(f32[128,1,384]{2,1,0:T(1,128)} %reshape.331), calls=%async_computation | async-start | bytes 393216 | tf_op jit(solution)/shard_map/all_to_all | solution.py:525
  28.5 2.7 %copy-start.10 = (f32[184832]{0:T(1024)S(1)}, f32[184832]{0:T(1024)}, u32[]{:S(2)}) copy-start(f32[184832]{0:T(1024)} %param.22) | copy-start | bytes 2217988
  31.2 4.7 %copy-start = (f32[8,152,152]{2,1,0:T(8,128)}, f32[8,152,152]{2,1,0:T(8,128)S(1)}, u32[]{:S(2)}) copy-start(f32[8,152,152]{2,1,0:T(8,128)S(1)} %reshape.296.m2m_ref) | copy-start | bytes 2217988
  35.5 0.9 copy-start.2
  35.6 0.9 copy-start.5
  61.4 0.9 copy-start.1
  90.3 0.9 copy-start.3
  91.3 0.9 copy-start.4

commit v3 on v2

--- a/solution.py
+++ b/solution.py
@@ -67,22 +67,22 @@
     return np.array(points_list, dtype=np.int32)
 
 
-def morton_decode(number):
-    x = y = z = jnp.zeros_like(number)
-    for bit in range(LEVEL):
-        digit = number >> (3 * bit)
-        x = x | (((digit >> 2) & 1) << bit)
-        y = y | (((digit >> 1) & 1) << bit)
-        z = z | ((digit & 1) << bit)
-    return x, y, z
-
-
-def morton_encode(x, y, z):
-    number = jnp.zeros_like(x)
-    for bit in range(LEVEL):
-        digit = (((x >> bit) & 1) << 2) | (((y >> bit) & 1) << 1) | ((z >> bit) & 1)
-        number = number | (digit << (3 * bit))
-    return number
+def dilate(value):
+    return sum(((value >> bit) & 1) << (3 * bit) for bit in range(LEVEL))
+
+
+def shift_rows():
+    rows = np.zeros((CLASS // 2, 4, 256), np.int32)
+    table = offset_table()
+    lane = np.arange(256)
+    for pair in range(CLASS // 2):
+        offset = CLASS * ((lane >> 5) & 3) + 2 * pair + (lane >> 7)
+        known = offset < OFFSETS
+        steps = table[np.minimum(offset, OFFSETS - 1)] % 8
+        for dim in range(3):
+            rows[pair, dim] = [dilate(int(v)) << (2 - dim) for v in steps[:, dim]]
+        rows[pair, 3] = np.where(known, 0, -1)
+    return jnp.asarray(rows)
 
 
 def split2(x):
@@ -123,10 +123,102 @@
     return jnp.where(mask, 1.0, 0.0).astype(BF16)
 
 
-def pack_kernel(pos_ref, dens_ref, slot_ref, out_ref, where_ref, load_ref):
+def matrices(flat_ref, main_ref, tail_ref):
+    lane = iota((76, 128), 1)
+    for r in range(16):
+        chunk, shift = divmod(COEF * r, 128)
+        count = 3 if shift + COEF > 256 else 2
+        turned = []
+        for c in range(count):
+            value = flat_ref[pl.ds(chunk + c, 76, stride=19), :]
+            turned.append(pltpu.roll(value, 128 - shift, 1) if shift else value)
+        keep = lane < 128 - shift
+        main = jnp.where(keep, turned[0], turned[1])
+        tail = jnp.where(keep, turned[1], turned[2]) if count == 3 else turned[1]
+        main_ref[pl.ds(r, 76, stride=16), :] = main
+        tail_ref[pl.ds(r, 76, stride=16), :] = tail
+
+
+def matrix(main_ref, tail_ref, octant):
+    rows = slice(COEF * octant, COEF * octant + COEF)
+    return jnp.concatenate([main_ref[rows], tail_ref[rows, 0:TAIL]], axis=1)
+
+
+def mix(first, second):
+    left = iota(first.shape, 1) % 128 < CAP
+    even = jnp.where(left, first, pltpu.roll(second, CAP, 1))
+    odd = jnp.where(left, pltpu.roll(first, CAP, 1), second)
+    return even, odd
+
+
+def place_of(index):
+    return {"pts": index // TOP, "top": index % TOP}
+
+
+def greet(barrier, me):
+    def hello(step, carry):
+        pl.semaphore_signal(
+            barrier, inc=1, device_id=place_of((me + step) % DEVS), device_id_type=MESH
+        )
+        return carry
+
+    lax.fori_loop(1, DEVS, hello, 0)
+
+
+def trade(me, source_ref, target_ref, sems):
+    def block(slot, target):
+        return pltpu.make_async_remote_copy(
+            src_ref=source_ref.at[target],
+            dst_ref=target_ref.at[slot],
+            send_sem=sems[0],
+            recv_sem=sems[1],
+            device_id=place_of(target),
+            device_id_type=MESH,
+        )
+
+    def push(step, carry):
+        block(me, (me + step) % DEVS).start()
+        return carry
+
+    lax.fori_loop(1, DEVS, push, 0)
+    target_ref[me] = source_ref[me]
+    return pltpu.make_async_remote_copy(
+        src_ref=source_ref.at[pl.ds(0, DEVS - 1)],
+        dst_ref=target_ref.at[pl.ds(0, DEVS - 1)],
+        send_sem=sems[0],
+        recv_sem=sems[1],
+        device_id=place_of((me + 1) % DEVS),
+        device_id_type=MESH,
+    )
+
+
+def pack_kernel(
+    pos_ref,
+    dens_ref,
+    slot_ref,
+    leaf_ref,
+    m2m_ref,
+    l2l_ref,
+    recv_ref,
+    where_ref,
+    leaves_ref,
+    m2m_main,
+    m2m_tail,
+    l2l_main,
+    l2l_tail,
+    load_ref,
+    send_ref,
+    send_sem,
+    recv_sem,
+    push_sem,
+    pull_sem,
+):
+    top = lax.axis_index("top")
+    me = TOP * lax.axis_index("pts") + top
+    barrier = pltpu.get_barrier_semaphore()
+    greet(barrier, me)
     slot = slot_ref[...]
     owner = slot >> 12
-    code = (slot & (OWN - 1)) + 1
     member = jnp.where(iota((OWNERS, PTS), 0) == owner, 1.0, 0.0)
     before = onehot(iota((PTS, PTS), 0) < iota((PTS, PTS), 1))
     prefix = dot_nn(member.astype(BF16), before)
@@ -134,57 +226,81 @@
     position = owner * CAP + rank.astype(jnp.int32)
     where_ref[...] = position
     load_ref[...] = jnp.zeros_like(load_ref)
-    pos = pos_ref[...]
-    hi = pos.astype(BF16).astype(F32)
-    rest = pos - hi
-    mid = rest.astype(BF16).astype(F32)
-    load_ref[0:3] = hi
-    load_ref[8:11] = mid
-    load_ref[16:19] = rest - mid
-    load_ref[3:4] = (code >> 6).astype(F32)
-    load_ref[4:5] = (code & 63).astype(F32)
-    dens = dens_ref[...]
-    hi = dens.astype(BF16).astype(F32)
-    rest = dens - hi
-    mid = rest.astype(BF16).astype(F32)
-    load_ref[24:32] = hi
-    load_ref[32:40] = mid
-    load_ref[40:48] = rest - mid
-    payload = load_ref[...].astype(BF16)
+    load_ref[0:1] = pos_ref[0:1]
+    load_ref[1:2] = pos_ref[2:3]
+    load_ref[8:9] = pos_ref[1:2]
+    load_ref[9:10] = ((slot & (OWN - 1)) + 1).astype(F32)
+    for pair in range(4):
+        load_ref[2 + pair : 3 + pair] = dens_ref[2 * pair : 2 * pair + 1]
+        load_ref[10 + pair : 11 + pair] = dens_ref[2 * pair + 1 : 2 * pair + 2]
+    payload = jnp.concatenate(split3(load_ref[...]), axis=0)
     for block in range(8):
         pick = onehot(iota((256, PTS), 0) + 256 * block == position)
         res = dot_nt(payload, pick)
-        head = res[0:8] + res[8:16] + res[16:24]
-        slots = head[3:4] * 64.0 + head[4:5]
-        dens_out = res[24:32] + res[32:40] + res[40:48]
-        for part in range(4):
-            own = 4 * block + part
-            lanes = slice(CAP * part, CAP * part + CAP)
-            for top in range(TOP):
-                out_ref[TOP * own + top, 0:3, :] = head[0:3, lanes]
-                out_ref[TOP * own + top, 3:4, :] = slots[:, lanes]
-                out_ref[TOP * own + top, 4:6, :] = dens_out[2 * top : 2 * top + 2, lanes]
-
-
-def green(recv_ref, surf_ref, cols):
+        value = res[0:16] + res[16:32] + res[32:48]
+        for pair in range(2):
+            lanes = slice(128 * pair, 128 * pair + 128)
+            tiles = mix(value[0:8, lanes], value[8:16, lanes])
+            for part, tile in enumerate(tiles):
+                own = 4 * block + 2 * pair + part
+                for column in range(TOP):
+                    send_ref[TOP * own + column, 0:2, :] = tile[0:2]
+                    send_ref[TOP * own + column, 2:3, :] = tile[2 + column : 3 + column]
+    pl.semaphore_wait(barrier, DEVS - 1)
+    waits = trade(me, send_ref, recv_ref, (send_sem, recv_sem))
+
+    def share(step, slot):
+        return pltpu.make_async_remote_copy(
+            src_ref=leaf_ref,
+            dst_ref=leaves_ref.at[slot],
+            send_sem=push_sem.at[step],
+            recv_sem=pull_sem.at[step],
+            device_id={"top": (top + step) % TOP},
+            device_id_type=MESH,
+        )
+
+    for step in range(1, TOP):
+        share(step, top).start()
+    leaves_ref[top] = leaf_ref[...]
+    matrices(m2m_ref, m2m_main, m2m_tail)
+    matrices(l2l_ref, l2l_main, l2l_tail)
+    for step in range(1, TOP):
+        share(step, (top + TOP - step) % TOP).wait_recv()
+        share(step, top).wait_send()
+    waits.wait_recv()
+    waits.wait_send()
+
+
+def row_of(tab_ref, index, start):
+    rows = [tab_ref[index, pl.ds(start + q, 1), :] for q in range(CHUNK // 128)]
+    return jnp.concatenate(rows, axis=1)
+
+
+def green(tab_ref, surf_ref, start):
     squared = None
     for dim in range(3):
-        gap = surf_ref[:, dim : dim + 1] - recv_ref[dim : dim + 1, cols]
+        gap = surf_ref[:, dim : dim + 1] - row_of(tab_ref, dim, start)
         squared = gap * gap if squared is None else squared + gap * gap
-    return lax.rsqrt(squared) * (1.0 / (4.0 * math.pi))
+    return lax.rsqrt(squared)
+
+
+FACTOR = 1.0 / (4.0 * math.pi)
 
 
 def p2m_kernel(
-    fb_ref,
     recv_ref,
-    leaf_ref,
+    leaves_ref,
     surf_ref,
     uc2e_ref,
-    m2m_ref,
+    m2m_main,
+    m2m_tail,
     gath_ref,
     code_ref,
+    tab_ref,
     acc_ref,
+    order_ref,
     pad_ref,
+    tmp_ref,
     send_sem,
     recv_sem,
     pass_sem,
@@ -206,33 +322,52 @@
 
     acc_ref[...] = jnp.zeros_like(acc_ref)
     pad_ref[...] = jnp.zeros_like(pad_ref)
-    table = leaf_ref[...].astype(BF16)
+    for pair in range(3):
+        tmp_ref[...] = recv_ref[:, pair, :]
+        tiles = mix(tmp_ref[pl.ds(0, 64, stride=2), :], tmp_ref[pl.ds(1, 64, stride=2), :])
+        tab_ref[2 * pair] = tiles[0]
+        tab_ref[2 * pair + 1] = tiles[1]
+    first = leaves_ref[0, 0:1, 0:1] >> 3
+    table = (leaves_ref[...].reshape(32, 128) - 8 * first).astype(F32).astype(BF16)
+    eye = onehot(iota((128, 128), 0) == iota((128, 128), 1))
+    table = dot_nt(eye, table).astype(BF16)
 
     def step(index, carry):
         cols = pl.ds(pl.multiple_of(index * CHUNK, CHUNK), CHUNK)
-        slot = recv_ref[3:4, cols].astype(jnp.int32) - 1
-        high = onehot(iota((64, CHUNK), 0) == (slot >> 6))
+        start = index * (CHUNK // 128)
+        slot = row_of(tab_ref, 3, start).astype(jnp.int32) - 1
+        high = onehot(iota((32, CHUNK), 0) == (slot >> 7))
         rows = dot_nn(table, high)
         leaf = jnp.sum(
-            jnp.where(iota((64, CHUNK), 0) == (slot & 63), rows, 0.0), axis=0, keepdims=True
+            jnp.where(iota((128, CHUNK), 0) == (slot & 127), rows, 0.0), axis=0, keepdims=True
         ).astype(jnp.int32)
         code = (leaf & 7) * WIN + (leaf >> 3)
         code_ref[:, cols] = code
         pick = onehot(iota((256, CHUNK), 0) == code)
-        kernel = green(recv_ref, surf_ref, cols)
+        kernel = green(tab_ref, surf_ref, start)
+        weighted = []
         for dens in range(2):
-            hi, lo = split2(kernel * recv_ref[4 + dens : 5 + dens, cols])
-            total = dot_nt(pick, hi) + dot_nt(pick, lo)
-            acc_ref[:, dens] += total.reshape(8, WIN, COEF)
+            value = kernel * (row_of(tab_ref, 4 + dens, start) * FACTOR)
+            high = value.astype(BF16).astype(F32)
+            weighted += [high, value - high]
+        acc_ref[...] += dot_nt(jnp.concatenate(weighted, axis=0).astype(BF16), pick)
         return carry
 
     lax.fori_loop(0, COLS // CHUNK, step, 0)
-    leaf_mult = nt3(acc_ref[...].reshape(2 * 256, COEF), uc2e_ref[...])
-    part = nt3(leaf_mult[0:64], m2m_ref[0])
+    eye = onehot(iota((256, 256), 0) == iota((256, 256), 1))
+    for dens in range(2):
+        base = 2 * COEF * dens
+        total = acc_ref[base : base + COEF] + acc_ref[base + COEF : base + 2 * COEF]
+        hi, mid, rest = split3(total)
+        turned = dot_nt(eye, hi) + dot_nt(eye, mid) + dot_nt(eye, rest)
+        order_ref[:, dens] = turned.reshape(8, WIN, COEF)
+    leaf_mult = nt3(order_ref[...].reshape(2 * 256, COEF), uc2e_ref[...])
+    part = nt3(leaf_mult[0:64], matrix(m2m_main, m2m_tail, 0))
     for octant in range(1, 8):
-        part = part + nt3(leaf_mult[64 * octant : 64 * octant + 64], m2m_ref[octant])
+        part = part + nt3(
+            leaf_mult[64 * octant : 64 * octant + 64], matrix(m2m_main, m2m_tail, octant)
+        )
     pad_ref[:, 0:COEF] = part
-    first = fb_ref[0]
     lane = iota((16, 128), 1)
     tail = jnp.where(
         lane == 96,
@@ -276,12 +411,14 @@
 
 
 def far_kernel(
-    fb_ref,
     parts_ref,
-    nbr_ref,
+    leaves_ref,
+    shift_ref,
     flat_hbm,
-    m2m_ref,
-    l2l_ref,
+    m2m_main,
+    m2m_tail,
+    l2l_main,
+    l2l_tail,
     lattice_ref,
     dc2e_ref,
     hi_ref,
@@ -343,8 +480,17 @@
     src_ref[128 + BROWS : 384 + BROWS] = jnp.zeros((256, 256), BF16)
     wide_ref[PIECES * PIECE : WIDE] = jnp.zeros((WIDE - PIECES * PIECE, 128), F32)
 
+    window = leaves_ref[0, 0:1, 0:1] >> 3
+    spot = (window + (iota((1, 256), 1) & 31)) & (BOXES - 1)
+    masks = (0o444, 0o222, 0o111)
+    based = [spot | (-1 - mask) for mask in masks]
+
     def build(pair, carry):
-        pick = onehot(box == nbr_ref[pair])
+        shifts = shift_ref[pair]
+        nbr = shifts[3:4]
+        for dim in range(3):
+            nbr = nbr | ((based[dim] + shifts[dim : dim + 1]) & masks[dim])
+        pick = onehot(box == nbr)
         found = dot_nn(low, pick)
         top = jnp.concatenate([found[0:COEF, 0:128], found[COEF:, 0:128]], axis=1)
         bottom = jnp.concatenate([found[0:COEF, 128:256], found[COEF:, 128:256]], axis=1)
@@ -380,17 +526,17 @@
         rows = jnp.concatenate(
             [level[0][64 * o : 64 * o + 64], level[1][64 * o : 64 * o + 64]], axis=0
         )
-        term = nt3(rows, m2m_ref[o])
+        term = nt3(rows, matrix(m2m_main, m2m_tail, o))
         up = term if up is None else up + term
     up2 = None
     for o in range(8):
         rows = jnp.concatenate([up[8 * o : 8 * o + 8], up[64 + 8 * o : 72 + 8 * o]], axis=0)
-        term = nt3(rows, m2m_ref[o])
+        term = nt3(rows, matrix(m2m_main, m2m_tail, o))
         up2 = term if up2 is None else up2 + term
     row16 = iota((16, 1), 0)
     up3 = None
     for o in range(8):
-        term = nt3(jnp.where((row16 & 7) == o, up2, 0.0), m2m_ref[o])
+        term = nt3(jnp.where((row16 & 7) == o, up2, 0.0), matrix(m2m_main, m2m_tail, o))
         up3 = term if up3 is None else up3 + term
     root0 = jnp.sum(up3[0:8], axis=0, keepdims=True)
     root1 = jnp.sum(up3[8:16], axis=0, keepdims=True)
@@ -398,18 +544,18 @@
     down = nt3(root, lattice_ref[...])
     down1 = None
     for o in range(8):
-        term = nt3(jnp.where((row16 & 7) == o, down, 0.0), l2l_ref[o])
+        term = nt3(jnp.where((row16 & 7) == o, down, 0.0), matrix(l2l_main, l2l_tail, o))
         down1 = term if down1 is None else down1 + term
-    down2 = jnp.concatenate([nt3(down1, l2l_ref[o]) for o in range(8)], axis=0)
+    down2 = jnp.concatenate([nt3(down1, matrix(l2l_main, l2l_tail, o)) for o in range(8)], axis=0)
     row64 = iota((64, 1), 0)
-    target = (fb_ref[0] + (row64 & 31)) & (BOXES - 1)
+    target = (window + (row64 & 31)) & (BOXES - 1)
     parent = ((target >> 3) & 7) * 16 + (row64 >> 5) * 8 + (target >> 6)
     choose = onehot(iota((64, 128), 1) == parent)
     hi, mid, rest = split3(down2)
     parents = dot_nn(choose, hi) + dot_nn(choose, mid) + dot_nn(choose, rest)
     far = None
     for o in range(8):
-        term = nt3(jnp.where((target & 7) == o, parents, 0.0), l2l_ref[o])
+        term = nt3(jnp.where((target & 7) == o, parents, 0.0), matrix(l2l_main, l2l_tail, o))
         far = term if far is None else far + term
 
     acc_ref[...] = jnp.zeros_like(acc_ref)
@@ -446,7 +592,7 @@
     hi, mid, rest = split3(jnp.concatenate([check_ref[0], check_ref[1]], axis=1))
     checks = dot_nt(fold, hi) + dot_nt(fold, mid) + dot_nt(fold, rest)
     local = nt3(checks, dc2e_ref[...]) + far
-    leaves = [nt3(local, l2l_ref[o]) for o in range(8)]
+    leaves = [nt3(local, matrix(l2l_main, l2l_tail, o)) for o in range(8)]
     for dens in range(2):
         value = jnp.concatenate([leaf[WIN * dens : WIN * dens + WIN] for leaf in leaves], axis=0)
         hi, lo = split2(value)
@@ -454,29 +600,70 @@
         lo_ref[dens] = dot_nt(eye, lo).astype(BF16)
 
 
-def l2p_kernel(recv_ref, code_ref, surf_ref, hi_ref, lo_ref, out_ref):
+def l2p_kernel(
+    tab_ref,
+    code_ref,
+    surf_ref,
+    hi_ref,
+    lo_ref,
+    where_ref,
+    out_ref,
+    pot_ref,
+    tmp_ref,
+    rows_ref,
+    reply_ref,
+    back_ref,
+    send_sem,
+    recv_sem,
+):
+    me = TOP * lax.axis_index("pts") + lax.axis_index("top")
+    barrier = pltpu.get_barrier_semaphore()
+    greet(barrier, me)
+    wide = jnp.concatenate(
+        [hi_ref[0], lo_ref[0], hi_ref[1], lo_ref[1]], axis=0
+    )
+
     def step(index, carry):
         cols = pl.ds(pl.multiple_of(index * CHUNK, CHUNK), CHUNK)
+        start = index * (CHUNK // 128)
         pick = onehot(iota((256, CHUNK), 0) == code_ref[:, cols])
-        kernel = green(recv_ref, surf_ref, cols)
+        kernel = green(tab_ref, surf_ref, start)
+        found = dot_nn(wide, pick)
         for dens in range(2):
-            value = dot_nn(hi_ref[dens], pick) + dot_nn(lo_ref[dens], pick)
-            out_ref[dens : dens + 1, cols] = jnp.sum(kernel * value, axis=0, keepdims=True)
+            base = 2 * COEF * dens
+            value = found[base : base + COEF] + found[base + COEF : base + 2 * COEF]
+            row = jnp.sum(kernel * value, axis=0, keepdims=True) * FACTOR
+            for q in range(CHUNK // 128):
+                pot_ref[dens, pl.ds(start + q, 1), :] = row[:, 128 * q : 128 * q + 128]
         return carry
 
     lax.fori_loop(0, COLS // CHUNK, step, 0)
-
-
-def unpack_kernel(back_ref, where_ref, out_ref):
-    pieces = split3(back_ref[...])
+    even, odd = mix(pot_ref[0], pot_ref[1])
+    tmp_ref[pl.ds(0, 64, stride=2), :] = even
+    tmp_ref[pl.ds(1, 64, stride=2), :] = odd
+    reply_ref[...] = tmp_ref[...].reshape(DEVS, 1, 128)
+    pl.semaphore_wait(barrier, DEVS - 1)
+    waits = trade(me, reply_ref, back_ref, (send_sem, recv_sem))
+    waits.wait_recv()
+    tmp_ref[...] = back_ref[...].reshape(DEVS, 128)
+    for top in range(TOP):
+        tiles = mix(
+            tmp_ref[pl.ds(top, 16, stride=8), :], tmp_ref[pl.ds(TOP + top, 16, stride=8), :]
+        )
+        for dens in range(2):
+            rows_ref[pl.ds(2 * top + dens, 16, stride=8), :] = tiles[dens]
+    value = jnp.concatenate([rows_ref[8 * j : 8 * j + 8] for j in range(16)], axis=1)
+    hi = value.astype(BF16).astype(F32)
+    mid = (value - hi).astype(BF16).astype(F32)
+    pieces = jnp.concatenate([hi, mid, value - hi - mid], axis=0).astype(BF16)
     position = where_ref[...]
-    total = jnp.zeros((8, PTS), F32)
+    total = None
     for block in range(8):
         pick = onehot(iota((256, PTS), 0) + 256 * block == position)
-        cols = slice(256 * block, 256 * block + 256)
-        for piece in pieces:
-            total = total + dot_nn(piece[:, cols], pick)
-    out_ref[...] = total
+        term = dot_nn(pieces[:, 256 * block : 256 * block + 256], pick)
+        total = term if total is None else total + term
+    out_ref[...] = total[0:8] + total[8:16] + total[16:24]
+    waits.wait_send()
 
 
 def whole(count):
@@ -485,69 +672,71 @@
 
 def limits(mib):
     return pltpu.CompilerParams(vmem_limit_bytes=mib * 1024 * 1024)
+
+
+def talking(mib, ident):
+    return pltpu.CompilerParams(
+        vmem_limit_bytes=mib * 1024 * 1024, collective_id=ident, has_side_effects=True
+    )
 
 
 def per_device(
     local_pos, densities, morton_slot, slot_leaf, uc2e, m2m, m2l_ops, dc2e, lattice, l2l
 ):
-    m2m = m2m.reshape(8, COEF, COEF)
-    l2l = l2l.reshape(8, COEF, COEF)
     surf = surface_columns()
-    leaves = lax.all_gather(slot_leaf, "top", axis=0, tiled=True)
-    first_box = leaves[0] >> 3
-    leaf_table = (leaves - 8 * first_box).reshape(64, 64).T.astype(F32)
-    slide = jnp.arange(WIN, dtype=jnp.int32)
-    targets = (first_box + slide) & (BOXES - 1)
-    tx, ty, tz = morton_decode(targets)
-    offsets = np.zeros((4 * CLASS, 3), np.int32)
-    offsets[:OFFSETS] = offset_table()
-    offsets = jnp.asarray(offsets.reshape(4, CLASS, 3).transpose(1, 0, 2))
-    known = jnp.asarray((np.arange(4 * CLASS) < OFFSETS).reshape(4, CLASS).T)
-    nbr = morton_encode(
-        (tx + offsets[:, :, 0:1]) & 7, (ty + offsets[:, :, 1:2]) & 7, (tz + offsets[:, :, 2:3]) & 7
-    )
-    nbr = jnp.where(known[:, :, None], nbr, -1).reshape(CLASS // 2, 1, 256)
-
     flat = m2l_ops.reshape(GROUPS * CHUNKS, 128)
-    send, position = pl.pallas_call(
+    smalls = (1216, 128)
+    recv, position, leaves, mm, mt, lm, lt = pl.pallas_call(
         pack_kernel,
         out_shape=(
-            jax.ShapeDtypeStruct((DEVS, 6, CAP), F32),
+            jax.ShapeDtypeStruct((DEVS, 3, 128), F32),
             jax.ShapeDtypeStruct((1, PTS), jnp.int32),
-        ),
-        in_specs=whole(3),
-        out_specs=tuple(whole(2)),
-        scratch_shapes=[pltpu.VMEM((48, PTS), F32)],
-        compiler_params=limits(32),
+            jax.ShapeDtypeStruct((TOP, 8, 128), jnp.int32),
+        )
+        + (jax.ShapeDtypeStruct(smalls, F32),) * 4,
+        in_specs=whole(6),
+        out_specs=tuple(whole(7)),
+        scratch_shapes=[
+            pltpu.VMEM((16, PTS), F32),
+            pltpu.VMEM((DEVS, 3, 128), F32),
+            pltpu.SemaphoreType.DMA,
+            pltpu.SemaphoreType.DMA,
+            pltpu.SemaphoreType.DMA((TOP,)),
+            pltpu.SemaphoreType.DMA((TOP,)),
+        ],
+        compiler_params=talking(32, 0),
         name="pack",
-    )(local_pos, densities, morton_slot.reshape(1, PTS))
-
-    recv = lax.all_to_all(send, ("pts", "top"), split_axis=0, concat_axis=0, tiled=True)
-    recv = recv.transpose(1, 0, 2).reshape(6, COLS)
-
-    fb = first_box.reshape(1)
-    smem = [pl.BlockSpec(memory_space=pltpu.MemorySpace.SMEM)]
-    parts, code = pl.pallas_call(
+    )(
+        local_pos,
+        densities,
+        morton_slot.reshape(1, PTS),
+        slot_leaf.reshape(8, 128),
+        m2m.reshape(1444, 128),
+        l2l.reshape(1444, 128),
+    )
+
+    parts, code, tab = pl.pallas_call(
         p2m_kernel,
         out_shape=(
             jax.ShapeDtypeStruct((OWNERS, 80, 128), BF16),
             jax.ShapeDtypeStruct((1, COLS), jnp.int32),
+            jax.ShapeDtypeStruct((6, 64, 128), F32),
         ),
-        in_specs=smem + whole(5),
-        out_specs=tuple(whole(2)),
+        in_specs=whole(6),
+        out_specs=tuple(whole(3)),
         scratch_shapes=[
+            pltpu.VMEM((4 * COEF, 256), F32),
             pltpu.VMEM((8, 2, WIN, COEF), F32),
             pltpu.VMEM((2 * WIN, 256), F32),
+            pltpu.VMEM((128, 128), F32),
             pltpu.SemaphoreType.DMA((16,)),
             pltpu.SemaphoreType.DMA((16,)),
             pltpu.SemaphoreType.DMA((16,)),
             pltpu.SemaphoreType.DMA((16,)),
         ],
-        compiler_params=pltpu.CompilerParams(
-            vmem_limit_bytes=32 * 1024 * 1024, collective_id=0, has_side_effects=True
-        ),
+        compiler_params=talking(32, 1),
         name="p2m",
-    )(fb, recv, leaf_table, surf, uc2e, m2m)
+    )(recv, leaves, surf, uc2e, mm, mt)
 
     hi, lo = pl.pallas_call(
         far_kernel,
@@ -555,7 +744,7 @@
             jax.ShapeDtypeStruct((2, COEF, 256), BF16),
             jax.ShapeDtypeStruct((2, COEF, 256), BF16),
         ),
-        in_specs=smem + whole(2) + [pl.BlockSpec(memory_space=pl.ANY)] + whole(4),
+        in_specs=whole(3) + [pl.BlockSpec(memory_space=pl.ANY)] + whole(6),
         out_specs=tuple(whole(2)),
         scratch_shapes=[
             pltpu.VMEM((DEPTH, PIECE, 128), BF16),
@@ -567,28 +756,25 @@
         ],
         compiler_params=limits(60),
         name="far",
-    )(fb, parts, nbr, flat, m2m, l2l, lattice, dc2e)
-
-    pot = pl.pallas_call(
+    )(parts, leaves, shift_rows(), flat, mm, mt, lm, lt, lattice, dc2e)
+
+    return pl.pallas_call(
         l2p_kernel,
-        out_shape=jax.ShapeDtypeStruct((2, COLS), F32),
-        in_specs=whole(5),
+        out_shape=jax.ShapeDtypeStruct((8, PTS), F32),
+        in_specs=whole(6),
         out_specs=whole(1)[0],
-        compiler_params=limits(32),
+        scratch_shapes=[
+            pltpu.VMEM((2, 64, 128), F32),
+            pltpu.VMEM((128, 128), F32),
+            pltpu.VMEM((128, 128), F32),
+            pltpu.VMEM((DEVS, 1, 128), F32),
+            pltpu.VMEM((DEVS, 1, 128), F32),
+            pltpu.SemaphoreType.DMA,
+            pltpu.SemaphoreType.DMA,
+        ],
+        compiler_params=talking(32, 2),
         name="l2p",
-    )(recv, code, surf, hi, lo)
-
-    reply = pot.reshape(2, DEVS, CAP).transpose(1, 0, 2)
-    back = lax.all_to_all(reply, ("pts", "top"), split_axis=0, concat_axis=0, tiled=True)
-    back = back.reshape(OWNERS, TOP, 2, CAP).transpose(1, 2, 0, 3).reshape(8, OWNERS * CAP)
-    return pl.pallas_call(
-        unpack_kernel,
-        out_shape=jax.ShapeDtypeStruct((8, PTS), F32),
-        in_specs=whole(2),
-        out_specs=whole(1)[0],
-        compiler_params=limits(32),
-        name="unpack",
-    )(back, position)
+    )(tab, code, surf, hi, lo, position)
 
 
 def solution(mesh):

time: 117 us -> 96.8 us (0.83)
  blocking collectives: 25.1 us -> 0 us
  Pallas kernels: 63 us -> 84.3 us
  starting transfers between devices: 11.5 us -> 0 us
  other arithmetic: 2.1 us -> 0 us
  local copies, waits for them, and re-layouts: 13.8 us -> 11.9 us
    pallas_call x3 -> x2, Pallas kernels: 10.1 us -> 34.1 us  [the longest x1 17.9 us: per_device(): pl.pallas_call(pack_kernel, out_shape=(jax.ShapeDtypeStruct((DEVS, 3, 128...]
    all_to_all x1 -> x0, blocking collectives: 14.6 us -> none  [per_device(): lax.all_to_all(reply, ('pts', 'top'), split_axis=0, concat_axis=0, tiled=...]
    all_to_all x1 -> x0, starting transfers between devices: 11.5 us -> none  [per_device(): lax.all_to_all(send, ('pts', 'top'), split_axis=0, concat_axis=0, tiled=T...]
    all_gather x1 -> x0, blocking collectives: 10.6 us -> none  [per_device(): leaves = lax.all_gather(slot_leaf, 'top', axis=0, tiled=True)]
    unnamed x34 -> x35, local copies, waits for them, and re-layouts: 6.8 us -> 11.9 us
    reshape x5 -> x0, local copies, waits for them, and re-layouts: 4.7 us -> none  [the longest x1 2.69 us: per_device(): l2l = l2l.reshape(8, COEF, COEF)]
    pallas_call x1, Pallas kernels: 24.9 us -> 21.6 us  [per_device(): pl.pallas_call(p2m_kernel, out_shape=(jax.ShapeDtypeStruct((OWNERS, 80, 1...]
    all_to_all x2 -> x0, other arithmetic: 1.92 us -> none  [the longest x1 1.12 us: per_device(): lax.all_to_all(send, ('pts', 'top'), split_axis=0, concat_axis=0, tiled=T...]
  transfers between devices with their start and end apart: 1 -> 0, of which waited for: 0 -> 0; matrix products, arithmetic and copies ran while one was open for 5% -> 0% of each run, Pallas kernels for 0% -> 0%
where the time goes in v3:
time: 96.8 us; the launch traced here: 96.3 us
  Pallas kernels  84.3 us (87%)
  local copies, waits for them, and re-layouts  11.9 us (12%)
    pallas_call x1, Pallas kernels, per_device(): pl.pallas_call(far_kernel, out_shape=(jax.ShapeDtypeStruct((2, COEF, 256)...  28.7 us
    pallas_call x1, Pallas kernels, per_device(): pl.pallas_call(p2m_kernel, out_shape=(jax.ShapeDtypeStruct((OWNERS, 80, 1...  21.6 us
    pallas_call x1, Pallas kernels, per_device(): pl.pallas_call(pack_kernel, out_shape=(jax.ShapeDtypeStruct((DEVS, 3, 128...  17.9 us
    pallas_call x1, Pallas kernels, per_device(): pl.pallas_call(l2p_kernel, out_shape=jax.ShapeDtypeStruct((8, PTS), F32),...  16.2 us
    unnamed x35, local copies, waits for them, and re-layouts  11.9 us

profile of v3, /device:TPU:1, one launch (start us, length us, event | category | flops | bytes accessed | tf_op | source)
XLA Modules:
  0.0 96.3 jit_solution(5189696092066425924)
XLA Ops:
  0.0 1.1 %copy-done.2 = f32[184832]{0:T(1024)S(1)} copy-done((f32[184832]{0:T(1024)S(1)}, f32[184832]{0:T(1024)}, u32[]{:S(2)}) %copy-start.2) | copy-done | bytes 739352
  1.1 1.1 %copy-done.3 = f32[184832]{0:T(1024)S(1)} copy-done((f32[184832]{0:T(1024)S(1)}, f32[184832]{0:T(1024)}, u32[]{:S(2)}) %copy-start.3) | copy-done | bytes 739352
  2.2 0.8 copy-done.13
  3.0 0.7 copy-done.14
  3.7 0.7 copy-done.15
  4.4 0.7 copy-done.16
  5.1 17.9 %pack.1 = (f32[128,3,128]{2,1,0:T(4,128)S(1)}, s32[1,1024]{1,0:T(1,128)S(1)}, s32[4,8,128]{2,1,0:T(8,128)S(1)}, f32[1216,128]{1,0:T(8,128)S(1)}, f32[1216,128]{1...) custom-call(f32[3,1024]{1,0:T(4,128)S(1)} %copy-done.14, f32[8,1024]{1,0:T(8,128)S(1)} %copy-done.13, ...), custom_call_target="tpu_custom_call" | custom-call | tf_op jit(solution)/shard_map/pack/pallas_call | solution.py:689
  23.0 0.0 copy-start.5
  23.0 0.8 copy-done.5
  23.8 0.8 copy-done.6
  24.7 1.0 copy-done.7
  25.6 0.9 copy-done.11
  26.5 21.6 %p2m.1 = (bf16[32,80,128]{2,1,0:T(8,128)(2,1)S(1)}, s32[1,8192]{1,0:T(1,128)S(1)}, f32[6,64,128]{2,1,0:T(8,128)S(1)}) custom-call(f32[128,3,128]{2,1,0:T(4,128)S(1)} %get-tuple-element.17.recv_ref, s32[4,8,128]{2,1,0:T(8,128)S(1)} %get-tuple-element.18.leaves_ref, f32[152,8]{1,0:T(8,128)S(1)} %copy-done.7, f32[152,152]{1,0:T(8,128)S(1)} %copy-done.11, ...), custom_call_target="tpu_custom_call" | custom-call | tf_op jit(solution)/shard_map/p2m/pallas_call | solution.py:718
  48.1 0.0 copy-start.4
  48.1 0.8 copy-done.4
  49.0 0.0 copy-done
  49.0 0.0 copy-done.1
  49.0 0.0 copy-done.12
  49.0 28.7 %far.1 = (bf16[2,152,256]{2,1,0:T(8,128)(2,1)}, bf16[2,152,256]{2,1,0:T(8,128)(2,1)}) custom-call(bf16[32,80,128]{2,1,0:T(8,128)(2,1)} %copy-done.4, s32[4,8,128]{2,1,0:T(8,128)} %copy-done.12, s32[40,4,256]{2,1,0:T(4,128)} %constant.5.clone.shift_ref, bf16[57038,128]{1,0:T(8,128)(2,1)} %bitcast.9, f32[1216,128]{1,0:T(8,128)} %copy-done, ...), custom_call_target="tpu_custom_call" | custom-call | tf_op jit(solution)/shard_map/far/pallas_call | solution.py:741
  77.7 0.0 copy-done.8
  77.7 0.9 copy-done.9
  78.6 0.9 copy-done.10
  79.5 16.2 %l2p.1 = f32[8,1024]{1,0:T(8,128)S(1)} custom-call(f32[6,64,128]{2,1,0:T(8,128)S(1)} %get-tuple-element.21.tab_ref, s32[1,8192]{1,0:T(1,128)S(1)} %get-tuple-element.22.code_ref, f32[152,8]{1,0:T(8,128)S(1)} %copy-done.8, bf16[2,152,256]{2,1,0:T(8,128)(2,1)S(1)} %copy-done.9, bf16[2,152,256]{2,1,0:T(8,128)(2,1)S(1)} %copy-done.10, ...), custom_call_target="tpu_custom_call" | custom-call | tf_op jit(solution)/shard_map/l2p/pallas_call | solution.py:761
  95.7 0.6 copy.14
  (15 shorter events, 0.0 us)
Async XLA Ops:
  0.0 1.1 %copy-start.2 = (f32[184832]{0:T(1024)S(1)}, f32[184832]{0:T(1024)}, u32[]{:S(2)}) copy-start(f32[184832]{0:T(1024)} %param.17) | copy-start | bytes 2217988
  1.1 1.1 %copy-start.3 = (f32[184832]{0:T(1024)S(1)}, f32[184832]{0:T(1024)}, u32[]{:S(2)}) copy-start(f32[184832]{0:T(1024)} %param.21) | copy-start | bytes 2217988
  2.2 0.8 copy-start.13
  3.0 0.7 copy-start.14
  3.7 0.7 copy-start.15
  4.4 0.7 copy-start.16
  5.1 72.6 %copy-start.8 = (f32[152,8]{1,0:T(8,128)S(1)}, f32[152,8]{1,0:T(8,128)}, u32[]{:S(2)}) copy-start(f32[152,8]{1,0:T(8,128)} %constant.4.clone.surf_ref) | copy-start | bytes 14596
  23.0 0.8 copy-start.5
  23.8 0.8 copy-start.6
  24.6 24.3 %copy-start = (f32[1216,128]{1,0:T(8,128)}, f32[1216,128]{1,0:T(8,128)S(1)}, u32[]{:S(2)}) copy-start(f32[1216,128]{1,0:T(8,128)S(1)} %get-tuple-element.19.m2m_main) | copy-start | bytes 1867780
  24.6 24.3 %copy-start.1 = (f32[1216,128]{1,0:T(8,128)}, f32[1216,128]{1,0:T(8,128)S(1)}, u32[]{:S(2)}) copy-start(f32[1216,128]{1,0:T(8,128)S(1)} %get-tuple-element.20.m2m_tail) | copy-start | bytes 1867780
  24.7 24.3 %copy-start.12 = (s32[4,8,128]{2,1,0:T(8,128)}, s32[4,8,128]{2,1,0:T(8,128)S(1)}, u32[]{:S(2)}) copy-start(s32[4,8,128]{2,1,0:T(8,128)S(1)} %get-tuple-element.18.leaves_ref) | copy-start | bytes 49156
  24.7 1.0 copy-start.7
  25.6 0.9 copy-start.11
  48.1 0.9 copy-start.4
  77.7 0.9 copy-start.9
  78.6 0.9 copy-start.10

commit v4 on v3

v4 whole, which is shorter than its diff:
```python
import functools
import math

import jax
import jax.numpy as jnp
import numpy as np
from jax import lax
from jax.experimental import pallas as pl
from jax.experimental.pallas import tpu as pltpu
from jax.sharding import PartitionSpec as P

LEVEL = 3
EDGE = 6
COEF = 152
OFFSETS = 316
PTS = 1024
OWN = 4096
CAP = 64
OWNERS = 32
TOP = 4
DEVS = 128
COLS = DEVS * CAP
BOXES = 512
WIN = 32
GROUPS = 38
CHUNKS = 1501
GPAD = 40
WIDE = 60048
PIECE = 1440
PIECES = 40
DEPTH = 8
TAIL = COEF - 128
CLASS = 80
BROWS = CLASS * COEF
CHUNK = 1024

F32 = jnp.float32
BF16 = jnp.bfloat16
VM = pltpu.MemorySpace.VMEM
MESH = pl.DeviceIdType.MESH


def surface_table():
    grid_vals = np.linspace(-1.0, 1.0, EDGE)
    points_list = []
    for a in range(EDGE):
        for b in range(EDGE):
            for c in range(EDGE):
                if min(a, b, c) == 0 or max(a, b, c) == EDGE - 1:
                    points_list.append([grid_vals[a], grid_vals[b], grid_vals[c]])
    return np.array(points_list, dtype=np.float32).T


def surface_columns():
    table = np.zeros((COEF, 8), np.float32)
    table[:, :3] = (np.float32(1.25) * surface_table()).T
    return jnp.asarray(table)


def offset_table():
    points_list = []
    for dx in range(-3, 4):
        for dy in range(-3, 4):
            for dz in range(-3, 4):
                if max(abs(dx), abs(dy), abs(dz)) >= 2:
                    points_list.append([dx, dy, dz])
    return np.array(points_list, dtype=np.int32)


def dilate(value):
    return sum(((value >> bit) & 1) << (3 * bit) for bit in range(LEVEL))


def shift_rows():
    rows = np.zeros((CLASS // 2, 4, 256), np.int32)
    table = offset_table()
    lane = np.arange(256)
    for pair in range(CLASS // 2):
        offset = CLASS * ((lane >> 5) & 3) + 2 * pair + (lane >> 7)
        known = offset < OFFSETS
        steps = table[np.minimum(offset, OFFSETS - 1)] % 8
        for dim in range(3):
            rows[pair, dim] = [dilate(int(v)) << (2 - dim) for v in steps[:, dim]]
        rows[pair, 3] = np.where(known, 0, -1)
    return jnp.asarray(rows)


def split2(x):
    hi = x.astype(BF16)
    lo = (x - hi.astype(F32)).astype(BF16)
    return hi, lo


def split3(x):
    hi = x.astype(BF16)
    rest = x - hi.astype(F32)
    mid = rest.astype(BF16)
    lo = (rest - mid.astype(F32)).astype(BF16)
    return hi, mid, lo


def dot_nn(a, b):
    return lax.dot_general(a, b, (((1,), (0,)), ((), ())), preferred_element_type=F32)


def dot_nt(a, b):
    return lax.dot_general(a, b, (((1,), (1,)), ((), ())), preferred_element_type=F32)


def nt3(x, w):
    rows = x.shape[0]
    xh, xl = split2(x)
    both = dot_nt(jnp.concatenate([xh, xl], axis=0), w[0])
    return both[:rows] + both[rows:] + dot_nt(xh, w[1])


def iota(shape, dim):
    return lax.broadcasted_iota(jnp.int32, shape, dim)


def onehot(mask):
    return jnp.where(mask, 1.0, 0.0).astype(BF16)


def matrices(flat_ref, main_ref, tail_ref):
    lane = iota((76, 128), 1)
    for r in range(16):
        chunk, shift = divmod(COEF * r, 128)
        count = 3 if shift + COEF > 256 else 2
        turned = []
        for c in range(count):
            value = flat_ref[pl.ds(chunk + c, 76, stride=19), :]
            turned.append(pltpu.roll(value, 128 - shift, 1) if shift else value)
        keep = lane < 128 - shift
        main = jnp.where(keep, turned[0], turned[1])
        tail = jnp.where(keep, turned[1], turned[2]) if count == 3 else turned[1]
        main_ref[pl.ds(r, 76, stride=16), :] = main
        tail_ref[pl.ds(r, 76, stride=16), :] = tail


def matrix(main_ref, tail_ref, octant):
    rows = slice(COEF * octant, COEF * octant + COEF)
    return jnp.concatenate([main_ref[rows], tail_ref[rows, 0:TAIL]], axis=1)


def mix(first, second):
    left = iota(first.shape, 1) % 128 < CAP
    even = jnp.where(left, first, pltpu.roll(second, CAP, 1))
    odd = jnp.where(left, pltpu.roll(first, CAP, 1), second)
    return even, odd


def place_of(index):
    return {"pts": index // TOP, "top": index % TOP}


def greet(barrier, me):
    def hello(step, carry):
        pl.semaphore_signal(
            barrier, inc=1, device_id=place_of((me + step) % DEVS), device_id_type=MESH
        )
        return carry

    lax.fori_loop(1, DEVS, hello, 0)


def trade(me, source_ref, target_ref, sems):
    def block(slot, target):
        return pltpu.make_async_remote_copy(
            src_ref=source_ref.at[target],
            dst_ref=target_ref.at[slot],
            send_sem=sems[0],
            recv_sem=sems[1],
            device_id=place_of(target),
            device_id_type=MESH,
        )

    def push(step, carry):
        block(me, (me + step) % DEVS).start()
        return carry

    lax.fori_loop(1, DEVS, push, 0)
    target_ref[me] = source_ref[me]
    return pltpu.make_async_remote_copy(
        src_ref=source_ref.at[pl.ds(0, DEVS - 1)],
        dst_ref=target_ref.at[pl.ds(0, DEVS - 1)],
        send_sem=sems[0],
        recv_sem=sems[1],
        device_id=place_of((me + 1) % DEVS),
        device_id_type=MESH,
    )


def row_of(tab_ref, index, start):
    rows = [tab_ref[index, pl.ds(start + q, 1), :] for q in range(CHUNK // 128)]
    return jnp.concatenate(rows, axis=1)


def green(tab_ref, surf_ref, start):
    squared = None
    for dim in range(3):
        gap = surf_ref[:, dim : dim + 1] - row_of(tab_ref, dim, start)
        squared = gap * gap if squared is None else squared + gap * gap
    return lax.rsqrt(squared)


FACTOR = 1.0 / (4.0 * math.pi)


def fmm_kernel(
    pos_hbm,
    dens_hbm,
    slot_hbm,
    leaf_hbm,
    m2m_hbm,
    l2l_hbm,
    uc2e_hbm,
    dc2e_hbm,
    lattice_hbm,
    surf_hbm,
    shift_hbm,
    flat_hbm,
    out_ref,
    pos_ref,
    dens_ref,
    slot_ref,
    leaf_ref,
    m2m_ref,
    l2l_ref,
    uc2e_ref,
    dc2e_ref,
    lattice_ref,
    surf_ref,
    shift_ref,
    in_sem,
    load_ref,
    send_ref,
    recv_ref,
    leaves_ref,
    main_ref,
    tail_ref,
    up_ref,
    down_ref,
    single_ref,
    stage_ref,
    wide_ref,
    stage_sem,
    tab_ref,
    code_ref,
    green_ref,
    sums_ref,
    order_ref,
    pad_ref,
    tmp_ref,
    gath_ref,
    roots_ref,
    src_ref,
    acc_ref,
    check_ref,
    leaf_mat_ref,
    pot_ref,
    rows_ref,
    reply_ref,
    back_ref,
    points_sems,
    push_sem,
    pull_sem,
    send_sem,
    recv_sem,
    pass_sem,
    take_sem,
    root_sems,
    reply_sems,
):
    own = lax.axis_index("pts")
    top = lax.axis_index("top")
    me = TOP * own + top
    x, y, core = own // 8, (own // 2) % 4, own % 2
    partner = own + 1 - 2 * core

    def other(step, sign, side):
        return ((x + sign * (step // 4) + 4) % 4) * 8 + ((y + sign * (step % 4) + 4) % 4) * 2 + side

    moves = [
        (pos_hbm, pos_ref),
        (dens_hbm, dens_ref),
        (slot_hbm, slot_ref),
        (leaf_hbm, leaf_ref),
        (m2m_hbm, m2m_ref),
        (l2l_hbm, l2l_ref),
        (uc2e_hbm, uc2e_ref),
        (dc2e_hbm, dc2e_ref),
        (lattice_hbm, lattice_ref),
        (surf_hbm, surf_ref),
        (shift_hbm, shift_ref),
    ]
    loads = [
        pltpu.make_async_copy(source, target, in_sem.at[index])
        for index, (source, target) in enumerate(moves)
    ]
    for load in loads:
        load.start()

    def fetch(index, size):
        return pltpu.make_async_copy(
            flat_hbm.at[pl.ds(index * PIECE, size)],
            stage_ref.at[index % DEPTH, pl.ds(0, size)],
            stage_sem.at[index % DEPTH],
        )

    last = GROUPS * CHUNKS - (PIECES - 1) * PIECE
    for index in range(DEPTH):
        fetch(index, PIECE).start()
    barrier = pltpu.get_barrier_semaphore()
    greet(barrier, me)

    for load in loads[:4]:
        load.wait()
    slot = slot_ref[...]
    owner = slot >> 12
    member = jnp.where(iota((OWNERS, PTS), 0) == owner, 1.0, 0.0)
    before = onehot(iota((PTS, PTS), 0) < iota((PTS, PTS), 1))
    prefix = dot_nn(member.astype(BF16), before)
    rank = jnp.sum(member * prefix, axis=0, keepdims=True)
    position = owner * CAP + rank.astype(jnp.int32)
    load_ref[...] = jnp.zeros_like(load_ref)
    load_ref[0:1] = pos_ref[0:1]
    load_ref[1:2] = pos_ref[2:3]
    load_ref[8:9] = pos_ref[1:2]
    load_ref[9:10] = ((slot & (OWN - 1)) + 1).astype(F32)
    for pair in range(4):
        load_ref[2 + pair : 3 + pair] = dens_ref[2 * pair : 2 * pair + 1]
        load_ref[10 + pair : 11 + pair] = dens_ref[2 * pair + 1 : 2 * pair + 2]
    payload = jnp.concatenate(split3(load_ref[...]), axis=0)
    for block in range(8):
        pick = onehot(iota((256, PTS), 0) + 256 * block == position)
        res = dot_nt(payload, pick)
        value = res[0:16] + res[16:32] + res[32:48]
        for pair in range(2):
            lanes = slice(128 * pair, 128 * pair + 128)
            tiles = mix(value[0:8, lanes], value[8:16, lanes])
            for part, tile in enumerate(tiles):
                target = 4 * block + 2 * pair + part
                for column in range(TOP):
                    send_ref[TOP * target + column, 0:2, :] = tile[0:2]
                    send_ref[TOP * target + column, 2:3, :] = tile[2 + column : 3 + column]
    pl.semaphore_wait(barrier, DEVS - 1)
    points = trade(me, send_ref, recv_ref, (points_sems.at[0], points_sems.at[1]))

    def share(step, place):
        return pltpu.make_async_remote_copy(
            src_ref=leaf_ref,
            dst_ref=leaves_ref.at[place],
            send_sem=push_sem.at[step],
            recv_sem=pull_sem.at[step],
            device_id={"top": (top + step) % TOP},
            device_id_type=MESH,
        )

    for step in range(1, TOP):
        share(step, top).start()
    leaves_ref[top] = leaf_ref[...]

    for load in loads[4:]:
        load.wait()
    for flat_ref, split_ref in ((m2m_ref, up_ref), (l2l_ref, down_ref)):
        matrices(flat_ref, main_ref, tail_ref)
        for octant in range(8):
            hi, lo = split2(matrix(main_ref, tail_ref, octant))
            split_ref[octant, 0] = hi
            split_ref[octant, 1] = lo
    for index, ref in enumerate((uc2e_ref, dc2e_ref, lattice_ref)):
        hi, lo = split2(ref[...])
        single_ref[index, 0] = hi
        single_ref[index, 1] = lo
    wide_ref[PIECES * PIECE : WIDE] = jnp.zeros((WIDE - PIECES * PIECE, 128), F32)
    src_ref[0:128] = jnp.zeros((128, 256), BF16)
    src_ref[128 + BROWS : 384 + BROWS] = jnp.zeros((256, 256), BF16)

    def widen(index, carry):
        @pl.when(index < PIECES - 1)
        def _():
            fetch(index, PIECE).wait()

        @pl.when(index == PIECES - 1)
        def _():
            fetch(index, last).wait()

        wide_ref[pl.ds(pl.multiple_of(index * PIECE, 32), PIECE)] = stage_ref[
            index % DEPTH
        ].astype(F32)

        @pl.when(index + DEPTH < PIECES - 1)
        def _():
            fetch(index + DEPTH, PIECE).start()

        @pl.when(index + DEPTH == PIECES - 1)
        def _():
            fetch(index + DEPTH, last).start()

        return carry

    lax.fori_loop(0, PIECES, widen, 0)
    sums_ref[...] = jnp.zeros_like(sums_ref)
    pad_ref[...] = jnp.zeros_like(pad_ref)

    for step in range(1, TOP):
        share(step, (top + TOP - step) % TOP).wait_recv()
        share(step, top).wait_send()
    points.wait_recv()

    for pair in range(3):
        tmp_ref[...] = recv_ref[:, pair, :]
        tiles = mix(tmp_ref[pl.ds(0, 64, stride=2), :], tmp_ref[pl.ds(1, 64, stride=2), :])
        tab_ref[2 * pair] = tiles[0]
        tab_ref[2 * pair + 1] = tiles[1]
    window = leaves_ref[0, 0:1, 0:1] >> 3
    table = (leaves_ref[...].reshape(32, 128) - 8 * window).astype(F32).astype(BF16)
    eye = onehot(iota((128, 128), 0) == iota((128, 128), 1))
    table = dot_nt(eye, table).astype(BF16)

    def gather(index, carry):
        cols = pl.ds(pl.multiple_of(index * CHUNK, CHUNK), CHUNK)
        start = index * (CHUNK // 128)
        place = row_of(tab_ref, 3, start).astype(jnp.int32) - 1
        high = onehot(iota((32, CHUNK), 0) == (place >> 7))
        rows = dot_nn(table, high)
        leaf = jnp.sum(
            jnp.where(iota((128, CHUNK), 0) == (place & 127), rows, 0.0), axis=0, keepdims=True
        ).astype(jnp.int32)
        code = (leaf & 7) * WIN + (leaf >> 3)
        code_ref[:, cols] = code
        pick = onehot(iota((256, CHUNK), 0) == code)
        kernel = green(tab_ref, surf_ref, start)
        green_ref[:, cols] = kernel
        weighted = []
        for dens in range(2):
            value = kernel * (row_of(tab_ref, 4 + dens, start) * FACTOR)
            high = value.astype(BF16).astype(F32)
            weighted += [high, value - high]
        sums_ref[...] += dot_nt(jnp.concatenate(weighted, axis=0).astype(BF16), pick)
        return carry

    lax.fori_loop(0, COLS // CHUNK, gather, 0)
    eye = onehot(iota((256, 256), 0) == iota((256, 256), 1))
    for dens in range(2):
        base = 2 * COEF * dens
        total = sums_ref[base : base + COEF] + sums_ref[base + COEF : base + 2 * COEF]
        hi, mid, rest = split3(total)
        turned = dot_nt(eye, hi) + dot_nt(eye, mid) + dot_nt(eye, rest)
        order_ref[:, dens] = turned.reshape(8, WIN, COEF)
    leaf_mult = nt3(order_ref[...].reshape(2 * 256, COEF), single_ref.at[0])
    part = nt3(leaf_mult[0:64], up_ref.at[0])
    for octant in range(1, 8):
        part = part + nt3(leaf_mult[64 * octant : 64 * octant + 64], up_ref.at[octant])
    pad_ref[:, 0:COEF] = part
    lane = iota((16, 128), 1)
    tail = jnp.where(
        lane == 96,
        (window >> 3).astype(F32),
        jnp.where(lane == 97, (window & 7).astype(F32), 0.0),
    )
    for group in range(4):
        piece = pad_ref[16 * group : 16 * group + 16, 128:256]
        tail = tail + (pltpu.roll(piece, TAIL * group, 1) if group else piece)
    gath_ref[own, 0:64] = pad_ref[:, 0:128].astype(BF16)
    gath_ref[own, 64:80] = tail.astype(BF16)

    def copy(place, sems, index, target):
        return pltpu.make_async_remote_copy(
            src_ref=gath_ref.at[place],
            dst_ref=gath_ref.at[place],
            send_sem=sems[0].at[index],
            recv_sem=sems[1].at[index],
            device_id={"pts": target},
            device_id_type=MESH,
        )

    far = (send_sem, recv_sem)
    near = (pass_sem, take_sem)
    copy(own, near, 0, partner).start()
    for step in range(1, 16):
        copy(own, far, step, other(step, 1, core)).start()

    row64 = iota((64, 1), 0)
    target = (window + (row64 & 31)) & (BOXES - 1)
    digits = [target & 7, (target >> 3) & 7, target >> 6]
    rise = part.astype(BF16).astype(F32)
    for digit in digits:
        total = None
        for o in range(8):
            term = nt3(jnp.where(digit == o, rise, 0.0), up_ref.at[o])
            total = term if total is None else total + term
        rise = total
    pad_ref[:, 0:COEF] = rise
    for dens in range(2):
        total = jnp.sum(pad_ref[WIN * dens : WIN * dens + WIN], axis=0, keepdims=True)
        roots_ref[own, dens : dens + 1, :] = total[:, 0:128]
        roots_ref[own, 2 + dens : 3 + dens, :] = total[:, 128:256]

    def tell(step, carry):
        pltpu.make_async_remote_copy(
            src_ref=roots_ref.at[own],
            dst_ref=roots_ref.at[own],
            send_sem=root_sems.at[0],
            recv_sem=root_sems.at[1],
            device_id={"pts": (own + step) % OWNERS},
            device_id_type=MESH,
        ).start()
        return carry

    lax.fori_loop(1, OWNERS, tell, 0)
    for step in range(1, 16):
        place = other(step, -1, core)
        copy(place, far, step, partner).wait_recv()
        copy(place, near, step, partner).start()
    told = pltpu.make_async_remote_copy(
        src_ref=roots_ref.at[pl.ds(0, OWNERS - 1)],
        dst_ref=roots_ref.at[pl.ds(0, OWNERS - 1)],
        send_sem=root_sems.at[0],
        recv_sem=root_sems.at[1],
        device_id={"pts": partner},
        device_id_type=MESH,
    )
    told.wait_recv()
    root = jnp.sum(roots_ref[...], axis=0)
    root = jnp.concatenate([root[0:2], root[2:4, 0:TAIL]], axis=1)
    fall = jnp.where(row64 < WIN, root[0:1], root[1:2])
    fall = nt3(fall, single_ref.at[2])
    for digit in digits[::-1]:
        total = None
        for o in range(8):
            term = nt3(jnp.where(digit == o, fall, 0.0), down_ref.at[o])
            total = term if total is None else total + term
        fall = total
    copy(partner, near, 0, partner).wait_recv()
    for step in range(1, 16):
        copy(other(step, -1, 1 - core), near, step, partner).wait_recv()

    row = iota((BOXES, 1), 0)
    box = ((row & 7) << 6) + (row & 56) + (row >> 6)
    eye = onehot(iota((COEF, COEF), 0) == iota((COEF, COEF), 1))
    codes = gath_ref[:, 64, :].astype(F32)
    lane = iota((OWNERS, 128), 1)
    first = jnp.sum(
        jnp.where(lane == 96, 8.0 * codes, jnp.where(lane == 97, codes, 0.0)),
        axis=1,
        keepdims=True,
    )
    spread = jnp.where(iota((OWNERS, 512), 0) == (iota((OWNERS, 512), 1) >> 4), first, 0.0)
    start = jnp.sum(spread, axis=0, keepdims=True).astype(jnp.int32)
    start = start + (iota((1, 512), 1) & 15)
    halves = []
    for half in range(2):
        place = onehot(box == start + 16 * half)
        pieces = [
            gath_ref[:, 32 * dens + 16 * half : 32 * dens + 16 * half + 16, :].reshape(512, 128)
            for dens in range(2)
        ]
        pieces.append(gath_ref[:, 64:80, :].reshape(512, 128))
        halves.append(dot_nn(place, jnp.concatenate(pieces, axis=1)))
    low = []
    for dens in range(2):
        main = slice(128 * dens, 128 * dens + 128)
        tail = 256 + 2 * TAIL * dens
        value = jnp.concatenate(
            [
                halves[0][:, main] + halves[1][:, main],
                halves[0][:, tail : tail + TAIL] + halves[1][:, tail + TAIL : tail + 2 * TAIL],
            ],
            axis=1,
        )
        low.append(dot_nt(eye, value.astype(BF16)))
    low = jnp.concatenate(low, axis=0).astype(BF16)

    spot = (window + (iota((1, 256), 1) & 31)) & (BOXES - 1)
    masks = (0o444, 0o222, 0o111)
    based = [spot | (-1 - mask) for mask in masks]

    def build(index, carry):
        for part in range(2):
            pair = 2 * index + part
            shifts = shift_ref[pair]
            nbr = shifts[3:4]
            for dim in range(3):
                nbr = nbr | ((based[dim] + shifts[dim : dim + 1]) & masks[dim])
            pick = onehot(box == nbr)
            found = dot_nn(low, pick)
            upper = jnp.concatenate([found[0:COEF, 0:128], found[COEF:, 0:128]], axis=1)
            lower = jnp.concatenate([found[0:COEF, 128:256], found[COEF:, 128:256]], axis=1)
            both = jnp.concatenate([upper, lower], axis=0).astype(BF16)
            src_ref[pl.ds(pl.multiple_of(128 + pair * 304, 16), 304)] = both
        return carry

    lax.fori_loop(0, CLASS // 4, build, 0)

    acc_ref[...] = jnp.zeros_like(acc_ref)

    def mult(index, carry):
        for r in range(4):
            lhs = []
            for m in range(4):
                chunk = 375 * r + 95 * m + index * 8
                lhs.append(
                    jnp.concatenate(
                        [wide_ref[pl.ds(chunk + q, GPAD, stride=CHUNKS), :] for q in range(8)],
                        axis=1,
                    )
                )
            begin = pl.multiple_of(128 - 32 * r + index * 1024, 32)
            acc_ref[r] += dot_nn(
                jnp.concatenate(lhs, axis=0).astype(BF16), src_ref[pl.ds(begin, 1024)]
            )
        return carry

    lax.fori_loop(0, 12, mult, 0)
    block = (iota((1, 256), 1) >> 5) & 3
    for r in range(4):
        value = None
        for m in range(4):
            term = jnp.where(block == m, acc_ref[r, GPAD * m : GPAD * m + GROUPS], 0.0)
            value = term if value is None else value + term
        for half in range(2):
            lanes = slice(128 * half, 128 * half + 128)
            check_ref[half, pl.ds(r, GROUPS, stride=4), :] = value[:, lanes]
    lane = iota((64, 256), 1)
    fold = onehot(((lane & 31) == (row64 & 31)) & ((lane >> 7) == (row64 >> 5)))
    hi, mid, rest = split3(jnp.concatenate([check_ref[0], check_ref[1]], axis=1))
    checks = dot_nt(fold, hi) + dot_nt(fold, mid) + dot_nt(fold, rest)
    local = nt3(checks, single_ref.at[1]) + fall
    leaves = [nt3(local, down_ref.at[o]) for o in range(8)]
    found = []
    for dens in range(2):
        value = jnp.concatenate([leaf[WIN * dens : WIN * dens + WIN] for leaf in leaves], axis=0)
        for piece in split2(value * FACTOR):
            found.append(dot_nt(eye, piece))
    leaf_mat_ref[...] = jnp.concatenate(found, axis=0).astype(BF16)

    def spread_out(index, carry):
        cols = pl.ds(pl.multiple_of(index * CHUNK, CHUNK), CHUNK)
        start = index * (CHUNK // 128)
        pick = onehot(iota((256, CHUNK), 0) == code_ref[:, cols])
        kernel = green_ref[:, cols]
        found = dot_nn(leaf_mat_ref[...], pick)
        for dens in range(2):
            base = 2 * COEF * dens
            value = found[base : base + COEF] + found[base + COEF : base + 2 * COEF]
            line = jnp.sum(kernel * value, axis=0, keepdims=True)
            for q in range(CHUNK // 128):
                pot_ref[dens, pl.ds(start + q, 1), :] = line[:, 128 * q : 128 * q + 128]
        return carry

    lax.fori_loop(0, COLS // CHUNK, spread_out, 0)
    even, odd = mix(pot_ref[0], pot_ref[1])
    tmp_ref[pl.ds(0, 64, stride=2), :] = even
    tmp_ref[pl.ds(1, 64, stride=2), :] = odd
    reply_ref[...] = tmp_ref[...].reshape(DEVS, 1, 128)
    replies = trade(me, reply_ref, back_ref, (reply_sems.at[0], reply_sems.at[1]))
    replies.wait_recv()
    tmp_ref[...] = back_ref[...].reshape(DEVS, 128)
    for column in range(TOP):
        tiles = mix(
            tmp_ref[pl.ds(column, 16, stride=8), :],
            tmp_ref[pl.ds(TOP + column, 16, stride=8), :],
        )
        for dens in range(2):
            rows_ref[pl.ds(2 * column + dens, 16, stride=8), :] = tiles[dens]
    value = jnp.concatenate([rows_ref[8 * j : 8 * j + 8] for j in range(16)], axis=1)
    hi = value.astype(BF16).astype(F32)
    mid = (value - hi).astype(BF16).astype(F32)
    pieces = jnp.concatenate([hi, mid, value - hi - mid], axis=0).astype(BF16)
    total = None
    for block in range(8):
        pick = onehot(iota((256, PTS), 0) + 256 * block == position)
        term = dot_nn(pieces[:, 256 * block : 256 * block + 256], pick)
        total = term if total is None else total + term
    out_ref[...] = total[0:8] + total[8:16] + total[16:24]

    points.wait_send()
    copy(own, near, 0, partner).wait_send()
    for step in range(1, 16):
        copy(own, far, step, partner).wait_send()
        copy(other(step, -1, core), near, step, partner).wait_send()
    told.wait_send()
    replies.wait_send()


def per_device(
    local_pos, densities, morton_slot, slot_leaf, uc2e, m2m, m2l_ops, dc2e, lattice, l2l
):
    vmem, sem = pltpu.VMEM, pltpu.SemaphoreType.DMA
    return pl.pallas_call(
        fmm_kernel,
        out_shape=jax.ShapeDtypeStruct((8, PTS), F32),
        in_specs=[pl.BlockSpec(memory_space=pl.ANY)] * 12,
        out_specs=pl.BlockSpec(memory_space=VM),
        scratch_shapes=[
            vmem((3, PTS), F32),
            vmem((8, PTS), F32),
            vmem((1, PTS), jnp.int32),
            vmem((8, 128), jnp.int32),
            vmem((1444, 128), F32),
            vmem((1444, 128), F32),
            vmem((COEF, COEF), F32),
            vmem((COEF, COEF), F32),
            vmem((COEF, COEF), F32),
            vmem((COEF, 8), F32),
            vmem((CLASS // 2, 4, 256), jnp.int32),
            sem((11,)),
            vmem((16, PTS), F32),
            vmem((DEVS, 3, 128), F32),
            vmem((DEVS, 3, 128), F32),
            vmem((TOP, 8, 128), jnp.int32),
            vmem((1216, 128), F32),
            vmem((1216, 128), F32),
            vmem((8, 2, COEF, COEF), BF16),
            vmem((8, 2, COEF, COEF), BF16),
            vmem((3, 2, COEF, COEF), BF16),
            vmem((DEPTH, PIECE, 128), BF16),
            vmem((WIDE, 128), F32),
            sem((DEPTH,)),
            vmem((6, 64, 128), F32),
            vmem((1, COLS), jnp.int32),
            vmem((COEF, COLS), F32),
            vmem((4 * COEF, 256), F32),
            vmem((8, 2, WIN, COEF), F32),
            vmem((2 * WIN, 256), F32),
            vmem((128, 128), F32),
            vmem((OWNERS, 80, 128), BF16),
            vmem((OWNERS, 4, 128), F32),
            vmem((BROWS + 384, 256), BF16),
            vmem((4, 4 * GPAD, 256), F32),
            vmem((2, COEF, 128), F32),
            vmem((4 * COEF, 256), BF16),
            vmem((2, 64, 128), F32),
            vmem((128, 128), F32),
            vmem((DEVS, 1, 128), F32),
            vmem((DEVS, 1, 128), F32),
            sem((2,)),
            sem((TOP,)),
            sem((TOP,)),
            sem((16,)),
            sem((16,)),
            sem((16,)),
            sem((16,)),
            sem((2,)),
            sem((2,)),
        ],
        compiler_params=pltpu.CompilerParams(
            vmem_limit_bytes=62 * 1024 * 1024, collective_id=0, has_side_effects=True
        ),
        name="fmm",
    )(
        local_pos,
        densities,
        morton_slot.reshape(1, PTS),
        slot_leaf.reshape(8, 128),
        m2m.reshape(1444, 128),
        l2l.reshape(1444, 128),
        uc2e,
        dc2e,
        lattice,
        surface_columns(),
        shift_rows(),
        m2l_ops.reshape(GROUPS * CHUNKS, 128),
    )


def solution(mesh):
    placed = (
        P(None, ("pts", "top")),
        P(None, ("pts", "top")),
        P(("pts", "top")),
        P(("pts", "top")),
        P(),
        P(),
        P(),
        P(),
        P(),
        P(),
    )
    return jax.shard_map(
        per_device, mesh=mesh, in_specs=placed, out_specs=P(None, ("pts", "top")), check_vma=False
    )
```

time: 96.8 us -> 72.1 us (0.74)
  Pallas kernels: 84.3 us -> 70.4 us
  local copies, waits for them, and re-layouts: 11.9 us -> 1.38 us
    pallas_call x4 -> x1, Pallas kernels: 84.3 us -> 70.4 us  [per_device(): pl.pallas_call(fmm_kernel, out_shape=jax.ShapeDtypeStruct((8, PTS), F32),...]
    unnamed x35 -> x1, local copies, waits for them, and re-layouts: 11.9 us -> 1.38 us
where the time goes in v4:
time: 72.1 us; the launch traced here: 71.8 us
  Pallas kernels  70.4 us (98%)
  local copies, waits for them, and re-layouts  1.38 us (2%)
    pallas_call x1, Pallas kernels, per_device(): pl.pallas_call(fmm_kernel, out_shape=jax.ShapeDtypeStruct((8, PTS), F32),...  70.4 us

profile of v4, /device:TPU:1, one launch (start us, length us, event | category | flops | bytes accessed | tf_op | source)
XLA Modules:
  0.0 71.8 jit_solution(8432987413322874552)
XLA Ops:
  0.0 70.4 %fmm.1 = f32[8,1024]{1,0:T(8,128)} custom-call(f32[3,1024]{1,0:T(4,128)} %pos_hbm.1, f32[8,1024]{1,0:T(8,128)} %dens_hbm.1, s32[1,1024]{1,0:T(1,128)} %bitcast.8, s32[8,128]{1,0:T(8,128)} %bitcast.9, f32[1444,128]{1,0:T(8,128)} %bitcast.6, f32[1444,128]{1,0:T(8,128)} %bitcast.7, f32[152,152]{1,0:T(8,128)} %uc2e_hbm.1, f32[152,152]{1,0:T(8,128)} %dc2e_hbm.1, ...), custom_call_target="tpu_custom_call" | custom-call | tf_op jit(solution)/shard_map/fmm/pallas_call | solution.py:692
  70.4 1.4 %copy.14 = f32[8,1024]{1,0:T(8,128)} copy(f32[8,1024]{1,0:T(8,128)} %fmm.1) | data formatting | bytes 65536

commit v5 on v4

--- a/solution.py
+++ b/solution.py
@@ -28,7 +28,7 @@
 WIDE = 60048
 PIECE = 1440
 PIECES = 40
-DEPTH = 8
+DEPTH = 5
 TAIL = COEF - 128
 CLASS = 80
 BROWS = CLASS * COEF
@@ -51,9 +51,18 @@
     return np.array(points_list, dtype=np.float32).T
 
 
-def surface_columns():
-    table = np.zeros((COEF, 8), np.float32)
-    table[:, :3] = (np.float32(1.25) * surface_table()).T
+def surface_picks():
+    table = np.zeros((COEF, 80), np.float32)
+    steps = np.rint((surface_table().T + 1.0) * (EDGE - 1) / 2.0).astype(int)
+    for piece in range(3):
+        for dim in range(3):
+            table[np.arange(COEF), 24 * piece + 8 * dim + steps[:, dim]] = 1.0
+    return jnp.asarray(table).astype(BF16)
+
+
+def edge_values():
+    table = np.zeros((8, 128), np.float32)
+    table[:EDGE] = (np.float32(1.25) * np.linspace(-1.0, 1.0, EDGE).astype(np.float32))[:, None]
     return jnp.asarray(table)
 
 
@@ -120,6 +129,17 @@
 
 def onehot(mask):
     return jnp.where(mask, 1.0, 0.0).astype(BF16)
+
+
+def equal(left, right):
+    shape = jnp.broadcast_shapes(left.shape, right.shape)
+    same = jnp.broadcast_to(left, shape) == jnp.broadcast_to(right, shape)
+    return jnp.where(same, jnp.bfloat16(1), jnp.bfloat16(0))
+
+
+def rows_equal(count, line, shift=0):
+    line = (line - shift).astype(jnp.int16)
+    return equal(iota((count, line.shape[1]), 0).astype(jnp.int16), line)
 
 
 def matrices(flat_ref, main_ref, tail_ref):
@@ -150,43 +170,41 @@
     return even, odd
 
 
-def place_of(index):
-    return {"pts": index // TOP, "top": index % TOP}
-
-
-def greet(barrier, me):
-    def hello(step, carry):
-        pl.semaphore_signal(
-            barrier, inc=1, device_id=place_of((me + step) % DEVS), device_id_type=MESH
-        )
+def every_peer(own, top, act):
+    tops = [lax.rem(top + step, TOP) for step in range(TOP)]
+    for step in range(1, TOP):
+        act(own, tops[step])
+
+    def body(step, carry):
+        place = lax.rem(own + step, OWNERS)
+        for column in tops:
+            act(place, column)
         return carry
 
-    lax.fori_loop(1, DEVS, hello, 0)
-
-
-def trade(me, source_ref, target_ref, sems):
-    def block(slot, target):
-        return pltpu.make_async_remote_copy(
-            src_ref=source_ref.at[target],
-            dst_ref=target_ref.at[slot],
-            send_sem=sems[0],
-            recv_sem=sems[1],
-            device_id=place_of(target),
+    lax.fori_loop(1, OWNERS, body, 0)
+
+
+def trade(own, top, source_ref, target_ref, sems):
+    me = TOP * own + top
+
+    def push(place, column):
+        pltpu.make_async_remote_copy(
+            src_ref=source_ref.at[TOP * place + column],
+            dst_ref=target_ref.at[me],
+            send_sem=sems.at[0],
+            recv_sem=sems.at[1],
+            device_id={"pts": place, "top": column},
             device_id_type=MESH,
-        )
-
-    def push(step, carry):
-        block(me, (me + step) % DEVS).start()
-        return carry
-
-    lax.fori_loop(1, DEVS, push, 0)
+        ).start()
+
+    every_peer(own, top, push)
     target_ref[me] = source_ref[me]
     return pltpu.make_async_remote_copy(
         src_ref=source_ref.at[pl.ds(0, DEVS - 1)],
         dst_ref=target_ref.at[pl.ds(0, DEVS - 1)],
-        send_sem=sems[0],
-        recv_sem=sems[1],
-        device_id=place_of((me + 1) % DEVS),
+        send_sem=sems.at[0],
+        recv_sem=sems.at[1],
+        device_id={"pts": lax.rem(own + 1, OWNERS), "top": top},
         device_id_type=MESH,
     )
 
@@ -196,12 +214,17 @@
     return jnp.concatenate(rows, axis=1)
 
 
-def green(tab_ref, surf_ref, start):
-    squared = None
+def green(tab_ref, edge_ref, surf_ref, start):
+    squares = []
     for dim in range(3):
-        gap = surf_ref[:, dim : dim + 1] - row_of(tab_ref, dim, start)
-        squared = gap * gap if squared is None else squared + gap * gap
-    return lax.rsqrt(squared)
+        gap = edge_ref[:, 0:1] - row_of(tab_ref, dim, start)
+        squares.append(gap * gap)
+    squares = jnp.concatenate(squares, axis=0)
+    hi = squares.astype(BF16).astype(F32)
+    rest = squares - hi
+    mid = rest.astype(BF16).astype(F32)
+    pieces = jnp.concatenate([hi, mid, rest - mid, jnp.zeros((8, CHUNK), F32)], axis=0)
+    return lax.rsqrt(dot_nn(surf_ref[...], pieces.astype(BF16)))
 
 
 FACTOR = 1.0 / (4.0 * math.pi)
@@ -217,6 +240,7 @@
     uc2e_hbm,
     dc2e_hbm,
     lattice_hbm,
+    edge_hbm,
     surf_hbm,
     shift_hbm,
     flat_hbm,
@@ -230,9 +254,12 @@
     uc2e_ref,
     dc2e_ref,
     lattice_ref,
+    edge_ref,
     surf_ref,
     shift_ref,
     in_sem,
+    spots_ref,
+    picks_ref,
     load_ref,
     send_ref,
     recv_ref,
@@ -246,7 +273,6 @@
     wide_ref,
     stage_sem,
     tab_ref,
-    code_ref,
     green_ref,
     sums_ref,
     order_ref,
@@ -257,6 +283,9 @@
     src_ref,
     acc_ref,
     check_ref,
+    box_ref,
+    low_ref,
+    fall_ref,
     leaf_mat_ref,
     pot_ref,
     rows_ref,
@@ -274,12 +303,13 @@
 ):
     own = lax.axis_index("pts")
     top = lax.axis_index("top")
-    me = TOP * own + top
     x, y, core = own // 8, (own // 2) % 4, own % 2
     partner = own + 1 - 2 * core
 
     def other(step, sign, side):
-        return ((x + sign * (step // 4) + 4) % 4) * 8 + ((y + sign * (step % 4) + 4) % 4) * 2 + side
+        across = lax.rem(x + sign * (step // 4) + 4, 4)
+        along = lax.rem(y + sign * (step % 4) + 4, 4)
+        return across * 8 + along * 2 + side
 
     moves = [
         (pos_hbm, pos_ref),
@@ -291,6 +321,7 @@
         (uc2e_hbm, uc2e_ref),
         (dc2e_hbm, dc2e_ref),
         (lattice_hbm, lattice_ref),
+        (edge_hbm, edge_ref),
         (surf_hbm, surf_ref),
         (shift_hbm, shift_ref),
     ]
@@ -312,7 +343,13 @@
     for index in range(DEPTH):
         fetch(index, PIECE).start()
     barrier = pltpu.get_barrier_semaphore()
-    greet(barrier, me)
+
+    def greet(place, column):
+        pl.semaphore_signal(
+            barrier, inc=1, device_id={"pts": place, "top": column}, device_id_type=MESH
+        )
+
+    every_peer(own, top, greet)
 
     for load in loads[:4]:
         load.wait()
@@ -333,7 +370,8 @@
         load_ref[10 + pair : 11 + pair] = dens_ref[2 * pair + 1 : 2 * pair + 2]
     payload = jnp.concatenate(split3(load_ref[...]), axis=0)
     for block in range(8):
-        pick = onehot(iota((256, PTS), 0) + 256 * block == position)
+        pick = rows_equal(256, position, 256 * block)
+        spots_ref[256 * block : 256 * block + 256] = pick
         res = dot_nt(payload, pick)
         value = res[0:16] + res[16:32] + res[32:48]
         for pair in range(2):
@@ -345,7 +383,7 @@
                     send_ref[TOP * target + column, 0:2, :] = tile[0:2]
                     send_ref[TOP * target + column, 2:3, :] = tile[2 + column : 3 + column]
     pl.semaphore_wait(barrier, DEVS - 1)
-    points = trade(me, send_ref, recv_ref, (points_sems.at[0], points_sems.at[1]))
+    points = trade(own, top, send_ref, recv_ref, points_sems)
 
     def share(step, place):
         return pltpu.make_async_remote_copy(
@@ -353,7 +391,7 @@
             dst_ref=leaves_ref.at[place],
             send_sem=push_sem.at[step],
             recv_sem=pull_sem.at[step],
-            device_id={"top": (top + step) % TOP},
+            device_id={"top": lax.rem(top + step, TOP)},
             device_id_type=MESH,
         )
 
@@ -363,12 +401,15 @@
 
     for load in loads[4:]:
         load.wait()
-    for flat_ref, split_ref in ((m2m_ref, up_ref), (l2l_ref, down_ref)):
+
+    def prepare(flat_ref, split_ref):
         matrices(flat_ref, main_ref, tail_ref)
         for octant in range(8):
             hi, lo = split2(matrix(main_ref, tail_ref, octant))
             split_ref[octant, 0] = hi
             split_ref[octant, 1] = lo
+
+    prepare(m2m_ref, up_ref)
     for index, ref in enumerate((uc2e_ref, dc2e_ref, lattice_ref)):
         hi, lo = split2(ref[...])
         single_ref[index, 0] = hi
@@ -405,7 +446,7 @@
     pad_ref[...] = jnp.zeros_like(pad_ref)
 
     for step in range(1, TOP):
-        share(step, (top + TOP - step) % TOP).wait_recv()
+        share(step, lax.rem(top + TOP - step, TOP)).wait_recv()
         share(step, top).wait_send()
     points.wait_recv()
 
@@ -416,22 +457,21 @@
         tab_ref[2 * pair + 1] = tiles[1]
     window = leaves_ref[0, 0:1, 0:1] >> 3
     table = (leaves_ref[...].reshape(32, 128) - 8 * window).astype(F32).astype(BF16)
-    eye = onehot(iota((128, 128), 0) == iota((128, 128), 1))
-    table = dot_nt(eye, table).astype(BF16)
+    row = iota((BOXES, 128), 0)
+    box_ref[...] = ((row & 7) << 6) + (row & 56) + (row >> 6)
 
     def gather(index, carry):
         cols = pl.ds(pl.multiple_of(index * CHUNK, CHUNK), CHUNK)
         start = index * (CHUNK // 128)
         place = row_of(tab_ref, 3, start).astype(jnp.int32) - 1
-        high = onehot(iota((32, CHUNK), 0) == (place >> 7))
-        rows = dot_nn(table, high)
+        rows = dot_nn(table, onehot(iota((128, CHUNK), 0) == (place & 127)))
         leaf = jnp.sum(
-            jnp.where(iota((128, CHUNK), 0) == (place & 127), rows, 0.0), axis=0, keepdims=True
+            jnp.where(iota((32, CHUNK), 0) == (place >> 7), rows, 0.0), axis=0, keepdims=True
         ).astype(jnp.int32)
         code = (leaf & 7) * WIN + (leaf >> 3)
-        code_ref[:, cols] = code
-        pick = onehot(iota((256, CHUNK), 0) == code)
-        kernel = green(tab_ref, surf_ref, start)
+        pick = rows_equal(256, code)
+        picks_ref[:, cols] = pick
+        kernel = green(tab_ref, edge_ref, surf_ref, start)
         green_ref[:, cols] = kernel
         weighted = []
         for dens in range(2):
@@ -504,12 +544,13 @@
             dst_ref=roots_ref.at[own],
             send_sem=root_sems.at[0],
             recv_sem=root_sems.at[1],
-            device_id={"pts": (own + step) % OWNERS},
+            device_id={"pts": lax.rem(own + step, OWNERS)},
             device_id_type=MESH,
         ).start()
         return carry
 
     lax.fori_loop(1, OWNERS, tell, 0)
+    prepare(l2l_ref, down_ref)
     for step in range(1, 16):
         place = other(step, -1, core)
         copy(place, far, step, partner).wait_recv()
@@ -537,8 +578,6 @@
     for step in range(1, 16):
         copy(other(step, -1, 1 - core), near, step, partner).wait_recv()
 
-    row = iota((BOXES, 1), 0)
-    box = ((row & 7) << 6) + (row & 56) + (row >> 6)
     eye = onehot(iota((COEF, COEF), 0) == iota((COEF, COEF), 1))
     codes = gath_ref[:, 64, :].astype(F32)
     lane = iota((OWNERS, 128), 1)
@@ -550,9 +589,13 @@
     spread = jnp.where(iota((OWNERS, 512), 0) == (iota((OWNERS, 512), 1) >> 4), first, 0.0)
     start = jnp.sum(spread, axis=0, keepdims=True).astype(jnp.int32)
     start = start + (iota((1, 512), 1) & 15)
+
+    def boxes(width):
+        return jnp.concatenate([box_ref[...]] * (width // 128), axis=1)
+
     halves = []
     for half in range(2):
-        place = onehot(box == start + 16 * half)
+        place = onehot(boxes(512) == start + 16 * half)
         pieces = [
             gath_ref[:, 32 * dens + 16 * half : 32 * dens + 16 * half + 16, :].reshape(512, 128)
             for dens in range(2)
@@ -571,25 +614,29 @@
             axis=1,
         )
         low.append(dot_nt(eye, value.astype(BF16)))
-    low = jnp.concatenate(low, axis=0).astype(BF16)
+    low_ref[...] = jnp.concatenate(low, axis=0).astype(BF16)
+    fall_ref[...] = fall
 
     spot = (window + (iota((1, 256), 1) & 31)) & (BOXES - 1)
     masks = (0o444, 0o222, 0o111)
     based = [spot | (-1 - mask) for mask in masks]
 
     def build(index, carry):
+        lines = []
         for part in range(2):
-            pair = 2 * index + part
-            shifts = shift_ref[pair]
+            shifts = shift_ref[2 * index + part]
             nbr = shifts[3:4]
             for dim in range(3):
                 nbr = nbr | ((based[dim] + shifts[dim : dim + 1]) & masks[dim])
-            pick = onehot(box == nbr)
-            found = dot_nn(low, pick)
-            upper = jnp.concatenate([found[0:COEF, 0:128], found[COEF:, 0:128]], axis=1)
-            lower = jnp.concatenate([found[0:COEF, 128:256], found[COEF:, 128:256]], axis=1)
-            both = jnp.concatenate([upper, lower], axis=0).astype(BF16)
-            src_ref[pl.ds(pl.multiple_of(128 + pair * 304, 16), 304)] = both
+            lines.append(nbr)
+        pick = onehot(boxes(512) == jnp.concatenate(lines, axis=1))
+        found = dot_nn(low_ref[...], pick)
+        tiles = []
+        for part in range(4):
+            lanes = slice(128 * part, 128 * part + 128)
+            tiles.append(jnp.concatenate([found[0:COEF, lanes], found[COEF:, lanes]], axis=1))
+        both = jnp.concatenate(tiles, axis=0).astype(BF16)
+        src_ref[pl.ds(pl.multiple_of(128 + index * 608, 16), 608)] = both
         return carry
 
     lax.fori_loop(0, CLASS // 4, build, 0)
@@ -624,27 +671,27 @@
             lanes = slice(128 * half, 128 * half + 128)
             check_ref[half, pl.ds(r, GROUPS, stride=4), :] = value[:, lanes]
     lane = iota((64, 256), 1)
+    row64 = iota((64, 1), 0)
+    eye = onehot(iota((COEF, COEF), 0) == iota((COEF, COEF), 1))
     fold = onehot(((lane & 31) == (row64 & 31)) & ((lane >> 7) == (row64 >> 5)))
     hi, mid, rest = split3(jnp.concatenate([check_ref[0], check_ref[1]], axis=1))
     checks = dot_nt(fold, hi) + dot_nt(fold, mid) + dot_nt(fold, rest)
-    local = nt3(checks, single_ref.at[1]) + fall
+    local = nt3(checks, single_ref.at[1]) + fall_ref[...]
     leaves = [nt3(local, down_ref.at[o]) for o in range(8)]
     found = []
     for dens in range(2):
         value = jnp.concatenate([leaf[WIN * dens : WIN * dens + WIN] for leaf in leaves], axis=0)
-        for piece in split2(value * FACTOR):
-            found.append(dot_nt(eye, piece))
+        found.append(dot_nt(eye, (value * FACTOR).astype(BF16)))
     leaf_mat_ref[...] = jnp.concatenate(found, axis=0).astype(BF16)
 
     def spread_out(index, carry):
         cols = pl.ds(pl.multiple_of(index * CHUNK, CHUNK), CHUNK)
         start = index * (CHUNK // 128)
-        pick = onehot(iota((256, CHUNK), 0) == code_ref[:, cols])
+        pick = picks_ref[:, cols]
         kernel = green_ref[:, cols]
         found = dot_nn(leaf_mat_ref[...], pick)
         for dens in range(2):
-            base = 2 * COEF * dens
-            value = found[base : base + COEF] + found[base + COEF : base + 2 * COEF]
+            value = found[COEF * dens : COEF * dens + COEF]
             line = jnp.sum(kernel * value, axis=0, keepdims=True)
             for q in range(CHUNK // 128):
                 pot_ref[dens, pl.ds(start + q, 1), :] = line[:, 128 * q : 128 * q + 128]
@@ -655,7 +702,7 @@
     tmp_ref[pl.ds(0, 64, stride=2), :] = even
     tmp_ref[pl.ds(1, 64, stride=2), :] = odd
     reply_ref[...] = tmp_ref[...].reshape(DEVS, 1, 128)
-    replies = trade(me, reply_ref, back_ref, (reply_sems.at[0], reply_sems.at[1]))
+    replies = trade(own, top, reply_ref, back_ref, reply_sems)
     replies.wait_recv()
     tmp_ref[...] = back_ref[...].reshape(DEVS, 128)
     for column in range(TOP):
@@ -671,10 +718,10 @@
     pieces = jnp.concatenate([hi, mid, value - hi - mid], axis=0).astype(BF16)
     total = None
     for block in range(8):
-        pick = onehot(iota((256, PTS), 0) + 256 * block == position)
+        pick = spots_ref[256 * block : 256 * block + 256]
         term = dot_nn(pieces[:, 256 * block : 256 * block + 256], pick)
         total = term if total is None else total + term
-    out_ref[...] = total[0:8] + total[8:16] + total[16:24]
+    out_ref[...] = total
 
     points.wait_send()
     copy(own, near, 0, partner).wait_send()
@@ -689,10 +736,10 @@
     local_pos, densities, morton_slot, slot_leaf, uc2e, m2m, m2l_ops, dc2e, lattice, l2l
 ):
     vmem, sem = pltpu.VMEM, pltpu.SemaphoreType.DMA
-    return pl.pallas_call(
+    pieces = pl.pallas_call(
         fmm_kernel,
-        out_shape=jax.ShapeDtypeStruct((8, PTS), F32),
-        in_specs=[pl.BlockSpec(memory_space=pl.ANY)] * 12,
+        out_shape=jax.ShapeDtypeStruct((24, PTS), F32),
+        in_specs=[pl.BlockSpec(memory_space=pl.ANY)] * 13,
         out_specs=pl.BlockSpec(memory_space=VM),
         scratch_shapes=[
             vmem((3, PTS), F32),
@@ -704,9 +751,12 @@
             vmem((COEF, COEF), F32),
             vmem((COEF, COEF), F32),
             vmem((COEF, COEF), F32),
-            vmem((COEF, 8), F32),
+            vmem((8, 128), F32),
+            vmem((COEF, 80), BF16),
             vmem((CLASS // 2, 4, 256), jnp.int32),
-            sem((11,)),
+            sem((12,)),
+            vmem((OWNERS * CAP, PTS), BF16),
+            vmem((256, COLS), BF16),
             vmem((16, PTS), F32),
             vmem((DEVS, 3, 128), F32),
             vmem((DEVS, 3, 128), F32),
@@ -720,7 +770,6 @@
             vmem((WIDE, 128), F32),
             sem((DEPTH,)),
             vmem((6, 64, 128), F32),
-            vmem((1, COLS), jnp.int32),
             vmem((COEF, COLS), F32),
             vmem((4 * COEF, 256), F32),
             vmem((8, 2, WIN, COEF), F32),
@@ -731,7 +780,10 @@
             vmem((BROWS + 384, 256), BF16),
             vmem((4, 4 * GPAD, 256), F32),
             vmem((2, COEF, 128), F32),
-            vmem((4 * COEF, 256), BF16),
+            vmem((BOXES, 128), jnp.int32),
+            vmem((2 * COEF, BOXES), BF16),
+            vmem((2 * WIN, COEF), F32),
+            vmem((2 * COEF, 256), BF16),
             vmem((2, 64, 128), F32),
             vmem((128, 128), F32),
             vmem((DEVS, 1, 128), F32),
@@ -747,7 +799,7 @@
             sem((2,)),
         ],
         compiler_params=pltpu.CompilerParams(
-            vmem_limit_bytes=62 * 1024 * 1024, collective_id=0, has_side_effects=True
+            vmem_limit_bytes=67_000_000, collective_id=0, has_side_effects=True
         ),
         name="fmm",
     )(
@@ -760,10 +812,12 @@
         uc2e,
         dc2e,
         lattice,
-        surface_columns(),
+        edge_values(),
+        surface_picks(),
         shift_rows(),
         m2l_ops.reshape(GROUPS * CHUNKS, 128),
     )
+    return pieces[0:8] + pieces[8:16] + pieces[16:24]
 
 
 def solution(mesh):

time: 72.1 us -> 67.7 us (0.939)
  Pallas kernels: 70.4 us -> 66 us
  other arithmetic: 0 us -> 1.41 us
  local copies, waits for them, and re-layouts: 1.38 us -> 0 us
    pallas_call x1, Pallas kernels: 70.4 us -> 66 us  [per_device(): pl.pallas_call(fmm_kernel, out_shape=jax.ShapeDtypeStruct((24, PTS), F32)...]
    add x0 -> x1, other arithmetic: none -> 1.41 us  [per_device(): return pieces[0:8] + pieces[8:16] + pieces[16:24]]
    unnamed x1 -> x0, local copies, waits for them, and re-layouts: 1.38 us -> none
where the time goes in v5:
time: 67.7 us; the launch traced here: 67.4 us
  Pallas kernels  66 us (97%)
  other arithmetic  1.41 us (2%)
    pallas_call x1, Pallas kernels, per_device(): pl.pallas_call(fmm_kernel, out_shape=jax.ShapeDtypeStruct((24, PTS), F32)...  66 us
    add x1, other arithmetic, per_device(): return pieces[0:8] + pieces[8:16] + pieces[16:24]  1.41 us

profile of v5, /device:TPU:1, one launch (start us, length us, event | category | flops | bytes accessed | tf_op | source)
XLA Modules:
  0.0 67.4 jit_solution(16115556983693106407)
XLA Ops:
  0.0 66.0 %fmm.1 = f32[24,1024]{1,0:T(8,128)} custom-call(f32[3,1024]{1,0:T(4,128)} %pos_hbm.1, f32[8,1024]{1,0:T(8,128)} %dens_hbm.1, s32[1,1024]{1,0:T(1,128)} %bitcast.8, s32[8,128]{1,0:T(8,128)} %bitcast.9, f32[1444,128]{1,0:T(8,128)} %bitcast.6, f32[1444,128]{1,0:T(8,128)} %bitcast.7, f32[152,152]{1,0:T(8,128)} %uc2e_hbm.1, f32[152,152]{1,0:T(8,128)} %dc2e_hbm.1, ...), custom_call_target="tpu_custom_call" | custom-call | tf_op jit(solution)/shard_map/fmm/pallas_call | solution.py:739
  66.0 1.4 %slice_add_fusion = f32[8,1024]{1,0:T(8,128)} fusion(f32[24,1024]{1,0:T(8,128)} %fmm.1), kind=kLoop, calls=%fused_computation | loop fusion | flops 16384 | bytes 131072 | tf_op jit(solution)/shard_map/add | solution.py:820

commit v6 on v5

--- a/solution.py
+++ b/solution.py
@@ -184,15 +184,15 @@
     lax.fori_loop(1, OWNERS, body, 0)
 
 
-def trade(own, top, source_ref, target_ref, sems):
+def trade(own, top, source_ref, target_ref, send_sem, recv_sem):
     me = TOP * own + top
 
     def push(place, column):
         pltpu.make_async_remote_copy(
             src_ref=source_ref.at[TOP * place + column],
             dst_ref=target_ref.at[me],
-            send_sem=sems.at[0],
-            recv_sem=sems.at[1],
+            send_sem=send_sem,
+            recv_sem=recv_sem,
             device_id={"pts": place, "top": column},
             device_id_type=MESH,
         ).start()
@@ -202,8 +202,8 @@
     return pltpu.make_async_remote_copy(
         src_ref=source_ref.at[pl.ds(0, DEVS - 1)],
         dst_ref=target_ref.at[pl.ds(0, DEVS - 1)],
-        send_sem=sems.at[0],
-        recv_sem=sems.at[1],
+        send_sem=send_sem,
+        recv_sem=recv_sem,
         device_id={"pts": lax.rem(own + 1, OWNERS), "top": top},
         device_id_type=MESH,
     )
@@ -258,7 +258,7 @@
     surf_ref,
     shift_ref,
     in_sem,
-    spots_ref,
+    where_ref,
     picks_ref,
     load_ref,
     send_ref,
@@ -273,6 +273,7 @@
     wide_ref,
     stage_sem,
     tab_ref,
+    batch_ref,
     green_ref,
     sums_ref,
     order_ref,
@@ -291,7 +292,8 @@
     rows_ref,
     reply_ref,
     back_ref,
-    points_sems,
+    points_sem,
+    group_sems,
     push_sem,
     pull_sem,
     send_sem,
@@ -310,6 +312,15 @@
         across = lax.rem(x + sign * (step // 4) + 4, 4)
         along = lax.rem(y + sign * (step % 4) + 4, 4)
         return across * 8 + along * 2 + side
+
+    barrier = pltpu.get_barrier_semaphore()
+
+    def greet(place, column):
+        pl.semaphore_signal(
+            barrier, inc=1, device_id={"pts": place, "top": column}, device_id_type=MESH
+        )
+
+    every_peer(own, top, greet)
 
     moves = [
         (pos_hbm, pos_ref),
@@ -342,14 +353,6 @@
     last = GROUPS * CHUNKS - (PIECES - 1) * PIECE
     for index in range(DEPTH):
         fetch(index, PIECE).start()
-    barrier = pltpu.get_barrier_semaphore()
-
-    def greet(place, column):
-        pl.semaphore_signal(
-            barrier, inc=1, device_id={"pts": place, "top": column}, device_id_type=MESH
-        )
-
-    every_peer(own, top, greet)
 
     for load in loads[:4]:
         load.wait()
@@ -360,6 +363,7 @@
     prefix = dot_nn(member.astype(BF16), before)
     rank = jnp.sum(member * prefix, axis=0, keepdims=True)
     position = owner * CAP + rank.astype(jnp.int32)
+    where_ref[...] = position
     load_ref[...] = jnp.zeros_like(load_ref)
     load_ref[0:1] = pos_ref[0:1]
     load_ref[1:2] = pos_ref[2:3]
@@ -371,7 +375,6 @@
     payload = jnp.concatenate(split3(load_ref[...]), axis=0)
     for block in range(8):
         pick = rows_equal(256, position, 256 * block)
-        spots_ref[256 * block : 256 * block + 256] = pick
         res = dot_nt(payload, pick)
         value = res[0:16] + res[16:32] + res[32:48]
         for pair in range(2):
@@ -383,7 +386,9 @@
                     send_ref[TOP * target + column, 0:2, :] = tile[0:2]
                     send_ref[TOP * target + column, 2:3, :] = tile[2 + column : 3 + column]
     pl.semaphore_wait(barrier, DEVS - 1)
-    points = trade(own, top, send_ref, recv_ref, points_sems)
+    points = trade(
+        own, top, send_ref, recv_ref, points_sem, group_sems.at[own // 4]
+    )
 
     def share(step, place):
         return pltpu.make_async_remote_copy(
@@ -441,28 +446,49 @@
 
         return carry
 
-    lax.fori_loop(0, PIECES, widen, 0)
     sums_ref[...] = jnp.zeros_like(sums_ref)
     pad_ref[...] = jnp.zeros_like(pad_ref)
 
     for step in range(1, TOP):
         share(step, lax.rem(top + TOP - step, TOP)).wait_recv()
         share(step, top).wait_send()
-    points.wait_recv()
-
-    for pair in range(3):
-        tmp_ref[...] = recv_ref[:, pair, :]
-        tiles = mix(tmp_ref[pl.ds(0, 64, stride=2), :], tmp_ref[pl.ds(1, 64, stride=2), :])
-        tab_ref[2 * pair] = tiles[0]
-        tab_ref[2 * pair + 1] = tiles[1]
     window = leaves_ref[0, 0:1, 0:1] >> 3
     table = (leaves_ref[...].reshape(32, 128) - 8 * window).astype(F32).astype(BF16)
     row = iota((BOXES, 128), 0)
     box_ref[...] = ((row & 7) << 6) + (row & 56) + (row >> 6)
 
-    def gather(index, carry):
+    def arrived(group, count):
+        pltpu.make_async_remote_copy(
+            src_ref=send_ref.at[pl.ds(0, count)],
+            dst_ref=recv_ref.at[pl.ds(0, count)],
+            send_sem=points_sem,
+            recv_sem=group_sems.at[group],
+            device_id={"pts": partner, "top": top},
+            device_id_type=MESH,
+        ).wait_recv()
+
+    def gather(step, carry):
+        lax.fori_loop(5 * step, 5 * step + 5, widen, 0)
+        far_half = step // 2
+        across = lax.rem(x + far_half + far_half // 2 - 2 * (far_half // 3), 4)
+        index = 2 * across + lax.rem(y // 2 + step, 2)
+
+        @pl.when(step == 0)
+        def _():
+            arrived(index, 15)
+
+        @pl.when(step > 0)
+        def _():
+            arrived(index, 16)
+
         cols = pl.ds(pl.multiple_of(index * CHUNK, CHUNK), CHUNK)
         start = index * (CHUNK // 128)
+        for pair in range(3):
+            batch_ref[...] = recv_ref[pl.ds(16 * index, 16), pair, :]
+            tiles = mix(batch_ref[pl.ds(0, 8, stride=2), :], batch_ref[pl.ds(1, 8, stride=2), :])
+            rows = pl.ds(pl.multiple_of(8 * index, 8), 8)
+            tab_ref[2 * pair, rows] = tiles[0]
+            tab_ref[2 * pair + 1, rows] = tiles[1]
         place = row_of(tab_ref, 3, start).astype(jnp.int32) - 1
         rows = dot_nn(table, onehot(iota((128, CHUNK), 0) == (place & 127)))
         leaf = jnp.sum(
@@ -702,7 +728,13 @@
     tmp_ref[pl.ds(0, 64, stride=2), :] = even
     tmp_ref[pl.ds(1, 64, stride=2), :] = odd
     reply_ref[...] = tmp_ref[...].reshape(DEVS, 1, 128)
-    replies = trade(own, top, reply_ref, back_ref, reply_sems)
+    replies = trade(own, top, reply_ref, back_ref, reply_sems.at[0], reply_sems.at[1])
+    points.wait_send()
+    copy(own, near, 0, partner).wait_send()
+    for step in range(1, 16):
+        copy(own, far, step, partner).wait_send()
+        copy(other(step, -1, core), near, step, partner).wait_send()
+    told.wait_send()
     replies.wait_recv()
     tmp_ref[...] = back_ref[...].reshape(DEVS, 128)
     for column in range(TOP):
@@ -718,17 +750,11 @@
     pieces = jnp.concatenate([hi, mid, value - hi - mid], axis=0).astype(BF16)
     total = None
     for block in range(8):
-        pick = spots_ref[256 * block : 256 * block + 256]
+        pick = rows_equal(256, where_ref[...], 256 * block)
         term = dot_nn(pieces[:, 256 * block : 256 * block + 256], pick)
         total = term if total is None else total + term
     out_ref[...] = total
 
-    points.wait_send()
-    copy(own, near, 0, partner).wait_send()
-    for step in range(1, 16):
-        copy(own, far, step, partner).wait_send()
-        copy(other(step, -1, core), near, step, partner).wait_send()
-    told.wait_send()
     replies.wait_send()
 
 
@@ -755,7 +781,7 @@
             vmem((COEF, 80), BF16),
             vmem((CLASS // 2, 4, 256), jnp.int32),
             sem((12,)),
-            vmem((OWNERS * CAP, PTS), BF16),
+            vmem((1, PTS), jnp.int32),
             vmem((256, COLS), BF16),
             vmem((16, PTS), F32),
             vmem((DEVS, 3, 128), F32),
@@ -770,6 +796,7 @@
             vmem((WIDE, 128), F32),
             sem((DEPTH,)),
             vmem((6, 64, 128), F32),
+            vmem((16, 128), F32),
             vmem((COEF, COLS), F32),
             vmem((4 * COEF, 256), F32),
             vmem((8, 2, WIN, COEF), F32),
@@ -788,7 +815,8 @@
             vmem((128, 128), F32),
             vmem((DEVS, 1, 128), F32),
             vmem((DEVS, 1, 128), F32),
-            sem((2,)),
+            sem,
+            sem((8,)),
             sem((TOP,)),
             sem((TOP,)),
             sem((16,)),

time: 67.7 us -> 66.1 us (0.976)
  Pallas kernels: 66 us -> 64.4 us
    pallas_call x1, Pallas kernels: 66 us -> 64.4 us  [per_device(): pl.pallas_call(fmm_kernel, out_shape=jax.ShapeDtypeStruct((24, PTS), F32)...]
where the time goes in v6:
time: 66.1 us; the launch traced here: 65.8 us
  Pallas kernels  64.4 us (97%)
  other arithmetic  1.41 us (2%)
    pallas_call x1, Pallas kernels, per_device(): pl.pallas_call(fmm_kernel, out_shape=jax.ShapeDtypeStruct((24, PTS), F32)...  64.4 us
    add x1, other arithmetic, per_device(): return pieces[0:8] + pieces[8:16] + pieces[16:24]  1.41 us

profile of v6, /device:TPU:1, one launch (start us, length us, event | category | flops | bytes accessed | tf_op | source)
XLA Modules:
  0.0 65.8 jit_solution(1347411278798205294)
XLA Ops:
  0.0 64.4 %fmm.1 = f32[24,1024]{1,0:T(8,128)} custom-call(f32[3,1024]{1,0:T(4,128)} %pos_hbm.1, f32[8,1024]{1,0:T(8,128)} %dens_hbm.1, s32[1,1024]{1,0:T(1,128)} %bitcast.8, s32[8,128]{1,0:T(8,128)} %bitcast.9, f32[1444,128]{1,0:T(8,128)} %bitcast.6, f32[1444,128]{1,0:T(8,128)} %bitcast.7, f32[152,152]{1,0:T(8,128)} %uc2e_hbm.1, f32[152,152]{1,0:T(8,128)} %dc2e_hbm.1, ...), custom_call_target="tpu_custom_call" | custom-call | tf_op jit(solution)/shard_map/fmm/pallas_call | solution.py:765
  64.4 1.4 %slice_add_fusion = f32[8,1024]{1,0:T(8,128)} fusion(f32[24,1024]{1,0:T(8,128)} %fmm.1), kind=kLoop, calls=%fused_computation | loop fusion | flops 16384 | bytes 131072 | tf_op jit(solution)/shard_map/add | solution.py:848

commit v7 on v6

--- a/solution.py
+++ b/solution.py
@@ -710,25 +710,54 @@
         found.append(dot_nt(eye, (value * FACTOR).astype(BF16)))
     leaf_mat_ref[...] = jnp.concatenate(found, axis=0).astype(BF16)
 
-    def spread_out(index, carry):
+    def spread_out(index, home):
         cols = pl.ds(pl.multiple_of(index * CHUNK, CHUNK), CHUNK)
-        start = index * (CHUNK // 128)
-        pick = picks_ref[:, cols]
         kernel = green_ref[:, cols]
-        found = dot_nn(leaf_mat_ref[...], pick)
+        found = dot_nn(leaf_mat_ref[...], picks_ref[:, cols])
         for dens in range(2):
             value = found[COEF * dens : COEF * dens + COEF]
             line = jnp.sum(kernel * value, axis=0, keepdims=True)
             for q in range(CHUNK // 128):
-                pot_ref[dens, pl.ds(start + q, 1), :] = line[:, 128 * q : 128 * q + 128]
+                pot_ref[dens, q : q + 1, :] = line[:, 128 * q : 128 * q + 128]
+        even, odd = mix(pot_ref[0], pot_ref[1])
+        batch_ref[pl.ds(0, 8, stride=2), :] = even
+        batch_ref[pl.ds(1, 8, stride=2), :] = odd
+        reply_ref[pl.ds(16 * index, 16)] = batch_ref[...].reshape(16, 1, 128)
+        for place in range(4):
+            for column in range(TOP):
+                block = 16 * index + TOP * place + column
+                send = pltpu.make_async_remote_copy(
+                    src_ref=reply_ref.at[block],
+                    dst_ref=back_ref.at[me],
+                    send_sem=reply_sems.at[0],
+                    recv_sem=reply_sems.at[1],
+                    device_id={"pts": 4 * index + place, "top": column},
+                    device_id_type=MESH,
+                )
+                if home:
+                    pl.when(block != me)(send.start)
+                else:
+                    send.start()
+
+    def answer(step, carry):
+        turned = 7 - step
+        far_half = turned // 2
+        across = lax.rem(x + far_half + far_half // 2 - 2 * (far_half // 3), 4)
+        spread_out(2 * across + lax.rem(y // 2 + turned, 2), False)
         return carry
 
-    lax.fori_loop(0, COLS // CHUNK, spread_out, 0)
-    even, odd = mix(pot_ref[0], pot_ref[1])
-    tmp_ref[pl.ds(0, 64, stride=2), :] = even
-    tmp_ref[pl.ds(1, 64, stride=2), :] = odd
-    reply_ref[...] = tmp_ref[...].reshape(DEVS, 1, 128)
-    replies = trade(own, top, reply_ref, back_ref, reply_sems.at[0], reply_sems.at[1])
+    me = TOP * own + top
+    lax.fori_loop(0, 7, answer, 0)
+    spread_out(own // 4, True)
+    back_ref[me] = reply_ref[me]
+    replies = pltpu.make_async_remote_copy(
+        src_ref=reply_ref.at[pl.ds(0, DEVS - 1)],
+        dst_ref=back_ref.at[pl.ds(0, DEVS - 1)],
+        send_sem=reply_sems.at[0],
+        recv_sem=reply_sems.at[1],
+        device_id={"pts": partner, "top": top},
+        device_id_type=MESH,
+    )
     points.wait_send()
     copy(own, near, 0, partner).wait_send()
     for step in range(1, 16):
@@ -811,7 +840,7 @@
             vmem((2 * COEF, BOXES), BF16),
             vmem((2 * WIN, COEF), F32),
             vmem((2 * COEF, 256), BF16),
-            vmem((2, 64, 128), F32),
+            vmem((2, 8, 128), F32),
             vmem((128, 128), F32),
             vmem((DEVS, 1, 128), F32),
             vmem((DEVS, 1, 128), F32),

time: 66.1 us -> 65.4 us (0.989)
  Pallas kernels: 64.4 us -> 63.7 us
where the time goes in v7:
time: 65.4 us; the launch traced here: 65.1 us
  Pallas kernels  63.7 us (97%)
  other arithmetic  1.41 us (2%)
    pallas_call x1, Pallas kernels, per_device(): pl.pallas_call(fmm_kernel, out_shape=jax.ShapeDtypeStruct((24, PTS), F32)...  63.7 us
    add x1, other arithmetic, per_device(): return pieces[0:8] + pieces[8:16] + pieces[16:24]  1.41 us

profile of v7, /device:TPU:1, one launch (start us, length us, event | category | flops | bytes accessed | tf_op | source)
XLA Modules:
  0.0 65.1 jit_solution(14010181297574941504)
XLA Ops:
  0.0 63.7 %fmm.1 = f32[24,1024]{1,0:T(8,128)} custom-call(f32[3,1024]{1,0:T(4,128)} %pos_hbm.1, f32[8,1024]{1,0:T(8,128)} %dens_hbm.1, s32[1,1024]{1,0:T(1,128)} %bitcast.8, s32[8,128]{1,0:T(8,128)} %bitcast.9, f32[1444,128]{1,0:T(8,128)} %bitcast.6, f32[1444,128]{1,0:T(8,128)} %bitcast.7, f32[152,152]{1,0:T(8,128)} %uc2e_hbm.1, f32[152,152]{1,0:T(8,128)} %dc2e_hbm.1, ...), custom_call_target="tpu_custom_call" | custom-call | tf_op jit(solution)/shard_map/fmm/pallas_call | solution.py:794
  63.7 1.4 %slice_add_fusion = f32[8,1024]{1,0:T(8,128)} fusion(f32[24,1024]{1,0:T(8,128)} %fmm.1), kind=kLoop, calls=%fused_computation | loop fusion | flops 16384 | bytes 131072 | tf_op jit(solution)/shard_map/add | solution.py:877
